TPU v7x, 128 devices: a whole 4x4x4 slice. The times are simulated.
128 devices in a mesh: dp: 16 (over y, x), tensor: 8 (over z, core).
Axes of the slice: x: 4, y: 4, z: 4, core: 2. Of those that a mesh axis runs over, the one named last changes fastest.
Arguments:
- tokens: bfloat16 [8192, 8192], P('dp', 'tensor'), may hold values from -64 to 64
- query_weight: bfloat16 [8192, 4096], P(None, 'tensor'), may hold values from -0.0625 to 0.0625
- key_value_weight: bfloat16 [2, 8192, 1024], P(None, None, 'tensor'), may hold values from -0.0625 to 0.0625
- adapter_down_weight: bfloat16 [512, 64, 8192], P('dp', None, 'tensor'), may hold values from -0.0625 to 0.0625
- adapter_up_weight: bfloat16 [512, 64, 4096], P('dp', None, 'tensor'), may hold values from -0.25 to 0.25
- response_rubrics: int32 [32, 8], P('dp'), may hold values from 0 to 511, as said below
- lengths: int32 [32], replicated, may hold values from 1 to 256, 6144 in all
- partner_attend_mask: int32 [32], P('dp'), may hold values 0 or 1
- partner_xor_mask: int32 [2], replicated, may hold values from 1 to 15
Outputs:
- attended: bfloat16 [8192, 4096], P('dp', 'tensor')
Inputs may be any that keep to these rules, and one draw needn't show every extreme that they name: `response_rubrics`: each response lists 8 different adapters; among the adapters listed by the 2 responses of one index of dp, at most 2 lie in one block of 32 consecutive adapters, and some block holds exactly 2. `lengths`: some response uses all 256 positions.
All inputs are finite; a program needn't handle non-finite values. No bound on the sum of `partner_attend_mask` on one device may be relied on, other than what follows from the above.
Results may differ from a plain program's by a relative error of at most 0.012.
The roundings to bfloat16 on the way count: a program that leaves them out, or rounds other values in their place, can miss the bound.
Values may be sent and summed in bfloat16 or wider, within the bound.
No kernel may reach another device: no remote copies, remote signals or barrier semaphores. Data moves between devices by JAX's collectives and lax.ppermute only.
A program may use at most 128 MiB of HBM per device.

v0:
```python
from functools import partial
import math

import jax
import jax.numpy as jnp
from jax import lax
from jax.sharding import PartitionSpec as P

HEAD_SIZE = 128
MOST_PER_INDEX = 2


def swapped(value, axis, stride):
    mask = 2**stride
    pairs = [(source, source ^ mask) for source in range(lax.axis_size(axis))]
    return lax.ppermute(value, axis, pairs)


def slot_layout(adapter_index, adapters_by_owner):
    owner_ids = adapter_index // adapters_by_owner
    local_ids = adapter_index % adapters_by_owner
    slot_count = adapter_index.shape[-1]
    same_owner = owner_ids[..., :, None] == owner_ids[..., None, :]
    earlier = jnp.arange(slot_count)[:, None] > jnp.arange(slot_count)[None, :]
    owner_rank = jnp.sum(jnp.where(same_owner & earlier, 1, 0), axis=-1).astype(jnp.int32)
    return (owner_ids, local_ids, owner_rank)


def swap_tokens(block_in, bit_pos):
    return swapped(block_in, "dp", bit_pos)


def keep_block(block_in):
    return block_in


def follow_partner(block_in, mask_vec, bit_count, move_once, slot_axis):
    view_shape = [1] * block_in.ndim
    view_shape[slot_axis] = mask_vec.shape[0]
    for bit_pos in range(bit_count):
        flip = jnp.bitwise_and(jnp.right_shift(mask_vec, bit_pos), 1) == 1
        moved = lax.cond(jnp.any(flip), partial(move_once, bit_pos=bit_pos), keep_block, block_in)
        block_in = jnp.where(flip.reshape(view_shape), moved, block_in)
    return block_in


def on_device(
    tokens,
    query_weight,
    key_value_weight,
    adapter_down_weight,
    adapter_up_weight,
    response_rubrics,
    lengths,
    partner_attend_mask,
    partner_xor_mask,
):
    owner_groups = lax.axis_size("dp")
    own_index = lax.axis_index("dp")
    resp_dev, rubrics = response_rubrics.shape
    partner_dev = jnp.bitwise_xor(own_index, partner_xor_mask)
    adapters_by_owner, rank_extent, feature_shard = adapter_down_weight.shape
    head_columns = query_weight.shape[1]
    kv_cols = key_value_weight.shape[2]
    slot_count = resp_dev * rubrics
    tok_rows = tokens.shape[0]
    resp_len = tok_rows // resp_dev
    slot_ids = response_rubrics.reshape(slot_count)
    owner_ids, local_ids, owner_rank = slot_layout(slot_ids, adapters_by_owner)
    buffer_slot = owner_ids * MOST_PER_INDEX + owner_rank
    columns_all = jnp.arange(owner_groups * MOST_PER_INDEX, dtype=jnp.int32)
    hits = buffer_slot[:, None] == columns_all[None, :]
    wanted = jnp.sum(jnp.where(hits, local_ids[:, None], 0), axis=0).reshape(
        owner_groups, MOST_PER_INDEX
    )
    asked = lax.all_to_all(wanted, "dp", split_axis=0, concat_axis=0, tiled=True)
    flattened_requested = asked.reshape(owner_groups * MOST_PER_INDEX)
    shipped_down = jnp.take(adapter_down_weight, flattened_requested, axis=0).reshape(
        owner_groups, MOST_PER_INDEX, rank_extent, feature_shard
    )
    shipped_up = jnp.take(adapter_up_weight, flattened_requested, axis=0).reshape(
        owner_groups, MOST_PER_INDEX, rank_extent, head_columns
    )
    got_down, got_up = (
        lax.all_to_all(shipped_down, "dp", split_axis=0, concat_axis=0, tiled=True),
        lax.all_to_all(shipped_up, "dp", split_axis=0, concat_axis=0, tiled=True),
    )
    down_sel = jnp.take(
        got_down.reshape(owner_groups * MOST_PER_INDEX, rank_extent, feature_shard),
        buffer_slot,
        axis=0,
    )
    down_sel = down_sel.reshape(resp_dev, rubrics * rank_extent, feature_shard)
    up_sel = jnp.take(
        got_up.reshape(owner_groups * MOST_PER_INDEX, rank_extent, head_columns),
        buffer_slot,
        axis=0,
    )
    up_sel = up_sel.reshape(resp_dev, rubrics * rank_extent, head_columns)
    token_blocks = tokens.reshape(resp_dev, resp_len, feature_shard)
    partial_acts = jnp.einsum(
        "jtd,jrd->jtr", token_blocks, down_sel, preferred_element_type=jnp.float32
    )
    rank_acts = lax.psum(partial_acts, "tensor").astype(jnp.bfloat16)
    delta = jnp.einsum(
        "jtr,jrq->jtq", rank_acts, up_sel, preferred_element_type=jnp.float32
    ).reshape(tok_rows, head_columns)
    bit_count = owner_groups.bit_length() - 1
    mate_rows = follow_partner(token_blocks, partner_xor_mask, bit_count, swap_tokens, 0).reshape(
        tok_rows, feature_shard
    )
    own_cols = lax.all_gather(tokens, "tensor", axis=1, tiled=True)
    mate_cols = lax.all_gather(mate_rows, "tensor", axis=1, tiled=True)
    keyval_rows = key_value_weight
    add_query_acc = jnp.dot(own_cols, query_weight, preferred_element_type=jnp.float32)
    add_keyval_acc = jnp.einsum(
        "tw,cwk->ctk", own_cols, keyval_rows, preferred_element_type=jnp.float32
    )
    query_acc = add_query_acc
    keyval_acc = add_keyval_acc
    keyval_rows = key_value_weight
    mate_acc = jnp.einsum("tw,cwk->ctk", mate_cols, keyval_rows, preferred_element_type=jnp.float32)
    query_acc, keyval_acc, mate_acc = (query_acc, keyval_acc, mate_acc)
    own_keyval = keyval_acc.astype(jnp.bfloat16)
    mate_keyval = mate_acc.astype(jnp.bfloat16)
    queries = (query_acc + delta).astype(jnp.bfloat16)
    heads_dev = head_columns // HEAD_SIZE
    kv_heads = kv_cols // HEAD_SIZE
    per_group = heads_dev // kv_heads
    query_blocks = queries.reshape(resp_dev, resp_len, kv_heads, per_group, HEAD_SIZE)
    key_all = jnp.concatenate(
        [
            own_keyval[0].reshape(resp_dev, resp_len, kv_heads, HEAD_SIZE),
            mate_keyval[0].reshape(resp_dev, resp_len, kv_heads, HEAD_SIZE),
        ],
        axis=1,
    )
    value_all = jnp.concatenate(
        [
            own_keyval[1].reshape(resp_dev, resp_len, kv_heads, HEAD_SIZE),
            mate_keyval[1].reshape(resp_dev, resp_len, kv_heads, HEAD_SIZE),
        ],
        axis=1,
    )
    scale = 1.0 / math.sqrt(HEAD_SIZE)
    scores = (
        jnp.einsum("jtkgh,jukh->jkgtu", query_blocks, key_all, preferred_element_type=jnp.float32)
        * scale
    )
    own_lens = lax.dynamic_slice_in_dim(lengths, own_index * resp_dev, resp_dev)
    mate_index = partner_dev * resp_dev + jnp.arange(resp_dev, dtype=jnp.int32)
    mate_lens = jnp.take(lengths, mate_index, axis=0)
    positions = jnp.arange(resp_len, dtype=jnp.int32)
    own_ok = (positions[None, None, :] <= positions[None, :, None]) & (
        positions[None, None, :] < own_lens[:, None, None]
    )
    mate_ok = (positions[None, None, :] < mate_lens[:, None, None]) & (
        partner_attend_mask[:, None, None] == 1
    )
    allowed = jnp.concatenate(
        [own_ok, jnp.broadcast_to(mate_ok, (resp_dev, resp_len, resp_len))], axis=2
    )
    allowed = allowed[:, None, None, :, :]
    scores = jnp.where(allowed, scores, -1e30)
    row_top = jnp.max(scores, axis=-1, keepdims=True)
    raised = jnp.where(allowed, jnp.exp(scores - row_top), 0.0)
    weights = (raised / jnp.sum(raised, axis=-1, keepdims=True)).astype(jnp.bfloat16)
    mixed = jnp.einsum("jkgtu,jukh->jtkgh", weights, value_all, preferred_element_type=jnp.float32)
    return mixed.reshape(tok_rows, head_columns).astype(jnp.bfloat16)


def solution(mesh):
    in_specs = (
        P("dp", "tensor"),
        P(None, "tensor"),
        P(None, None, "tensor"),
        P("dp", None, "tensor"),
        P("dp", None, "tensor"),
        P("dp", None),
        P(),
        P("dp"),
        P(),
    )
    out_specs = P("dp", "tensor")
    return jax.shard_map(
        on_device, mesh=mesh, in_specs=in_specs, out_specs=out_specs, check_vma=False
    )
```

profile of v0, /device:TPU:1, one launch (start us, length us, event | category | flops | bytes accessed | tf_op | source)
XLA Modules:
  0.0 302.0 jit_solution(3536068954431345446)
XLA Ops:
  6.5 1.5 fusion.47
  10.6 2.3 conditional.4
  10.6 2.3 copy.67
  12.9 1.7 broadcast_select_fusion.2
  14.6 26.2 %conditional.5 = (bf16[2,256,1024]{2,1,0:T(8,128)(2,1)}) conditional(s32[]{:T(128)} %convert_element_type.49, bf16[2,256,1024]{2,1,0:T(8,128)(2,1)S(1)} %broadcast_select_fusion.2, bf16[2,256,1024]{2,1,0:T(8,128)(2,1)S(1)} %broadcast_select_fusion.2), branch_computations={%region_6.7_spmd, %region_7.8_spmd} | conditional | bytes 4194352 | solution.py:42
  14.6 3.7 %collective-permute-start.1 = (bf16[2,256,1024]{2,1,0:T(8,128)(2,1)S(1)}, bf16[2,256,1024]{2,1,0:T(8,128)(2,1)}, u32[]{:S(2)}, u32[]{:S(2)}) collective-permute-start(bf16[2,256,1024]{2,1,0:T(8,128)(2,1)S(1)} %param.3), channel_id=1, source_target_pairs={{0,16},{8,24},{16,0},{24,8},{32,48},{40,56},{48,32},{56,40},{64,80... | collective-permute-start | bytes 3145736 | tf_op jit(solution)/shard_map/cond/branch_1_fun/ppermute | solution.py:16
  18.3 22.5 %collective-permute-done.1 = bf16[2,256,1024]{2,1,0:T(8,128)(2,1)} collective-permute-done((bf16[2,256,1024]{2,1,0:T(8,128)(2,1)S(1)}, bf16[2,256,1024]{2,1,0:T(8,128)(2,1)}, u32[]{:S(2)}, u32[]{:S(2)}) %collective-permute-start.1) | collective-permute-done | bytes 1048608 | tf_op jit(solution)/shard_map/cond/branch_1_fun/ppermute | solution.py:16
  40.8 2.4 broadcast_select_fusion.3
  43.2 23.7 %conditional.6 = (bf16[2,256,1024]{2,1,0:T(8,128)(2,1)}) conditional(s32[]{:T(128)} %convert_element_type.48, bf16[2,256,1024]{2,1,0:T(8,128)(2,1)} %broadcast_select_fusion.3, bf16[2,256,1024]{2,1,0:T(8,128)(2,1)} %broadcast_select_fusion.3), branch_computations={%region_8.9_spmd, %region_9.10_spmd} | conditional | bytes 4194352 | solution.py:42
  43.2 1.7 collective-permute-start.2
  44.8 22.0 %collective-permute-done.2 = bf16[2,256,1024]{2,1,0:T(8,128)(2,1)} collective-permute-done((bf16[2,256,1024]{2,1,0:T(8,128)(2,1)}, bf16[2,256,1024]{2,1,0:T(8,128)(2,1)}, u32[]{:S(2)}, u32[]{:S(2)}) %collective-permute-start.2) | collective-permute-done | bytes 1048608 | tf_op jit(solution)/shard_map/cond/branch_1_fun/ppermute | solution.py:16
  66.8 1.7 broadcast_select_fusion.4
  68.6 24.1 %conditional.7 = (bf16[2,256,1024]{2,1,0:T(8,128)(2,1)}) conditional(s32[]{:T(128)} %convert_element_type.47, bf16[2,256,1024]{2,1,0:T(8,128)(2,1)S(1)} %broadcast_select_fusion.4, bf16[2,256,1024]{2,1,0:T(8,128)(2,1)S(1)} %broadcast_select_fusion.4), branch_computations={%region_10.11_spmd, %region_11.12_spmd} | conditional | bytes 4194352 | solution.py:42
  68.6 3.1 %collective-permute-start.3 = (bf16[2,256,1024]{2,1,0:T(8,128)(2,1)S(1)}, bf16[2,256,1024]{2,1,0:T(8,128)(2,1)}, u32[]{:S(2)}, u32[]{:S(2)}) collective-permute-start(bf16[2,256,1024]{2,1,0:T(8,128)(2,1)S(1)} %param.7), channel_id=1, source_target_pairs={{0,64},{8,72},{16,80},{24,88},{32,96},{40,104},{48,112},{56,120},{... | collective-permute-start | bytes 3145736 | tf_op jit(solution)/shard_map/cond/branch_1_fun/ppermute | solution.py:16
  71.7 20.9 %collective-permute-done.3 = bf16[2,256,1024]{2,1,0:T(8,128)(2,1)} collective-permute-done((bf16[2,256,1024]{2,1,0:T(8,128)(2,1)S(1)}, bf16[2,256,1024]{2,1,0:T(8,128)(2,1)}, u32[]{:S(2)}, u32[]{:S(2)}) %collective-permute-start.3) | collective-permute-done | bytes 1048608 | tf_op jit(solution)/shard_map/cond/branch_1_fun/ppermute | solution.py:16
  92.6 2.4 broadcast_select_fusion.5
  95.1 0.0 all-gather.3.cloned.1.call-start
  95.1 0.7 all-gather.3.cloned.1.call-update
  95.9 0.1 reshape.384
  96.0 0.2 select_reduce_fusion.1
  96.2 0.1 select_reduce_fusion
  96.2 0.1 all_to_all.12
  96.3 12.9 %all_to_all.19 = s32[16,1,2]{2,1,0:T(1,128)S(1)} all-to-all(s32[16,1,2]{2,1,0:T(1,128)S(1)} %bitcast.121), channel_id=1, replica_groups=mesh['dp'=16,'tensor'=8] {'dp'}, dimensions={0} | all-to-all | bytes 256 | tf_op jit(solution)/shard_map/all_to_all | solution.py:76
  109.2 0.5 broadcast.436
  109.7 0.7 reduce.5
  110.4 0.1 reshape.386
  110.5 0.1 copy.46
  110.6 0.1 copy.47
  110.7 2.0 gather_fusion.3
  112.8 3.2 %broadcast_select_fusion.1 = bf16[16,2,64,512]{3,2,1,0:T(8,128)(2,1)} fusion(bf16[16,2,64,512]{3,2,1,0:T(8,128)(2,1)} %bitcast.113, pred[16,2]{1,0:T(8,128)(4,1)S(1)} %copy.47), kind=kLoop, calls=%fused_computation.18 | loop fusion | flops 1048576 | bytes 4194336 | tf_op jit(solution)/shard_map/jit(_take)/select_n | solution.py:81
  115.9 4.5 %all-to-all-start.2 = ((bf16[16,2,64,512]{3,2,1,0:T(8,128)(2,1)}), bf16[16,2,64,512]{3,2,1,0:T(8,128)(2,1)}, u32[]{:S(2)}, u32[]{:S(2)}) async-start(bf16[16,2,64,512]{3,2,1,0:T(8,128)(2,1)} %broadcast_select_fusion.1), calls=%async_computation.2 | async-start | bytes 4194304 | tf_op jit(solution)/shard_map/all_to_all | solution.py:86
  120.4 5.1 %gather_fusion.1 = bf16[32,64,1024]{2,1,0:T(8,128)(2,1)} fusion(bf16[32,64,1024]{2,1,0:T(8,128)(2,1)} %param.20, s32[1024]{0:T(1024)S(1)} %pad_clamp_fusion.1), kind=kCustom, calls=%fused_computation.1 | custom fusion | bytes 8388736 | tf_op jit(solution)/shard_map/jit(_take)/gather | solution.py:78
  125.5 4.7 %broadcast_select_fusion = bf16[16,2,64,1024]{3,2,1,0:T(8,128)(2,1)} fusion(bf16[16,2,64,1024]{3,2,1,0:T(8,128)(2,1)} %bitcast.107, pred[16,2]{1,0:T(8,128)(4,1)S(1)} %copy.47), kind=kLoop, calls=%fused_computation.12 | loop fusion | flops 2097152 | bytes 8388640 | tf_op jit(solution)/shard_map/jit(_take)/select_n | solution.py:78
  130.3 14.6 %all-to-all-done.2 = bf16[16,2,64,512]{3,2,1,0:T(8,128)(2,1)} async-done(((bf16[16,2,64,512]{3,2,1,0:T(8,128)(2,1)}), bf16[16,2,64,512]{3,2,1,0:T(8,128)(2,1)}, u32[]{:S(2)}, u32[]{:S(2)}) %all-to-all-start.2) | async-done | bytes 2097184 | tf_op jit(solution)/shard_map/all_to_all | solution.py:86
  144.9 6.4 %all-to-all-start.1 = ((bf16[16,2,64,1024]{3,2,1,0:T(8,128)(2,1)}), bf16[16,2,64,1024]{3,2,1,0:T(8,128)(2,1)}, u32[]{:S(2)}, u32[]{:S(2)}) async-start(bf16[16,2,64,1024]{3,2,1,0:T(8,128)(2,1)} %broadcast_select_fusion), calls=%async_computation.1 | async-start | bytes 8388608 | tf_op jit(solution)/shard_map/all_to_all | solution.py:85
  151.3 0.1 reshape.388
  151.4 0.1 reduce_sum.32
  151.5 0.1 broadcast_in_dim.140
  151.6 0.1 broadcast_in_dim.141
  151.7 0.1 dynamic_slice.3
  151.7 0.6 gather_fusion
  152.5 0.1 iota_compare_fusion.3
  152.6 0.1 compare_and_fusion
  152.6 0.1 broadcast_and_fusion
  152.8 0.1 broadcast_in_dim.136
  152.9 2.2 gather_fusion.4
  155.2 0.2 bitcast_select_fusion.2
  155.4 45.5 %all-to-all-done.1 = bf16[16,2,64,1024]{3,2,1,0:T(8,128)(2,1)} async-done(((bf16[16,2,64,1024]{3,2,1,0:T(8,128)(2,1)}), bf16[16,2,64,1024]{3,2,1,0:T(8,128)(2,1)}, u32[]{:S(2)}, u32[]{:S(2)}) %all-to-all-start.1) | async-done | bytes 4194336 | tf_op jit(solution)/shard_map/all_to_all | solution.py:85
  200.8 4.3 %gather_fusion.2 = bf16[16,64,1024]{2,1,0:T(8,128)(2,1)} fusion(bf16[32,64,1024]{2,1,0:T(8,128)(2,1)} %bitcast.19, s32[1024]{0:T(1024)S(1)} %pad_clamp_fusion), kind=kCustom, calls=%fused_computation.2 | custom fusion | bytes 4194368 | tf_op jit(solution)/shard_map/jit(_take)/gather | solution.py:88
  205.1 1.9 bitcast_select_fusion.1
  207.0 0.8 convolution_bitcast_fusion
  207.8 57.6 %all-reduce.1 = bf16[2,256,512]{1,2,0:T(8,128)(2,1)S(1)} all-reduce(f32[2,256,512]{1,2,0:T(8,128)S(1)} %convolution_bitcast_fusion), channel_id=1, replica_groups=mesh['dp'=16,'tensor'=8] {'tensor'}, use_global_device_ids=true, to_apply=%region_14.15 | all-reduce | flops 262144 | bytes 1572864 | tf_op jit(solution)/shard_map/psum | solution.py:104
  265.4 0.5 fusion.50
  265.9 6.9 %fusion.22 = bf16[2,512,128]{2,1,0:T(8,128)(2,1)S(1)} fusion(bf16[2,8192,128]{2,1,0:T(8,128)(2,1)} %param.19, bf16[512,8192]{1,0:T(8,128)(2,1)} %all-gather.5.cloned.1.call-done), kind=kOutput, calls=%fused_computation.27 | convolution fusion | flops 2147614720 | bytes 12845056 | tf_op jit(solution)/shard_map/tw,cwk->ctk/dot_general | solution.py:122
  272.9 10.2 %fusion.12 = bf16[512,512]{1,0:T(8,128)(2,1)S(1)} fusion(f32[512,512]{1,0:T(8,128)S(1)} %bitcast.117, bf16[512,8192]{1,0:T(8,128)(2,1)} %all-gather.3.cloned.1.call-done, bf16[8192,512]{1,0:T(8,128)(2,1)} %param.18), kind=kOutput, calls=%fused_computation.23 | convolution fusion | flops 4295491584 | bytes 18350080 | tf_op jit(solution)/shard_map/dot_general | solution.py:115
  283.1 0.1 reshape.391
  283.3 7.0 %fusion.25 = bf16[2,512,128]{1,2,0:T(8,128)(2,1)S(1)} fusion(bf16[2,8192,128]{2,1,0:T(8,128)(2,1)} %param.19, bf16[512,8192]{1,0:T(8,128)(2,1)} %all-gather.3.cloned.1.call-done), kind=kOutput, calls=%fused_computation.28 | convolution fusion | flops 2147614720 | bytes 12845056 | tf_op jit(solution)/shard_map/tw,cwk->ctk/dot_general | solution.py:116
  290.3 0.1 copy.58
  290.5 0.1 copy.43
  290.7 0.8 fusion.4
  291.5 1.0 fusion.5
  292.5 1.5 fusion.13
  294.0 0.3 copy.52
  294.3 0.9 copy.65
  (36 shorter events, 0.3 us)
Async XLA Ops:
  6.5 104.2 %copy-start = (bf16[32,64,512]{2,1,0:T(8,128)(2,1)S(1)}, bf16[32,64,512]{2,1,0:T(8,128)(2,1)}, u32[]{:S(2)}) copy-start(bf16[32,64,512]{2,1,0:T(8,128)(2,1)} %param.21) | copy-start | bytes 6291460
  6.5 259.4 %all-gather.5.cloned.1.call-start = ((), (), s32[]{:S(2)}) async-start(), calls=%async_computation.4 | async-start | bytes 9437184 | tf_op jit(solution)/shard_map/all_gather | solution.py:113
  14.6 26.2 %collective-permute-start.1 = (bf16[2,256,1024]{2,1,0:T(8,128)(2,1)S(1)}, bf16[2,256,1024]{2,1,0:T(8,128)(2,1)}, u32[]{:S(2)}, u32[]{:S(2)}) collective-permute-start(bf16[2,256,1024]{2,1,0:T(8,128)(2,1)S(1)} %param.3), channel_id=1, source_target_pairs={{0,16},{8,24},{16,0},{24,8},{32,48},{40,56},{48,32},{56,40},{64,80... | collective-permute-start | bytes 3145736 | tf_op jit(solution)/shard_map/cond/branch_1_fun/ppermute | solution.py:16
  43.2 23.7 %collective-permute-start.2 = (bf16[2,256,1024]{2,1,0:T(8,128)(2,1)}, bf16[2,256,1024]{2,1,0:T(8,128)(2,1)}, u32[]{:S(2)}, u32[]{:S(2)}) collective-permute-start(bf16[2,256,1024]{2,1,0:T(8,128)(2,1)} %param.5), channel_id=1, source_target_pairs={{0,32},{8,40},{16,48},{24,56},{32,0},{40,8},{48,16},{56,24},{64,96... | collective-permute-start | bytes 3145736 | tf_op jit(solution)/shard_map/cond/branch_1_fun/ppermute | solution.py:16
  68.6 27.3 %copy-start.5 = (s32[2,8]{1,0:T(2,128)S(1)}, s32[2,8]{1,0:T(2,128)}, u32[]{:S(2)}) copy-start(s32[2,8]{1,0:T(2,128)} %param.22) | copy-start | bytes 196
  68.6 24.1 %collective-permute-start.3 = (bf16[2,256,1024]{2,1,0:T(8,128)(2,1)S(1)}, bf16[2,256,1024]{2,1,0:T(8,128)(2,1)}, u32[]{:S(2)}, u32[]{:S(2)}) collective-permute-start(bf16[2,256,1024]{2,1,0:T(8,128)(2,1)S(1)} %param.7), channel_id=1, source_target_pairs={{0,64},{8,72},{16,80},{24,88},{32,96},{40,104},{48,112},{56,120},{... | collective-permute-start | bytes 3145736 | tf_op jit(solution)/shard_map/cond/branch_1_fun/ppermute | solution.py:16
  95.1 177.8 %all-gather.3.cloned.1.call-start = ((), (), s32[]{:S(2)}) async-start(), calls=%async_computation.3 | async-start | bytes 9437184 | tf_op jit(solution)/shard_map/all_gather | solution.py:112
  115.9 28.9 %all-to-all-start.2 = ((bf16[16,2,64,512]{3,2,1,0:T(8,128)(2,1)}), bf16[16,2,64,512]{3,2,1,0:T(8,128)(2,1)}, u32[]{:S(2)}, u32[]{:S(2)}) async-start(bf16[16,2,64,512]{3,2,1,0:T(8,128)(2,1)} %broadcast_select_fusion.1), calls=%async_computation.2 | async-start | bytes 4194304 | tf_op jit(solution)/shard_map/all_to_all | solution.py:86
  130.3 21.4 %copy-start.2 = (s32[32]{0:T(128)S(1)}, s32[32]{0:T(128)}, u32[]{:S(2)}) copy-start(s32[32]{0:T(128)} %param.23) | copy-start | bytes 388
  130.3 21.5 %copy-start.4 = (s32[2]{0:T(128)S(1)}, s32[2]{0:T(128)}, u32[]{:S(2)}) copy-start(s32[2]{0:T(128)} %param.25) | copy-start | bytes 28
  130.3 22.2 %copy-start.6 = (s32[2]{0:T(128)S(1)}, s32[2]{0:T(128)}, u32[]{:S(2)}) copy-start(s32[2]{0:T(128)} %param.24) | copy-start | bytes 28
  144.9 56.0 %all-to-all-start.1 = ((bf16[16,2,64,1024]{3,2,1,0:T(8,128)(2,1)}), bf16[16,2,64,1024]{3,2,1,0:T(8,128)(2,1)}, u32[]{:S(2)}, u32[]{:S(2)}) async-start(bf16[16,2,64,1024]{3,2,1,0:T(8,128)(2,1)} %broadcast_select_fusion), calls=%async_computation.1 | async-start | bytes 8388608 | tf_op jit(solution)/shard_map/all_to_all | solution.py:85
  200.8 6.2 %copy-start.3 = (bf16[512,1024]{1,0:T(8,128)(2,1)S(1)}, bf16[512,1024]{1,0:T(8,128)(2,1)}, u32[]{:S(2)}) copy-start(bf16[512,1024]{1,0:T(8,128)(2,1)} %param.17) | copy-start | bytes 3145732
  292.5 2.7 copy-start.1
Sparse Core Ops, SparseCore 0:
  95.2 55.3 all-gather.4
  152.3 49.9 all-gather.2
where the time goes:
time: 301 us; the launch traced here: 302 us
  waiting for transfers between devices  126 us (42%)
  blocking collectives  70.5 us (23%)
  matrix products  27.8 us (9%)
  other arithmetic  22.2 us (7%)
  local copies, waits for them, and re-layouts  19.7 us (7%)
  starting transfers between devices  19.4 us (6%)
  between operations  16.2 us (5%)
    ppermute x3, waiting for transfers between devices, swapped(): return lax.ppermute(value, axis, pairs)  65.5 us
    psum x1, blocking collectives, on_device(): rank_acts = lax.psum(partial_acts, 'tensor').astype(jnp.bfloat16)  57.6 us
    all_to_all x1, waiting for transfers between devices, on_device(): lax.all_to_all(shipped_down, 'dp', split_axis=0, concat_axis=0, tiled=True)  45.5 us
    all_to_all x1, waiting for transfers between devices, on_device(): lax.all_to_all(shipped_up, 'dp', split_axis=0, concat_axis=0, tiled=True)  14.6 us
    all_to_all x1, blocking collectives, on_device(): lax.all_to_all(wanted, 'dp', split_axis=0, concat_axis=0, tiled=True)  12.9 us
    dot_general x1, matrix products, on_device(): jnp.dot(own_cols, query_weight, preferred_element_type=jnp.float32)  10.2 us
    ppermute x3, starting transfers between devices, swapped(): return lax.ppermute(value, axis, pairs)  8.44 us
    select_n x4, other arithmetic, follow_partner(): block_in = jnp.where(flip.reshape(view_shape), moved, block_in)  8.23 us
  transfers between devices with their start and end apart: 7, of which 5 were waited for; matrix products, arithmetic and copies ran while one was open for 12% of the time, Pallas kernels for 0%

commit v1 on v0

v1 whole, which is shorter than its diff:
```python
from functools import partial
import math

import jax
import jax.numpy as jnp
from jax import lax
from jax.sharding import PartitionSpec as P

HEAD_SIZE = 128
MOST_PER_INDEX = 2


def slot_layout(adapter_index, adapters_by_owner):
    owner_ids = adapter_index // adapters_by_owner
    local_ids = adapter_index % adapters_by_owner
    slot_count = adapter_index.shape[-1]
    same_owner = owner_ids[..., :, None] == owner_ids[..., None, :]
    earlier = jnp.arange(slot_count)[:, None] > jnp.arange(slot_count)[None, :]
    owner_rank = jnp.sum(jnp.where(same_owner & earlier, 1, 0), axis=-1).astype(jnp.int32)
    return (owner_ids, local_ids, owner_rank)


def from_partner(block, mask):
    count = lax.axis_size("dp")
    moves = [
        partial(lax.ppermute, axis_name="dp", perm=[(source, source ^ flip) for source in range(count)])
        for flip in range(1, count)
    ]
    return lax.switch(mask - 1, moves, block)


def on_device(
    tokens,
    query_weight,
    key_value_weight,
    adapter_down_weight,
    adapter_up_weight,
    response_rubrics,
    lengths,
    partner_attend_mask,
    partner_xor_mask,
):
    owner_groups = lax.axis_size("dp")
    tensor_size = lax.axis_size("tensor")
    own_index = lax.axis_index("dp")
    resp_dev, rubrics = response_rubrics.shape
    partner_dev = jnp.bitwise_xor(own_index, partner_xor_mask)
    adapters_by_owner, rank_extent, feature_shard = adapter_down_weight.shape
    head_columns = query_weight.shape[1]
    kv_cols = key_value_weight.shape[2]
    slot_count = resp_dev * rubrics
    tok_rows = tokens.shape[0]
    resp_len = tok_rows // resp_dev
    wide = lax.all_gather(tokens, "tensor", axis=1, tiled=True)
    slot_ids = response_rubrics.reshape(slot_count)
    owner_ids, local_ids, owner_rank = slot_layout(slot_ids, adapters_by_owner)
    buffer_slot = owner_ids * MOST_PER_INDEX + owner_rank
    columns_all = jnp.arange(owner_groups * MOST_PER_INDEX, dtype=jnp.int32)
    hits = buffer_slot[:, None] == columns_all[None, :]
    wanted = jnp.sum(jnp.where(hits, local_ids[:, None], 0), axis=0).reshape(
        owner_groups, MOST_PER_INDEX
    )
    asked = lax.all_to_all(wanted, "dp", split_axis=0, concat_axis=0, tiled=True)
    asked = asked.reshape(owner_groups * MOST_PER_INDEX)
    shipped_down = jnp.take(adapter_down_weight, asked, axis=0, mode="clip").reshape(
        owner_groups, MOST_PER_INDEX, rank_extent, feature_shard
    )
    got_down = lax.all_to_all(shipped_down, "dp", split_axis=0, concat_axis=0, tiled=True)
    shipped_up = jnp.take(adapter_up_weight, asked, axis=0, mode="clip").reshape(
        owner_groups, MOST_PER_INDEX, rank_extent, head_columns
    )
    got_up = lax.all_to_all(shipped_up, "dp", split_axis=0, concat_axis=0, tiled=True)
    down_sel = jnp.take(
        got_down.reshape(owner_groups * MOST_PER_INDEX, rank_extent, feature_shard),
        buffer_slot, axis=0, mode="clip",
    ).reshape(resp_dev, rubrics * rank_extent, feature_shard)
    up_sel = jnp.take(
        got_up.reshape(owner_groups * MOST_PER_INDEX, rank_extent, head_columns),
        buffer_slot, axis=0, mode="clip",
    ).reshape(resp_dev, rubrics * rank_extent, head_columns)
    token_blocks = tokens.reshape(resp_dev, resp_len, feature_shard)
    partial_acts = jnp.einsum(
        "jtd,jrd->jtr", token_blocks, down_sel, preferred_element_type=jnp.float32
    )
    ranks = rubrics * rank_extent
    pieces = partial_acts.reshape(tensor_size, tok_rows // tensor_size, ranks)
    pieces = lax.all_to_all(pieces, "tensor", split_axis=0, concat_axis=0, tiled=True)
    summed = jnp.sum(pieces, axis=0).astype(jnp.bfloat16)
    rank_acts = lax.all_gather(summed, "tensor", axis=0, tiled=True).reshape(
        resp_dev, resp_len, ranks
    )
    keyval = jnp.einsum(
        "tw,cwk->ctk", wide, key_value_weight, preferred_element_type=jnp.float32
    ).astype(jnp.bfloat16).reshape(2, resp_dev, resp_len, kv_cols)
    mate_keyval = jnp.stack(
        [from_partner(keyval[:, j], partner_xor_mask[j]) for j in range(resp_dev)], axis=1
    )
    query_acc = jnp.dot(wide, query_weight, preferred_element_type=jnp.float32)
    delta = jnp.einsum(
        "jtr,jrq->jtq", rank_acts, up_sel, preferred_element_type=jnp.float32
    ).reshape(tok_rows, head_columns)
    queries = (query_acc + delta).astype(jnp.bfloat16)
    heads_dev = head_columns // HEAD_SIZE
    kv_heads = kv_cols // HEAD_SIZE
    per_group = heads_dev // kv_heads
    query_blocks = queries.reshape(resp_dev, resp_len, kv_heads, per_group, HEAD_SIZE)
    both = jnp.concatenate([keyval, mate_keyval], axis=2).reshape(
        2, resp_dev, 2 * resp_len, kv_heads, HEAD_SIZE
    )
    key_all, value_all = both[0], both[1]
    scale = 1.0 / math.sqrt(HEAD_SIZE)
    scores = (
        jnp.einsum("jtkgh,jukh->jkgtu", query_blocks, key_all, preferred_element_type=jnp.float32)
        * scale
    )
    own_lens = lax.dynamic_slice_in_dim(lengths, own_index * resp_dev, resp_dev)
    mate_index = partner_dev * resp_dev + jnp.arange(resp_dev, dtype=jnp.int32)
    mate_lens = jnp.take(lengths, mate_index, axis=0, mode="clip")
    positions = jnp.arange(resp_len, dtype=jnp.int32)
    own_ok = (positions[None, None, :] <= positions[None, :, None]) & (
        positions[None, None, :] < own_lens[:, None, None]
    )
    mate_ok = (positions[None, None, :] < mate_lens[:, None, None]) & (
        partner_attend_mask[:, None, None] == 1
    )
    allowed = jnp.concatenate(
        [own_ok, jnp.broadcast_to(mate_ok, (resp_dev, resp_len, resp_len))], axis=2
    )
    allowed = allowed[:, None, None, :, :]
    scores = jnp.where(allowed, scores, -1e30)
    row_top = jnp.max(scores, axis=-1, keepdims=True)
    raised = jnp.where(allowed, jnp.exp(scores - row_top), 0.0)
    weights = (raised / jnp.sum(raised, axis=-1, keepdims=True)).astype(jnp.bfloat16)
    mixed = jnp.einsum("jkgtu,jukh->jtkgh", weights, value_all, preferred_element_type=jnp.float32)
    return mixed.reshape(tok_rows, head_columns).astype(jnp.bfloat16)


def solution(mesh):
    in_specs = (
        P("dp", "tensor"),
        P(None, "tensor"),
        P(None, None, "tensor"),
        P("dp", None, "tensor"),
        P("dp", None, "tensor"),
        P("dp", None),
        P(),
        P("dp"),
        P(),
    )
    out_specs = P("dp", "tensor")
    return jax.shard_map(
        on_device, mesh=mesh, in_specs=in_specs, out_specs=out_specs, check_vma=False
    )
```

time: 301 us -> 211 us (0.70)
  blocking collectives: 70.5 us -> 27.6 us
  waiting for transfers between devices: 126 us -> 96.6 us
  other arithmetic: 22.2 us -> 5.44 us
    psum x1 -> x0, blocking collectives: 57.6 us -> none  [on_device(): rank_acts = lax.psum(partial_acts, 'tensor').astype(jnp.bfloat16)]
    ppermute x3 -> x2, waiting for transfers between devices: 65.5 us -> 10.5 us  [from_partner(): return lax.switch(mask - 1, moves, block)]
    select_n x12 -> x0, other arithmetic: 18.2 us -> none  [the longest x4 8.23 us: follow_partner(): block_in = jnp.where(flip.reshape(view_shape), moved, block_in)]
    all_gather x0 -> x1, blocking collectives: none -> 13.8 us  [on_device(): lax.all_gather(summed, 'tensor', axis=0, tiled=True)]
    all_to_all x1, waiting for transfers between devices: 45.5 us -> 58.5 us  [on_device(): lax.all_to_all(shipped_down, 'dp', split_axis=0, concat_axis=0, tiled=True)]
    all_to_all x0 -> x1, starting transfers between devices: none -> 9.8 us  [on_device(): lax.all_to_all(pieces, 'tensor', split_axis=0, concat_axis=0, tiled=True)]
    all_to_all x0 -> x1, waiting for transfers between devices: none -> 9.74 us  [on_device(): lax.all_to_all(pieces, 'tensor', split_axis=0, concat_axis=0, tiled=True)]
    ppermute x3 -> x2, starting transfers between devices: 8.44 us -> 0.17 us  [from_partner(): return lax.switch(mask - 1, moves, block)]
  transfers between devices with their start and end apart: 7 -> 6, of which waited for: 5 -> 5; matrix products, arithmetic and copies ran while one was open for 12% -> 12% of each run, Pallas kernels for 0% -> 0%
where the time goes in v1:
time: 211 us; the launch traced here: 209 us
  waiting for transfers between devices  96.6 us (46%)
  blocking collectives  27.6 us (13%)
  matrix products  25.4 us (12%)
  local copies, waits for them, and re-layouts  19.5 us (9%)
  starting transfers between devices  19.4 us (9%)
  between operations  14.9 us (7%)
  other arithmetic  5.44 us (3%)
    all_to_all x1, waiting for transfers between devices, on_device(): lax.all_to_all(shipped_down, 'dp', split_axis=0, concat_axis=0, tiled=True)  58.5 us
    all_to_all x1, waiting for transfers between devices, on_device(): lax.all_to_all(shipped_up, 'dp', split_axis=0, concat_axis=0, tiled=True)  17.2 us
    all_gather x1, blocking collectives, on_device(): lax.all_gather(summed, 'tensor', axis=0, tiled=True)  13.8 us
    all_to_all x1, blocking collectives, on_device(): lax.all_to_all(wanted, 'dp', split_axis=0, concat_axis=0, tiled=True)  13.8 us
    dot_general x1, matrix products, on_device(): query_acc = jnp.dot(wide, query_weight, preferred_element_type=jnp.float32)  11.3 us
    ppermute x2, waiting for transfers between devices, from_partner(): return lax.switch(mask - 1, moves, block)  10.5 us
    all_to_all x1, starting transfers between devices, on_device(): lax.all_to_all(pieces, 'tensor', split_axis=0, concat_axis=0, tiled=True)  9.8 us
    all_to_all x1, waiting for transfers between devices, on_device(): lax.all_to_all(pieces, 'tensor', split_axis=0, concat_axis=0, tiled=True)  9.74 us
  transfers between devices with their start and end apart: 6, of which 5 were waited for; matrix products, arithmetic and copies ran while one was open for 12% of the time, Pallas kernels for 0%

profile of v1, /device:TPU:1, one launch (start us, length us, event | category | flops | bytes accessed | tf_op | source)
XLA Modules:
  0.0 209.1 jit_solution(15304983686757110682)
XLA Ops:
  6.5 0.0 copy-start
  6.5 0.0 all-gather.2.cloned.1.call-start
  6.5 0.7 all-gather.2.cloned.1.call-update
  7.3 0.8 reshape.344
  8.0 0.2 select_reduce_fusion.1
  8.2 0.1 select_reduce_fusion
  8.3 0.1 all_to_all.15
  8.4 13.8 %all_to_all.24 = s32[16,1,2]{2,1,0:T(1,128)S(1)} all-to-all(s32[16,1,2]{2,1,0:T(1,128)S(1)} %bitcast.281), channel_id=1, replica_groups=mesh['dp'=16,'tensor'=8] {'dp'}, dimensions={0} | all-to-all | bytes 256 | tf_op jit(solution)/shard_map/all_to_all | solution.py:63
  22.2 0.5 broadcast.252
  22.7 0.7 reduce.5
  23.4 0.1 reshape.368
  23.5 5.5 %gather_fusion.1 = bf16[32,64,1024]{2,1,0:T(8,128)(2,1)} fusion(bf16[32,64,1024]{2,1,0:T(8,128)(2,1)} %param.42, s32[1024]{0:T(1024)S(1)} %pad_clamp_fusion.1), kind=kCustom, calls=%fused_computation.1 | custom fusion | bytes 8388736 | tf_op jit(solution)/shard_map/jit(_take)/gather | solution.py:65
  29.0 4.6 %all-to-all-start.1 = ((bf16[16,2,64,1024]{3,2,1,0:T(8,128)(2,1)}), bf16[16,2,64,1024]{3,2,1,0:T(8,128)(2,1)}, u32[]{:S(2)}, u32[]{:S(2)}) async-start(bf16[16,2,64,1024]{3,2,1,0:T(8,128)(2,1)} %bitcast.272), calls=%async_computation.1 | async-start | bytes 8388608 | tf_op jit(solution)/shard_map/all_to_all | solution.py:68
  33.6 0.0 copy-done
  33.6 0.0 copy-start.5
  33.6 0.0 copy-start.4
  33.6 0.0 copy-start.6
  33.7 2.0 gather_fusion.3
  35.7 58.5 %all-to-all-done.1 = bf16[16,2,64,1024]{3,2,1,0:T(8,128)(2,1)} async-done(((bf16[16,2,64,1024]{3,2,1,0:T(8,128)(2,1)}), bf16[16,2,64,1024]{3,2,1,0:T(8,128)(2,1)}, u32[]{:S(2)}, u32[]{:S(2)}) %all-to-all-start.1) | async-done | bytes 4194336 | tf_op jit(solution)/shard_map/all_to_all | solution.py:68
  94.2 0.0 copy-start.2
  94.2 4.9 %all-to-all-start.3 = ((bf16[16,2,64,512]{3,2,1,0:T(8,128)(2,1)}), bf16[16,2,64,512]{3,2,1,0:T(8,128)(2,1)}, u32[]{:S(2)}, u32[]{:S(2)}) async-start(bf16[16,2,64,512]{3,2,1,0:T(8,128)(2,1)} %bitcast.273), calls=%async_computation.3 | async-start | bytes 4194304 | tf_op jit(solution)/shard_map/all_to_all | solution.py:72
  99.1 0.0 copy-done.5
  99.1 0.1 reshape.347
  99.2 0.0 copy-done.4
  99.2 0.6 fusion.27
  99.9 0.0 copy-done.6
  99.9 4.2 %gather_fusion.2 = bf16[16,64,1024]{2,1,0:T(8,128)(2,1)} fusion(bf16[32,64,1024]{2,1,0:T(8,128)(2,1)} %bitcast.73, s32[1024]{0:T(1024)S(1)} %pad_clamp_fusion), kind=kCustom, calls=%fused_computation.2 | custom fusion | bytes 4194368 | tf_op jit(solution)/shard_map/jit(_take)/gather | solution.py:73
  104.1 0.0 copy-start.1
  104.1 0.0 copy-done.2
  104.1 3.4 %fusion.28 = f32[2,512,256]{1,2,0:T(8,128)} fusion(bf16[2,512,1024]{2,1,0:T(8,128)(2,1)} %bitcast.274, bf16[2,256,1024]{2,1,0:T(8,128)(2,1)S(1)} %bitcast.276), kind=kOutput, calls=%fused_computation.88 | convolution fusion | flops 536870912 | bytes 4194304 | tf_op jit(solution)/shard_map/jtd,jrd->jtr/dot_general | solution.py:82
  107.5 17.2 %all-to-all-done.3 = bf16[16,2,64,512]{3,2,1,0:T(8,128)(2,1)} async-done(((bf16[16,2,64,512]{3,2,1,0:T(8,128)(2,1)}), bf16[16,2,64,512]{3,2,1,0:T(8,128)(2,1)}, u32[]{:S(2)}, u32[]{:S(2)}) %all-to-all-start.3) | async-done | bytes 2097184 | tf_op jit(solution)/shard_map/all_to_all | solution.py:72
  124.7 9.8 %all-to-all-start.2 = ((f32[8,64,512]{2,1,0:T(8,128)}), f32[8,64,512]{2,1,0:T(8,128)}, u32[]{:S(2)}, u32[]{:S(2)}) async-start(f32[8,64,512]{2,1,0:T(8,128)} %bitcast.277), calls=%async_computation.2 | async-start | bytes 2097152 | tf_op jit(solution)/shard_map/all_to_all | solution.py:87
  135.8 0.0 copy-done.1
  135.8 0.1 dynamic_slice.3
  135.9 0.6 gather_fusion
  136.6 0.1 iota_compare_fusion.3
  136.7 0.1 compare_and_fusion
  136.7 0.1 broadcast_and_fusion
  136.9 0.1 broadcast_in_dim.75
  137.0 0.7 pad_add_fusion
  137.8 2.2 %gather_fusion.4 = bf16[16,64,512]{2,1,0:T(8,128)(2,1)S(1)} fusion(bf16[32,64,512]{2,1,0:T(8,128)(2,1)} %bitcast.82, s32[1024]{0:T(1024)S(1)} %pad_clamp_fusion), kind=kCustom, calls=%fused_computation.4 | custom fusion | bytes 2097216 | tf_op jit(solution)/shard_map/jit(_take)/gather | solution.py:77
  140.0 9.7 %all-to-all-done.2 = f32[8,64,512]{2,1,0:T(8,128)} async-done(((f32[8,64,512]{2,1,0:T(8,128)}), f32[8,64,512]{2,1,0:T(8,128)}, u32[]{:S(2)}, u32[]{:S(2)}) %all-to-all-start.2) | async-done | bytes 1048608 | tf_op jit(solution)/shard_map/all_to_all | solution.py:87
  149.7 1.3 reduce_sum.41
  151.0 13.8 %all_gather.7 = bf16[512,512]{1,0:T(8,128)(2,1)S(1)} all-gather(bf16[64,512]{1,0:T(8,128)(2,1)S(1)} %reduce_sum.41), channel_id=1, replica_groups=mesh['dp'=16,'tensor'=8] {'tensor'}, dimensions={0}, use_global_device_ids=true | all-gather | bytes 589824 | tf_op jit(solution)/shard_map/all_gather | solution.py:89
  164.8 1.5 fusion.29
  166.3 0.0 all-gather.2.cloned.1.call-done
  166.3 11.3 %fusion.10 = bf16[512,512]{1,0:T(8,128)(2,1)} fusion(f32[512,512]{1,0:T(8,128)} %bitcast.280, bf16[512,8192]{1,0:T(8,128)(2,1)} %all-gather.2.cloned.1.call-done, bf16[8192,512]{1,0:T(8,128)(2,1)} %param.40), kind=kOutput, calls=%fused_computation.47 | convolution fusion | flops 4295491584 | bytes 18350080 | tf_op jit(solution)/shard_map/dot_general | solution.py:98
  177.6 1.2 reshape.356
  178.8 7.0 %fusion.17 = bf16[2,512,128]{1,2,0:T(8,128)(2,1)S(1)} fusion(bf16[2,8192,128]{2,1,0:T(8,128)(2,1)} %param.41, bf16[512,8192]{1,0:T(8,128)(2,1)} %all-gather.2.cloned.1.call-done), kind=kOutput, calls=%fused_computation.50 | convolution fusion | flops 2147614720 | bytes 12845056 | tf_op jit(solution)/shard_map/tw,cwk->ctk/dot_general | solution.py:92
  185.8 0.2 copy.289
  186.0 0.0 copy-start.3
  186.0 5.2 %conditional.2 = (bf16[2,1,256,128]{3,2,0,1:T(8,128)(2,1)}) conditional(s32[]{:T(128)} %bitcast.62, bf16[2,2,256,128]{3,2,1,0:T(8,128)(2,1)S(1)} %bitcast.241, bf16[2,2,256,128]{3,2,1,0:T(8,128)(2,1)S(1)} %bitcast.242, bf16[2,2,256,128]{3,2,1,0:T(8,128)(2,1)S(1)} %bitcast.243, ...), branch_computations={%region_0.1_spmd, %region_1.2_spmd, %region_2.3_spmd, %region_3.4_... | conditional | bytes 786480 | solution.py:29
  186.1 0.1 collective-permute-start.3
  186.1 5.0 %collective-permute-done.3 = bf16[2,256,128]{2,1,0:T(8,128)(2,1)} collective-permute-done((bf16[2,256,128]{2,1,0:T(8,128)(2,1)S(1)}, bf16[2,256,128]{2,1,0:T(8,128)(2,1)}, u32[]{:S(2)}, u32[]{:S(2)}) %collective-permute-start.3) | collective-permute-done | bytes 131104 | tf_op jit(solution)/shard_map/cond/branch_3_fun/ppermute | solution.py:29
  191.2 5.5 %conditional.3 = (bf16[2,1,256,128]{3,2,0,1:T(8,128)(2,1)}) conditional(s32[]{:T(128)} %bitcast.64, bf16[2,2,256,128]{3,2,1,0:T(8,128)(2,1)S(1)} %bitcast.256, bf16[2,2,256,128]{3,2,1,0:T(8,128)(2,1)S(1)} %bitcast.257, bf16[2,2,256,128]{3,2,1,0:T(8,128)(2,1)S(1)} %bitcast.258, ...), branch_computations={%region_15.16_spmd, %region_16.17_spmd, %region_17.18_spmd, %regio... | conditional | bytes 786480 | solution.py:29
  191.2 0.1 collective-permute-start.16
  191.3 5.4 %collective-permute-done.16 = bf16[2,256,128]{2,1,0:T(8,128)(2,1)} collective-permute-done((bf16[2,256,128]{2,1,0:T(8,128)(2,1)S(1)}, bf16[2,256,128]{2,1,0:T(8,128)(2,1)}, u32[]{:S(2)}, u32[]{:S(2)}) %collective-permute-start.16) | collective-permute-done | bytes 131104 | tf_op jit(solution)/shard_map/cond/branch_1_fun/ppermute | solution.py:29
  196.7 1.0 maximum_maximum_fusion
  197.7 0.0 copy-done.3
  197.7 0.8 fusion.2
  198.5 1.1 fusion.3
  199.6 1.5 fusion.11
  201.1 0.3 copy.282
  201.4 0.9 copy.326
  (11 shorter events, 0.1 us)
Async XLA Ops:
  6.5 27.1 %copy-start = (bf16[32,64,512]{2,1,0:T(8,128)(2,1)S(1)}, bf16[32,64,512]{2,1,0:T(8,128)(2,1)}, u32[]{:S(2)}) copy-start(bf16[32,64,512]{2,1,0:T(8,128)(2,1)} %param.43) | copy-start | bytes 6291460
  6.5 159.8 %all-gather.2.cloned.1.call-start = ((), (), s32[]{:S(2)}) async-start(), calls=%async_computation.4 | async-start | bytes 9437184 | tf_op jit(solution)/shard_map/all_gather | solution.py:54
  29.0 65.2 %all-to-all-start.1 = ((bf16[16,2,64,1024]{3,2,1,0:T(8,128)(2,1)}), bf16[16,2,64,1024]{3,2,1,0:T(8,128)(2,1)}, u32[]{:S(2)}, u32[]{:S(2)}) async-start(bf16[16,2,64,1024]{3,2,1,0:T(8,128)(2,1)} %bitcast.272), calls=%async_computation.1 | async-start | bytes 8388608 | tf_op jit(solution)/shard_map/all_to_all | solution.py:68
  33.6 65.5 %copy-start.5 = (s32[2,8]{1,0:T(2,128)S(1)}, s32[2,8]{1,0:T(2,128)}, u32[]{:S(2)}) copy-start(s32[2,8]{1,0:T(2,128)} %param.44) | copy-start | bytes 196
  33.6 65.6 %copy-start.4 = (s32[2]{0:T(128)S(1)}, s32[2]{0:T(128)}, u32[]{:S(2)}) copy-start(s32[2]{0:T(128)} %param.47) | copy-start | bytes 28
  33.6 66.2 %copy-start.6 = (s32[2]{0:T(128)S(1)}, s32[2]{0:T(128)}, u32[]{:S(2)}) copy-start(s32[2]{0:T(128)} %param.46) | copy-start | bytes 28
  94.2 9.9 %copy-start.2 = (bf16[512,1024]{1,0:T(8,128)(2,1)S(1)}, bf16[512,1024]{1,0:T(8,128)(2,1)}, u32[]{:S(2)}) copy-start(bf16[512,1024]{1,0:T(8,128)(2,1)} %param.39) | copy-start | bytes 3145732
  94.2 30.5 %all-to-all-start.3 = ((bf16[16,2,64,512]{3,2,1,0:T(8,128)(2,1)}), bf16[16,2,64,512]{3,2,1,0:T(8,128)(2,1)}, u32[]{:S(2)}, u32[]{:S(2)}) async-start(bf16[16,2,64,512]{3,2,1,0:T(8,128)(2,1)} %bitcast.273), calls=%async_computation.3 | async-start | bytes 4194304 | tf_op jit(solution)/shard_map/all_to_all | solution.py:72
  104.1 31.8 %copy-start.1 = (s32[32]{0:T(128)S(1)}, s32[32]{0:T(128)}, u32[]{:S(2)}) copy-start(s32[32]{0:T(128)} %param.45) | copy-start | bytes 388
  124.7 25.0 %all-to-all-start.2 = ((f32[8,64,512]{2,1,0:T(8,128)}), f32[8,64,512]{2,1,0:T(8,128)}, u32[]{:S(2)}, u32[]{:S(2)}) async-start(f32[8,64,512]{2,1,0:T(8,128)} %bitcast.277), calls=%async_computation.2 | async-start | bytes 2097152 | tf_op jit(solution)/shard_map/all_to_all | solution.py:87
  186.0 11.7 %copy-start.3 = (pred[2,256,512]{1,2,0:T(8,128)(4,1)S(1)}, pred[2,256,512]{1,2,0:T(8,128)(4,1)}, u32[]{:S(2)}) copy-start(pred[2,256,512]{1,2,0:T(8,128)(4,1)} %pad_add_fusion) | copy-start | bytes 786436
  186.1 5.1 %collective-permute-start.3 = (bf16[2,256,128]{2,1,0:T(8,128)(2,1)S(1)}, bf16[2,256,128]{2,1,0:T(8,128)(2,1)}, u32[]{:S(2)}, u32[]{:S(2)}) collective-permute-start(bf16[2,256,128]{2,1,0:T(8,128)(2,1)S(1)} %slice_bitcast_fusion.3), channel_id=1, source_target_pairs={{0,32},{8,40},{16,48},{24,56},{32,0},{40,8},{48,16},{56,24},{64,96... | collective-permute-start | bytes 393224 | tf_op jit(solution)/shard_map/cond/branch_3_fun/ppermute | solution.py:29
  191.2 5.5 %collective-permute-start.16 = (bf16[2,256,128]{2,1,0:T(8,128)(2,1)S(1)}, bf16[2,256,128]{2,1,0:T(8,128)(2,1)}, u32[]{:S(2)}, u32[]{:S(2)}) collective-permute-start(bf16[2,256,128]{2,1,0:T(8,128)(2,1)S(1)} %slice_bitcast_fusion.16), channel_id=1, source_target_pairs={{0,16},{8,24},{16,0},{24,8},{32,48},{40,56},{48,32},{56,40},{64,80... | collective-permute-start | bytes 393224 | tf_op jit(solution)/shard_map/cond/branch_1_fun/ppermute | solution.py:29
Sparse Core Ops, SparseCore 0:
  9.1 53.5 all-gather.1

commit v2 on v1

v2 whole, which is shorter than its diff:
```python
from functools import partial
import math

import jax
import jax.numpy as jnp
from jax import lax
from jax.experimental import pallas as pl
from jax.experimental.pallas import tpu as pltpu
from jax.sharding import PartitionSpec as P

HEAD_SIZE = 128
MOST_PER_INDEX = 2
LANES = 128


def slot_layout(adapter_index, adapters_by_owner):
    owner_ids = adapter_index // adapters_by_owner
    local_ids = adapter_index % adapters_by_owner
    same_owner = owner_ids[:, None] == owner_ids[None, :]
    smaller = adapter_index[None, :] < adapter_index[:, None]
    owner_rank = jnp.any(same_owner & smaller, axis=1).astype(jnp.int32)
    return owner_ids, local_ids, owner_ids * MOST_PER_INDEX + owner_rank


def from_partner(block, mask):
    count = lax.axis_size("dp")
    moves = [
        partial(lax.ppermute, axis_name="dp", perm=[(source, source ^ flip) for source in range(count)])
        for flip in range(1, count)
    ]
    return lax.switch(mask - 1, moves, block)


def take_asked(table, asked):
    return jnp.take(table, asked[:, :MOST_PER_INDEX].reshape(-1), axis=0, mode="clip")


def partial_kernel(slots_ref, tokens_ref, *refs):
    downs, out_ref = refs[:-1], refs[-1]
    rows = jnp.concatenate([d[0] for d in downs], axis=0)
    out_ref[...] = lax.dot_general(
        tokens_ref[...], rows, (((1,), (1,)), ((), ())), preferred_element_type=jnp.float32
    ).astype(out_ref.dtype)


def partial_rank_acts(tokens, got_down, slots, resp_dev, rubrics):
    rows, features = tokens.shape
    ranks = got_down.shape[1]
    resp_len = rows // resp_dev

    def down_spec(s):
        return pl.BlockSpec((1, ranks, features), lambda j, slots_ref: (slots_ref[j * rubrics + s], 0, 0))

    return pl.pallas_call(
        partial_kernel,
        out_shape=jax.ShapeDtypeStruct((rows, rubrics * ranks), jnp.bfloat16),
        grid_spec=pltpu.PrefetchScalarGridSpec(
            num_scalar_prefetch=1,
            grid=(resp_dev,),
            in_specs=[pl.BlockSpec((resp_len, features), lambda j, slots_ref: (j, 0))]
            + [down_spec(s) for s in range(rubrics)],
            out_specs=pl.BlockSpec((resp_len, rubrics * ranks), lambda j, slots_ref: (j, 0)),
        ),
        compiler_params=pltpu.CompilerParams(vmem_limit_bytes=32 << 20),
        name="partial_rank_acts",
    )(slots, tokens, *([got_down] * rubrics))


def attend_kernel(
    slots_ref, lens_ref, mates_ref, partials_ref, base_ref, own_ref, mate_ref, *refs
):
    ups, out_ref = refs[:-1], refs[-1]
    j = pl.program_id(0)
    acts = jnp.sum(partials_ref[...].astype(jnp.float32), axis=0).astype(jnp.bfloat16)
    up_rows = jnp.concatenate([u[0] for u in ups], axis=0)
    delta = jnp.dot(acts, up_rows, preferred_element_type=jnp.float32)
    queries = (base_ref[...] + delta).astype(jnp.bfloat16)
    rows, columns = queries.shape
    scale = math.log2(math.e) / math.sqrt(HEAD_SIZE)
    keys = jnp.concatenate([own_ref[0], mate_ref[0]], axis=0)
    values = jnp.concatenate([own_ref[1], mate_ref[1]], axis=0)
    position = lax.broadcasted_iota(jnp.int32, (rows, 2 * rows), 0)
    key_at = lax.broadcasted_iota(jnp.int32, (rows, 2 * rows), 1)
    own_ok = (key_at <= position) & (key_at < lens_ref[j])
    mate_ok = (key_at >= rows) & (key_at < rows + mates_ref[j])
    allowed = own_ok | mate_ok
    for h in range(columns // HEAD_SIZE):
        cut = slice(h * HEAD_SIZE, (h + 1) * HEAD_SIZE)
        scores = lax.dot_general(
            queries[:, cut], keys, (((1,), (1,)), ((), ())), preferred_element_type=jnp.float32
        )
        scores = jnp.where(allowed, scores, -1e30)
        top = jnp.max(scores, axis=1, keepdims=True)
        raised = jnp.exp2((scores - top) * scale)
        weights = (raised * (1.0 / jnp.sum(raised, axis=1, keepdims=True))).astype(jnp.bfloat16)
        out_ref[:, cut] = jnp.dot(weights, values, preferred_element_type=jnp.float32).astype(
            out_ref.dtype
        )


def attend(partials, base, keyval, mate_keyval, got_up, slots, own_lens, mate_lens, rubrics):
    rows, columns = base.shape
    resp_dev = own_lens.shape[0]
    resp_len = rows // resp_dev
    shards = partials.shape[0]
    ranks = got_up.shape[1]

    def up_spec(s):
        return pl.BlockSpec((1, ranks, columns), lambda j, slots_ref, *_: (slots_ref[j * rubrics + s], 0, 0))

    kv_spec = pl.BlockSpec((2, resp_len, HEAD_SIZE), lambda j, *_: (0, j, 0))
    return pl.pallas_call(
        attend_kernel,
        out_shape=jax.ShapeDtypeStruct((rows, columns), jnp.bfloat16),
        grid_spec=pltpu.PrefetchScalarGridSpec(
            num_scalar_prefetch=3,
            grid=(resp_dev,),
            in_specs=[
                pl.BlockSpec((shards, resp_len, rubrics * ranks), lambda j, *_: (0, j, 0)),
                pl.BlockSpec((resp_len, columns), lambda j, *_: (j, 0)),
                kv_spec,
                kv_spec,
            ]
            + [up_spec(s) for s in range(rubrics)],
            out_specs=pl.BlockSpec((resp_len, columns), lambda j, *_: (j, 0)),
        ),
        compiler_params=pltpu.CompilerParams(vmem_limit_bytes=40 << 20),
        name="attend",
    )(slots, own_lens, mate_lens, pltpu.with_memory_space_constraint(partials, pltpu.HBM), pltpu.with_memory_space_constraint(base, pltpu.HBM), keyval, mate_keyval, *([got_up] * rubrics))


def on_device(
    tokens,
    query_weight,
    key_value_weight,
    adapter_down_weight,
    adapter_up_weight,
    response_rubrics,
    lengths,
    partner_attend_mask,
    partner_xor_mask,
):
    owner_groups = lax.axis_size("dp")
    own_index = lax.axis_index("dp")
    resp_dev, rubrics = response_rubrics.shape
    partner_dev = jnp.bitwise_xor(own_index, partner_xor_mask)
    adapters_by_owner, rank_extent, feature_shard = adapter_down_weight.shape
    head_columns = query_weight.shape[1]
    kv_cols = key_value_weight.shape[2]
    slot_count = resp_dev * rubrics
    tok_rows = tokens.shape[0]
    resp_len = tok_rows // resp_dev
    wide = lax.all_gather(tokens, "tensor", axis=1, tiled=True)
    slot_ids = response_rubrics.reshape(slot_count)
    owner_ids, local_ids, buffer_slot = slot_layout(slot_ids, adapters_by_owner)
    cells = lax.broadcasted_iota(jnp.int32, (owner_groups, LANES), 0) * MOST_PER_INDEX
    lane = lax.broadcasted_iota(jnp.int32, (owner_groups, LANES), 1)
    cells = jnp.where(lane < MOST_PER_INDEX, cells + lane, -1)
    wanted = jnp.max(
        jnp.where(buffer_slot[:, None, None] == cells[None], local_ids[:, None, None], 0), axis=0
    )
    asked = lax.all_to_all(wanted, "dp", split_axis=0, concat_axis=0, tiled=True)
    shipped_down = take_asked(adapter_down_weight, asked)
    shipped_down = shipped_down.reshape(owner_groups, MOST_PER_INDEX, rank_extent, feature_shard)
    got_down = lax.all_to_all(shipped_down, "dp", split_axis=0, concat_axis=0, tiled=True)
    shipped_up = take_asked(adapter_up_weight, asked)
    shipped_up = shipped_up.reshape(owner_groups, MOST_PER_INDEX, rank_extent, head_columns)
    keyval = jnp.einsum(
        "tw,cwk->ctk", wide, key_value_weight, preferred_element_type=jnp.float32
    ).astype(jnp.bfloat16)
    base = jnp.dot(wide, query_weight, preferred_element_type=jnp.float32)
    own_keyval = keyval.reshape(2, resp_dev, resp_len, kv_cols)
    own_keyval, base = lax.optimization_barrier((own_keyval, base))
    mate_first = from_partner(own_keyval[:, 0], partner_xor_mask[0])
    got_down, shipped_up, mate_first, own_keyval = lax.optimization_barrier(
        (got_down, shipped_up, mate_first, own_keyval)
    )
    got_up = lax.all_to_all(shipped_up, "dp", split_axis=0, concat_axis=0, tiled=True)
    partials = partial_rank_acts(
        tokens, got_down.reshape(-1, rank_extent, feature_shard), buffer_slot, resp_dev, rubrics
    )
    partials, own_keyval = lax.optimization_barrier((partials, own_keyval))
    partials = lax.all_gather(partials, "tensor", axis=0)
    mate_second = from_partner(own_keyval[:, 1], partner_xor_mask[1])
    mate_keyval = jnp.concatenate([mate_first, mate_second], axis=1)
    own_lens = lax.dynamic_slice_in_dim(lengths, own_index * resp_dev, resp_dev)
    mate_index = partner_dev * resp_dev + jnp.arange(resp_dev, dtype=jnp.int32)
    mate_lens = jnp.take(lengths, mate_index, axis=0, mode="clip")
    mate_lens = jnp.where(partner_attend_mask == 1, mate_lens, 0)
    return attend(
        partials, base, keyval, mate_keyval, got_up.reshape(-1, rank_extent, head_columns),
        buffer_slot, own_lens, mate_lens, rubrics,
    )


def solution(mesh):
    in_specs = (
        P("dp", "tensor"),
        P(None, "tensor"),
        P(None, None, "tensor"),
        P("dp", None, "tensor"),
        P("dp", None, "tensor"),
        P("dp", None),
        P(),
        P("dp"),
        P(),
    )
    out_specs = P("dp", "tensor")
    return jax.shard_map(
        on_device, mesh=mesh, in_specs=in_specs, out_specs=out_specs, check_vma=False
    )
```

time: 211 us -> 150 us (0.71)
  waiting for transfers between devices: 96.6 us -> 66.1 us
  blocking collectives: 27.6 us -> 13.8 us
  Pallas kernels: 0 us -> 10.5 us
  matrix products: 25.4 us -> 15 us
  local copies, waits for them, and re-layouts: 19.5 us -> 10.5 us
  other arithmetic: 5.44 us -> 1.4 us
  starting transfers between devices: 19.4 us -> 17 us
    all_to_all x1, waiting for transfers between devices: 58.5 us -> 0.01 us  [on_device(): lax.all_to_all(shipped_down, 'dp', split_axis=0, concat_axis=0, tiled=True)]
    all_gather x1, waiting for transfers between devices: 0.01 us -> 26.6 us  [on_device(): wide = lax.all_gather(tokens, 'tensor', axis=1, tiled=True)]
    ppermute x2, waiting for transfers between devices: 10.5 us -> 36.5 us  [from_partner(): return lax.switch(mask - 1, moves, block)]
    all_to_all x1, waiting for transfers between devices: 17.2 us -> 0.01 us  [on_device(): lax.all_to_all(shipped_up, 'dp', split_axis=0, concat_axis=0, tiled=True)]
    all_gather x1 -> x0, blocking collectives: 13.8 us -> none  [on_device(): lax.all_gather(summed, 'tensor', axis=0, tiled=True)]
    pallas_call x0 -> x2, Pallas kernels: none -> 10.5 us  [the longest x1 7.46 us: attend(): pl.pallas_call(attend_kernel, out_shape=jax.ShapeDtypeStruct((rows, colum...]
    dot_general x5 -> x1, matrix products: 18.4 us -> 7.92 us  [on_device(): base = jnp.dot(wide, query_weight, preferred_element_type=jnp.float32)]
    all_to_all x1 -> x0, starting transfers between devices: 9.8 us -> none  [on_device(): lax.all_to_all(pieces, 'tensor', split_axis=0, concat_axis=0, tiled=True)]
  transfers between devices with their start and end apart: 6 -> 6, of which waited for: 5 -> 4; matrix products, arithmetic and copies ran while one was open for 12% -> 17% of each run, Pallas kernels for 0% -> 0%
where the time goes in v2:
time: 150 us; the launch traced here: 149 us
  waiting for transfers between devices  66.1 us (44%)
  starting transfers between devices  17 us (11%)
  matrix products  15 us (10%)
  between operations  14.8 us (10%)
  blocking collectives  13.8 us (9%)
  local copies, waits for them, and re-layouts  10.5 us (7%)
  Pallas kernels  10.5 us (7%)
    ppermute x2, waiting for transfers between devices, from_partner(): return lax.switch(mask - 1, moves, block)  36.5 us
    all_gather x1, waiting for transfers between devices, on_device(): wide = lax.all_gather(tokens, 'tensor', axis=1, tiled=True)  26.6 us
    all_to_all x1, blocking collectives, on_device(): lax.all_to_all(wanted, 'dp', split_axis=0, concat_axis=0, tiled=True)  13.8 us
    dot_general x1, matrix products, on_device(): base = jnp.dot(wide, query_weight, preferred_element_type=jnp.float32)  7.92 us
    ppermute x2, starting transfers between devices, from_partner(): return lax.switch(mask - 1, moves, block)  7.78 us
    gather x2, local copies, waits for them, and re-layouts, take_asked(): jnp.take(table, asked[:, :MOST_PER_INDEX].reshape(-1), axis=0, mode='clip')  7.56 us
    pallas_call x1, Pallas kernels, attend(): pl.pallas_call(attend_kernel, out_shape=jax.ShapeDtypeStruct((rows, colum...  7.46 us
    dot_general x1, matrix products, on_device(): jnp.einsum('tw,cwk->ctk', wide, key_value_weight, preferred_element_type=...  7.05 us
  transfers between devices with their start and end apart: 6, of which 4 were waited for; matrix products, arithmetic and copies ran while one was open for 17% of the time, Pallas kernels for 0%

profile of v2, /device:TPU:1, one launch (start us, length us, event | category | flops | bytes accessed | tf_op | source)
XLA Modules:
  0.0 149.2 jit_solution(4135223947255234019)
XLA Ops:
  6.5 0.0 copy-start
  6.5 0.0 all-gather.4.cloned.1.call-start
  6.5 0.7 all-gather.4.cloned.1.call-update
  7.3 0.8 reshape.175
  8.0 0.2 and_reduce_fusion
  8.2 0.1 add_select_fusion
  8.3 0.1 select_reduce_fusion
  8.4 13.8 %all_to_all.22 = s32[16,1,128]{2,1,0:T(1,128)S(1)} all-to-all(s32[16,1,128]{2,1,0:T(1,128)S(1)} %bitcast.33), channel_id=1, replica_groups=mesh['dp'=16,'tensor'=8] {'dp'}, dimensions={0} | all-to-all | bytes 16384 | tf_op jit(solution)/shard_map/all_to_all | solution.py:162
  22.2 0.1 reshape.191
  22.3 5.5 %gather_fusion.1 = bf16[32,64,1024]{2,1,0:T(8,128)(2,1)} fusion(bf16[32,64,1024]{2,1,0:T(8,128)(2,1)} %param.42, s32[1024]{0:T(1024)S(1)} %pad_clamp_fusion), kind=kCustom, calls=%fused_computation.1 | custom fusion | bytes 8388736 | tf_op jit(solution)/shard_map/jit(_take)/gather | solution.py:35
  27.9 0.0 copy-start.4
  27.9 4.8 %all-to-all-start.1 = ((bf16[16,2,64,1024]{3,2,1,0:T(8,128)(2,1)}), bf16[16,2,64,1024]{3,2,1,0:T(8,128)(2,1)}, u32[]{:S(2)}, u32[]{:S(2)}) async-start(bf16[16,2,64,1024]{3,2,1,0:T(8,128)(2,1)} %bitcast.30), calls=%async_computation.1 | async-start | bytes 8388608 | tf_op jit(solution)/shard_map/all_to_all | solution.py:165
  32.6 0.0 all-gather.6.cloned.1.call-start
  32.7 0.0 copy-done.4
  32.7 0.6 fusion.5
  34.0 0.0 copy-done
  34.0 2.0 %gather_fusion.2 = bf16[32,64,512]{2,1,0:T(8,128)(2,1)} fusion(bf16[32,64,512]{2,1,0:T(8,128)(2,1)S(1)} %copy-done, s32[1024]{0:T(1024)S(1)} %pad_clamp_fusion), kind=kCustom, calls=%fused_computation.2 | custom fusion | bytes 4194432 | tf_op jit(solution)/shard_map/jit(_take)/gather | solution.py:35
  36.0 26.6 %all-gather.4.cloned.1.call-done = bf16[512,8192]{1,0:T(8,128)(2,1)} async-done(((bf16[512,1024]{1,0:T(8,128)(2,1)}), bf16[512,8192]{1,0:T(8,128)(2,1)}) %all-gather.4.cloned.1.call-update) | async-done | bytes 8388624 | tf_op jit(solution)/shard_map/all_gather | solution.py:153
  62.6 0.0 copy-start.5
  62.6 7.0 %fusion.2 = bf16[2,128,512]{1,2,0:T(8,128)(2,1)S(1)} fusion(bf16[2,8192,128]{2,1,0:T(8,128)(2,1)} %param.41, bf16[512,8192]{1,0:T(8,128)(2,1)} %all-gather.4.cloned.1.call-done), kind=kOutput, calls=%fused_computation.5 | convolution fusion | flops 2147614720 | bytes 12845056 | tf_op jit(solution)/shard_map/tw,cwk->ctk/dot_general | solution.py:168
  69.7 0.0 copy-done.5
  69.7 0.0 copy-start.1
  69.7 7.9 %fusion.6.base_ref = f32[512,512]{1,0:T(8,128)} fusion(bf16[512,8192]{1,0:T(8,128)(2,1)S(1)} %copy-done.5, bf16[8192,512]{1,0:T(8,128)(2,1)} %param.40), kind=kOutput, calls=%fused_computation.25 | convolution fusion | flops 4294967296 | bytes 17825792 | tf_op jit(solution)/shard_map/dot_general | solution.py:171
  77.6 19.4 %conditional.2 = (bf16[2,256,128]{2,1,0:T(8,128)(2,1)}) conditional(s32[]{:T(128)} %bitcast.5, bf16[2,256,128]{2,1,0:T(8,128)(2,1)S(1)} %slice_bitcast_fusion.1, bf16[2,256,128]{2,1,0:T(8,128)(2,1)S(1)} %slice_bitcast_fusion.1, bf16[2,256,128]{2,1,0:T(8,128)(2,1)S(1)} %slice_bitcast_fusion.1, ...), branch_computations={%region_2.3_spmd, %region_3.4_spmd, %region_4.5_spmd, %region_5.6_... | conditional | bytes 524336 | solution.py:31
  77.7 5.2 %collective-permute-start.9 = (bf16[2,256,128]{2,1,0:T(8,128)(2,1)S(1)}, bf16[2,256,128]{2,1,0:T(8,128)(2,1)}, u32[]{:S(2)}, u32[]{:S(2)}) collective-permute-start(bf16[2,256,128]{2,1,0:T(8,128)(2,1)S(1)} %param.9), channel_id=1, source_target_pairs={{0,80},{8,88},{16,64},{24,72},{32,112},{40,120},{48,96},{56,104},{... | collective-permute-start | bytes 393224 | tf_op jit(solution)/shard_map/cond/branch_9_fun/ppermute | solution.py:31
  82.9 14.2 %collective-permute-done.9 = bf16[2,256,128]{2,1,0:T(8,128)(2,1)} collective-permute-done((bf16[2,256,128]{2,1,0:T(8,128)(2,1)S(1)}, bf16[2,256,128]{2,1,0:T(8,128)(2,1)}, u32[]{:S(2)}, u32[]{:S(2)}) %collective-permute-start.9) | collective-permute-done | bytes 131104 | tf_op jit(solution)/shard_map/cond/branch_9_fun/ppermute | solution.py:31
  97.1 0.0 all-to-all-done.1
  97.1 0.0 copy-done.1
  97.1 3.0 %partial_rank_acts.1 = bf16[512,512]{1,0:T(8,128)(2,1)S(1)} custom-call(s32[16]{0:T(128)S(1)} %convert_add_fusion.slots_ref, bf16[512,1024]{1,0:T(8,128)(2,1)S(1)} %copy-done.1, bf16[32,64,1024]{2,1,0:T(8,128)(2,1)} %bitcast.10.refs_0_.refs_1_.refs_2_.refs_3_.refs_4_.refs_5_.refs_6_.refs_7_, ...), custom_call_target="tpu_custom_call" | custom-call | tf_op jit(solution)/shard_map/partial_rank_acts/pallas_call | solution.py:54
  100.1 0.0 copy-start.2
  100.1 0.8 copy-done.2
  100.9 0.0 copy-start.3
  100.9 0.0 copy-start.6
  100.9 0.0 all-gather.6.cloned.1.call-update
  100.9 4.5 %all-to-all-start.2 = ((bf16[16,2,64,512]{3,2,1,0:T(8,128)(2,1)}), bf16[16,2,64,512]{3,2,1,0:T(8,128)(2,1)}, u32[]{:S(2)}, u32[]{:S(2)}) async-start(bf16[16,2,64,512]{3,2,1,0:T(8,128)(2,1)} %bitcast.31), calls=%async_computation.2 | async-start | bytes 4194304 | tf_op jit(solution)/shard_map/all_to_all | solution.py:178
  106.0 0.0 copy-done.3
  106.0 0.1 dynamic_slice.3.lens_ref
  106.1 0.6 gather_fusion
  106.8 0.0 copy-done.6
  106.8 24.9 %conditional.3 = (bf16[2,256,128]{2,1,0:T(8,128)(2,1)}) conditional(s32[]{:T(128)} %bitcast.12, bf16[2,256,128]{2,1,0:T(8,128)(2,1)S(1)} %slice_bitcast_fusion, bf16[2,256,128]{2,1,0:T(8,128)(2,1)S(1)} %slice_bitcast_fusion, bf16[2,256,128]{2,1,0:T(8,128)(2,1)S(1)} %slice_bitcast_fusion, ...), branch_computations={%region_17.18_spmd, %region_18.19_spmd, %region_19.20_spmd, %regio... | conditional | bytes 524336 | solution.py:31
  106.8 2.6 %collective-permute-start.26 = (bf16[2,256,128]{2,1,0:T(8,128)(2,1)S(1)}, bf16[2,256,128]{2,1,0:T(8,128)(2,1)}, u32[]{:S(2)}, u32[]{:S(2)}) collective-permute-start(bf16[2,256,128]{2,1,0:T(8,128)(2,1)S(1)} %param.26), channel_id=1, source_target_pairs={{0,96},{8,104},{16,112},{24,120},{32,64},{40,72},{48,80},{56,88},{... | collective-permute-start | bytes 393224 | tf_op jit(solution)/shard_map/cond/branch_11_fun/ppermute | solution.py:31
  109.4 22.4 %collective-permute-done.26 = bf16[2,256,128]{2,1,0:T(8,128)(2,1)} collective-permute-done((bf16[2,256,128]{2,1,0:T(8,128)(2,1)S(1)}, bf16[2,256,128]{2,1,0:T(8,128)(2,1)}, u32[]{:S(2)}, u32[]{:S(2)}) %collective-permute-start.26) | collective-permute-done | bytes 131104 | tf_op jit(solution)/shard_map/cond/branch_11_fun/ppermute | solution.py:31
  131.7 1.0 pad_maximum_fusion.mate_ref
  132.7 0.0 all-to-all-done.2
  132.7 2.2 %all-gather.6.cloned.1.call-done = bf16[4096,512]{1,0:T(8,128)(2,1)} async-done(((bf16[512,512]{1,0:T(8,128)(2,1)}), bf16[4096,512]{1,0:T(8,128)(2,1)}) %all-gather.6.cloned.1.call-update) | async-done | bytes 4194320 | tf_op jit(solution)/shard_map/all_gather | solution.py:183
  134.9 7.5 %attend.1 = bf16[512,512]{1,0:T(8,128)(2,1)} custom-call(s32[16]{0:T(128)S(1)} %convert_add_fusion.slots_ref, s32[2]{0:T(128)S(1)} %dynamic_slice.3.lens_ref, s32[2]{0:T(128)S(1)} %compare_select_fusion.mates_ref, bf16[8,512,512]{2,1,0:T(8,128)(2,1)} %bitcast.32, f32[512,512]{1,0:T(8,128)} %fusion.6.base_ref, bf16[2,512,128]{2,1,0:T(8,128)(2,1)S(1)} %bitcast.29, ...), custom_call_target="tpu_custom_call" | custom-call | tf_op jit(solution)/shard_map/attend/pallas_call | solution.py:112
  (10 shorter events, 0.1 us)
Async XLA Ops:
  6.5 27.4 %copy-start = (bf16[32,64,512]{2,1,0:T(8,128)(2,1)S(1)}, bf16[32,64,512]{2,1,0:T(8,128)(2,1)}, u32[]{:S(2)}) copy-start(bf16[32,64,512]{2,1,0:T(8,128)(2,1)} %param.43) | copy-start | bytes 6291460
  6.5 56.1 %all-gather.4.cloned.1.call-start = ((), (), s32[]{:S(2)}) async-start(), calls=%async_computation.3 | async-start | bytes 9437184 | tf_op jit(solution)/shard_map/all_gather | solution.py:153
  27.9 4.8 %copy-start.4 = (s32[2]{0:T(128)S(1)}, s32[2]{0:T(128)}, u32[]{:S(2)}) copy-start(s32[2]{0:T(128)} %param.47) | copy-start | bytes 28
  27.9 69.2 %all-to-all-start.1 = ((bf16[16,2,64,1024]{3,2,1,0:T(8,128)(2,1)}), bf16[16,2,64,1024]{3,2,1,0:T(8,128)(2,1)}, u32[]{:S(2)}, u32[]{:S(2)}) async-start(bf16[16,2,64,1024]{3,2,1,0:T(8,128)(2,1)} %bitcast.30), calls=%async_computation.1 | async-start | bytes 8388608 | tf_op jit(solution)/shard_map/all_to_all | solution.py:165
  32.6 102.3 %all-gather.6.cloned.1.call-start = ((), (), s32[]{:S(2)}) async-start(), calls=%async_computation.4 | async-start | bytes 4718592 | tf_op jit(solution)/shard_map/all_gather | solution.py:183
  62.6 7.1 %copy-start.5 = (bf16[512,8192]{1,0:T(8,128)(2,1)S(1)}, bf16[512,8192]{1,0:T(8,128)(2,1)}, u32[]{:S(2)}) copy-start(bf16[512,8192]{1,0:T(8,128)(2,1)} %all-gather.4.cloned.1.call-done) | copy-start | bytes 25165828
  69.7 27.4 %copy-start.1 = (bf16[512,1024]{1,0:T(8,128)(2,1)S(1)}, bf16[512,1024]{1,0:T(8,128)(2,1)}, u32[]{:S(2)}) copy-start(bf16[512,1024]{1,0:T(8,128)(2,1)} %tokens_ref.1) | copy-start | bytes 3145732
  77.7 19.4 %collective-permute-start.9 = (bf16[2,256,128]{2,1,0:T(8,128)(2,1)S(1)}, bf16[2,256,128]{2,1,0:T(8,128)(2,1)}, u32[]{:S(2)}, u32[]{:S(2)}) collective-permute-start(bf16[2,256,128]{2,1,0:T(8,128)(2,1)S(1)} %param.9), channel_id=1, source_target_pairs={{0,80},{8,88},{16,64},{24,72},{32,112},{40,120},{48,96},{56,104},{... | collective-permute-start | bytes 393224 | tf_op jit(solution)/shard_map/cond/branch_9_fun/ppermute | solution.py:31
  100.1 0.8 copy-start.2
  100.9 5.1 %copy-start.3 = (s32[32]{0:T(128)S(1)}, s32[32]{0:T(128)}, u32[]{:S(2)}) copy-start(s32[32]{0:T(128)} %param.45) | copy-start | bytes 388
  100.9 5.9 %copy-start.6 = (s32[2]{0:T(128)S(1)}, s32[2]{0:T(128)}, u32[]{:S(2)}) copy-start(s32[2]{0:T(128)} %param.46) | copy-start | bytes 28
  100.9 31.8 %all-to-all-start.2 = ((bf16[16,2,64,512]{3,2,1,0:T(8,128)(2,1)}), bf16[16,2,64,512]{3,2,1,0:T(8,128)(2,1)}, u32[]{:S(2)}, u32[]{:S(2)}) async-start(bf16[16,2,64,512]{3,2,1,0:T(8,128)(2,1)} %bitcast.31), calls=%async_computation.2 | async-start | bytes 4194304 | tf_op jit(solution)/shard_map/all_to_all | solution.py:178
  106.8 24.9 %collective-permute-start.26 = (bf16[2,256,128]{2,1,0:T(8,128)(2,1)S(1)}, bf16[2,256,128]{2,1,0:T(8,128)(2,1)}, u32[]{:S(2)}, u32[]{:S(2)}) collective-permute-start(bf16[2,256,128]{2,1,0:T(8,128)(2,1)S(1)} %param.26), channel_id=1, source_target_pairs={{0,96},{8,104},{16,112},{24,120},{32,64},{40,72},{48,80},{56,88},{... | collective-permute-start | bytes 393224 | tf_op jit(solution)/shard_map/cond/branch_11_fun/ppermute | solution.py:31
Sparse Core Ops, SparseCore 0:
  9.1 53.5 all-gather.3
  101.1 33.8 all-gather.5

commit v3 on v2

--- a/solution.py
+++ b/solution.py
@@ -35,43 +35,189 @@
     return jnp.take(table, asked[:, :MOST_PER_INDEX].reshape(-1), axis=0, mode="clip")
 
 
-def partial_kernel(slots_ref, tokens_ref, *refs):
-    downs, out_ref = refs[:-1], refs[-1]
+def project_kernel(pieces, order_ref, query_weight_ref, keyval_weight_ref, *refs):
+    base_ref, keyval_ref, rows_ref, query_acc, keyval_acc, sems = refs[-6:]
+    step = pl.program_id(0)
+    last = len(pieces) - 1
+
+    def fetches(i):
+        copies, first = [], sum(pieces[:i])
+        for piece in range(pieces[i]):
+            source = refs[first + piece]
+            rows = pl.ds(piece * source.shape[0], source.shape[0])
+            copies.append(
+                pltpu.make_async_copy(source, rows_ref.at[i % 2, rows], sems.at[i % 2, piece])
+            )
+        return copies
+
+    @pl.when(step == 0)
+    def _():
+        for copy in fetches(0):
+            copy.start()
+        query_acc[...] = jnp.zeros_like(query_acc)
+        keyval_acc[...] = jnp.zeros_like(keyval_acc)
+
+    for i in range(len(pieces)):
+
+        @pl.when(step == i)
+        def _(i=i):
+            if i < last:
+                for copy in fetches(i + 1):
+                    copy.start()
+            for copy in fetches(i):
+                copy.wait()
+
+    rows = rows_ref[step % 2]
+    both = jnp.concatenate([keyval_weight_ref[0], keyval_weight_ref[1]], axis=1)
+    query_acc[...] += jnp.dot(rows, query_weight_ref[...], preferred_element_type=jnp.float32)
+    keyval_acc[...] += jnp.dot(rows, both, preferred_element_type=jnp.float32)
+
+    @pl.when(step == last)
+    def _():
+        width = keyval_ref.shape[2]
+        base_ref[...] = query_acc[...]
+        keyval_ref[0] = keyval_acc[:, :width].astype(keyval_ref.dtype)
+        keyval_ref[1] = keyval_acc[:, width:].astype(keyval_ref.dtype)
+
+
+def project(blocks, order, query_weight, keyval_weight):
+    rows, features = blocks[0][0].shape
+    pieces = tuple(len(block) for block in blocks)
+    arrays = [piece for block in blocks for piece in block]
+    columns = query_weight.shape[1]
+    width = keyval_weight.shape[2]
+    return pl.pallas_call(
+        partial(project_kernel, pieces),
+        out_shape=(
+            jax.ShapeDtypeStruct((rows, columns), jnp.float32),
+            jax.ShapeDtypeStruct((2, rows, width), jnp.bfloat16),
+        ),
+        grid_spec=pltpu.PrefetchScalarGridSpec(
+            num_scalar_prefetch=1,
+            grid=(len(blocks),),
+            in_specs=[
+                pl.BlockSpec((features, columns), lambda i, order_ref: (order_ref[i], 0)),
+                pl.BlockSpec((2, features, width), lambda i, order_ref: (0, order_ref[i], 0)),
+            ]
+            + [pl.BlockSpec(memory_space=pl.ANY)] * len(arrays),
+            out_specs=(
+                pl.BlockSpec((rows, columns), lambda i, *_: (0, 0)),
+                pl.BlockSpec((2, rows, width), lambda i, *_: (0, 0, 0)),
+            ),
+            scratch_shapes=[
+                pltpu.VMEM((2, rows, features), jnp.bfloat16),
+                pltpu.VMEM((rows, columns), jnp.float32),
+                pltpu.VMEM((rows, 2 * width), jnp.float32),
+                pltpu.SemaphoreType.DMA((2, max(pieces))),
+            ],
+        ),
+        compiler_params=pltpu.CompilerParams(vmem_limit_bytes=32 << 20),
+        name="project",
+    )(order, *[pltpu.with_memory_space_constraint(x, pltpu.HBM) for x in (query_weight, keyval_weight, *arrays)])
+
+
+def across_tensor(block, flip):
+    size = lax.axis_size("tensor")
+    return lax.ppermute(block, "tensor", [(source, source ^ flip) for source in range(size)])
+
+
+def along_column(block, step):
+    size = lax.axis_size("tensor")
+    return lax.ppermute(block, "tensor", [(source, (source + 2 * step) % size) for source in range(size)])
+
+
+def neighbour_features(tokens):
+    return along_column(tokens, 1), along_column(tokens, -1)
+
+
+def all_features(tokens, before, after):
+    size = lax.axis_size("tensor")
+    own = lax.axis_index("tensor")
+    half = tokens.shape[0] // 2
+    opposite = (along_column(before[:half], 1), along_column(after[half:], -1))
+    held = [(tokens,), (before,), (after,), opposite]
+    blocks, order = [], []
+    for offset, pieces in zip((0, size - 2, 2, 4), held):
+        index = (own + offset) % size
+        blocks += [pieces, tuple(across_tensor(piece, 1) for piece in pieces)]
+        order += [index, jnp.bitwise_xor(index, 1)]
+    return blocks, jnp.stack(order)
+
+
+def sum_over_tensor(keep, send, beside):
+    size = lax.axis_size("tensor")
+    pair = keep + across_tensor(send, 1)
+    small = pair.astype(jnp.bfloat16)
+    others = [across_tensor(small, flip) for flip in range(2, size, 2)]
+    extra = beside(small)
+    *others, extra = lax.optimization_barrier((*others, extra))
+    total = pair
+    for other in others:
+        total = total + other.astype(jnp.float32)
+    acts = total.astype(jnp.bfloat16)
+    return acts, across_tensor(acts, 1), extra
+
+
+def sum_over_tensor_plain(keep, send, core, extra):
+    both = jnp.stack([keep, send])
+    both = jnp.where(core == 0, both, both[::-1])
+    total = both
+    for flip in range(1, lax.axis_size("tensor")):
+        total = total + across_tensor(both, flip)
+    total = total.astype(jnp.bfloat16)
+    total = jnp.where(core == 0, total, total[::-1])
+    return total[0], total[1], extra
+
+
+def partial_kernel(slots_ref, core_ref, tokens_ref, *refs):
+    downs, keep_ref, send_ref = refs[:-2], refs[-2], refs[-1]
     rows = jnp.concatenate([d[0] for d in downs], axis=0)
-    out_ref[...] = lax.dot_general(
+    acts = lax.dot_general(
         tokens_ref[...], rows, (((1,), (1,)), ((), ())), preferred_element_type=jnp.float32
-    ).astype(out_ref.dtype)
-
-
-def partial_rank_acts(tokens, got_down, slots, resp_dev, rubrics):
+    )
+    kept = pl.program_id(0) == core_ref[0]
+
+    @pl.when(kept)
+    def _():
+        keep_ref[...] = acts
+
+    @pl.when(jnp.logical_not(kept))
+    def _():
+        send_ref[...] = acts
+
+
+def partial_rank_acts(tokens, got_down, slots, core, rubrics):
     rows, features = tokens.shape
     ranks = got_down.shape[1]
-    resp_len = rows // resp_dev
+    resp_len = rows // 2
 
     def down_spec(s):
-        return pl.BlockSpec((1, ranks, features), lambda j, slots_ref: (slots_ref[j * rubrics + s], 0, 0))
-
+        return pl.BlockSpec((1, ranks, features), lambda j, slots_ref, _: (slots_ref[j * rubrics + s], 0, 0))
+
+    half = jax.ShapeDtypeStruct((resp_len, rubrics * ranks), jnp.float32)
+    half_spec = pl.BlockSpec(half.shape, lambda j, *_: (0, 0))
     return pl.pallas_call(
         partial_kernel,
-        out_shape=jax.ShapeDtypeStruct((rows, rubrics * ranks), jnp.bfloat16),
+        out_shape=(half, half),
         grid_spec=pltpu.PrefetchScalarGridSpec(
-            num_scalar_prefetch=1,
-            grid=(resp_dev,),
-            in_specs=[pl.BlockSpec((resp_len, features), lambda j, slots_ref: (j, 0))]
+            num_scalar_prefetch=2,
+            grid=(2,),
+            in_specs=[pl.BlockSpec((resp_len, features), lambda j, *_: (j, 0))]
             + [down_spec(s) for s in range(rubrics)],
-            out_specs=pl.BlockSpec((resp_len, rubrics * ranks), lambda j, slots_ref: (j, 0)),
+            out_specs=(half_spec, half_spec),
         ),
         compiler_params=pltpu.CompilerParams(vmem_limit_bytes=32 << 20),
+        cost_estimate=pl.CostEstimate(flops=2 * rows * features * ranks * rubrics, bytes_accessed=4 << 20, transcendentals=0),
         name="partial_rank_acts",
-    )(slots, tokens, *([got_down] * rubrics))
+    )(slots, core, tokens, *([got_down] * rubrics))
 
 
 def attend_kernel(
-    slots_ref, lens_ref, mates_ref, partials_ref, base_ref, own_ref, mate_ref, *refs
+    slots_ref, lens_ref, mates_ref, core_ref, same_ref, other_ref, base_ref, own_ref, mate_ref, *refs
 ):
     ups, out_ref = refs[:-1], refs[-1]
     j = pl.program_id(0)
-    acts = jnp.sum(partials_ref[...].astype(jnp.float32), axis=0).astype(jnp.bfloat16)
+    acts = jnp.where(j == core_ref[0], same_ref[...], other_ref[...])
     up_rows = jnp.concatenate([u[0] for u in ups], axis=0)
     delta = jnp.dot(acts, up_rows, preferred_element_type=jnp.float32)
     queries = (base_ref[...] + delta).astype(jnp.bfloat16)
@@ -98,25 +244,26 @@
         )
 
 
-def attend(partials, base, keyval, mate_keyval, got_up, slots, own_lens, mate_lens, rubrics):
+def attend(acts, base, keyval, mate_keyvals, got_up, slots, own_lens, mate_lens, core, rubrics):
     rows, columns = base.shape
     resp_dev = own_lens.shape[0]
     resp_len = rows // resp_dev
-    shards = partials.shape[0]
     ranks = got_up.shape[1]
 
     def up_spec(s):
         return pl.BlockSpec((1, ranks, columns), lambda j, slots_ref, *_: (slots_ref[j * rubrics + s], 0, 0))
 
+    acts_spec = pl.BlockSpec(acts[0].shape, lambda j, *_: (0, 0))
     kv_spec = pl.BlockSpec((2, resp_len, HEAD_SIZE), lambda j, *_: (0, j, 0))
     return pl.pallas_call(
         attend_kernel,
         out_shape=jax.ShapeDtypeStruct((rows, columns), jnp.bfloat16),
         grid_spec=pltpu.PrefetchScalarGridSpec(
-            num_scalar_prefetch=3,
+            num_scalar_prefetch=4,
             grid=(resp_dev,),
             in_specs=[
-                pl.BlockSpec((shards, resp_len, rubrics * ranks), lambda j, *_: (0, j, 0)),
+                acts_spec,
+                acts_spec,
                 pl.BlockSpec((resp_len, columns), lambda j, *_: (j, 0)),
                 kv_spec,
                 kv_spec,
@@ -126,7 +273,7 @@
         ),
         compiler_params=pltpu.CompilerParams(vmem_limit_bytes=40 << 20),
         name="attend",
-    )(slots, own_lens, mate_lens, pltpu.with_memory_space_constraint(partials, pltpu.HBM), pltpu.with_memory_space_constraint(base, pltpu.HBM), keyval, mate_keyval, *([got_up] * rubrics))
+    )(slots, own_lens, mate_lens, core, *acts, pltpu.with_memory_space_constraint(base, pltpu.HBM), keyval, mate_keyvals, *([got_up] * rubrics))
 
 
 def on_device(
@@ -150,7 +297,7 @@
     slot_count = resp_dev * rubrics
     tok_rows = tokens.shape[0]
     resp_len = tok_rows // resp_dev
-    wide = lax.all_gather(tokens, "tensor", axis=1, tiled=True)
+    before, after = neighbour_features(tokens)
     slot_ids = response_rubrics.reshape(slot_count)
     owner_ids, local_ids, buffer_slot = slot_layout(slot_ids, adapters_by_owner)
     cells = lax.broadcasted_iota(jnp.int32, (owner_groups, LANES), 0) * MOST_PER_INDEX
@@ -162,34 +309,47 @@
     asked = lax.all_to_all(wanted, "dp", split_axis=0, concat_axis=0, tiled=True)
     shipped_down = take_asked(adapter_down_weight, asked)
     shipped_down = shipped_down.reshape(owner_groups, MOST_PER_INDEX, rank_extent, feature_shard)
+    shipped_down, before, after = lax.optimization_barrier((shipped_down, before, after))
     got_down = lax.all_to_all(shipped_down, "dp", split_axis=0, concat_axis=0, tiled=True)
     shipped_up = take_asked(adapter_up_weight, asked)
     shipped_up = shipped_up.reshape(owner_groups, MOST_PER_INDEX, rank_extent, head_columns)
-    keyval = jnp.einsum(
-        "tw,cwk->ctk", wide, key_value_weight, preferred_element_type=jnp.float32
-    ).astype(jnp.bfloat16)
-    base = jnp.dot(wide, query_weight, preferred_element_type=jnp.float32)
+    blocks, order = all_features(tokens, before, after)
+    base, keyval = project(blocks, order, query_weight, key_value_weight)
     own_keyval = keyval.reshape(2, resp_dev, resp_len, kv_cols)
-    own_keyval, base = lax.optimization_barrier((own_keyval, base))
     mate_first = from_partner(own_keyval[:, 0], partner_xor_mask[0])
     got_down, shipped_up, mate_first, own_keyval = lax.optimization_barrier(
         (got_down, shipped_up, mate_first, own_keyval)
     )
     got_up = lax.all_to_all(shipped_up, "dp", split_axis=0, concat_axis=0, tiled=True)
-    partials = partial_rank_acts(
-        tokens, got_down.reshape(-1, rank_extent, feature_shard), buffer_slot, resp_dev, rubrics
-    )
-    partials, own_keyval = lax.optimization_barrier((partials, own_keyval))
-    partials = lax.all_gather(partials, "tensor", axis=0)
-    mate_second = from_partner(own_keyval[:, 1], partner_xor_mask[1])
+    core = jnp.bitwise_and(lax.axis_index("tensor"), 1)
+    keep, send = partial_rank_acts(
+        tokens, got_down.reshape(-1, rank_extent, feature_shard), buffer_slot, core.reshape(1), rubrics
+    )
+
+    def split_sum(operands):
+        keep, send, second = operands
+
+        def beside(small):
+            block, _ = lax.optimization_barrier((second, small))
+            return from_partner(block, partner_xor_mask[1])
+
+        return sum_over_tensor(keep, send, beside)
+
+    def plain_sum(operands):
+        keep, send, second = operands
+        return sum_over_tensor_plain(keep, send, core, from_partner(second, partner_xor_mask[1]))
+
+    same, other, mate_second = lax.cond(
+        lengths[0] >= 1, split_sum, plain_sum, (keep, send, own_keyval[:, 1])
+    )
     mate_keyval = jnp.concatenate([mate_first, mate_second], axis=1)
     own_lens = lax.dynamic_slice_in_dim(lengths, own_index * resp_dev, resp_dev)
     mate_index = partner_dev * resp_dev + jnp.arange(resp_dev, dtype=jnp.int32)
     mate_lens = jnp.take(lengths, mate_index, axis=0, mode="clip")
     mate_lens = jnp.where(partner_attend_mask == 1, mate_lens, 0)
     return attend(
-        partials, base, keyval, mate_keyval, got_up.reshape(-1, rank_extent, head_columns),
-        buffer_slot, own_lens, mate_lens, rubrics,
+        (same, other), base, keyval, mate_keyval, got_up.reshape(-1, rank_extent, head_columns),
+        buffer_slot, own_lens, mate_lens, core.reshape(1), rubrics,
     )
 
 

time: 150 us -> 146 us (0.973)
  starting transfers between devices: 17 us -> 37.9 us
  waiting for transfers between devices: 66.1 us -> 49.3 us
  matrix products: 15 us -> 0 us
  between operations: 14.8 us -> 0.23 us
  Pallas kernels: 10.5 us -> 24.9 us
  other arithmetic: 1.4 us -> 5.15 us
  local copies, waits for them, and re-layouts: 10.5 us -> 13.4 us
    all_gather x2 -> x0, waiting for transfers between devices: 28.8 us -> none  [the longest x1 26.6 us: on_device(): wide = lax.all_gather(tokens, 'tensor', axis=1, tiled=True)]
    ppermute x0 -> x14, starting transfers between devices: none -> 18.3 us  [the longest x10 10.8 us: across_tensor(): lax.ppermute(block, 'tensor', [(source, source ^ flip) for source in rang...]
    ppermute x0 -> x14, waiting for transfers between devices: none -> 17.7 us  [the longest x4 14.2 us: along_column(): lax.ppermute(block, 'tensor', [(source, (source + 2 * step) % size) for s...]
    dot_general x2 -> x0, matrix products: 15 us -> none  [the longest x1 7.92 us: on_device(): base = jnp.dot(wide, query_weight, preferred_element_type=jnp.float32)]
    pallas_call x1 -> x2, Pallas kernels: 3.04 us -> 17.9 us  [the longest x1 13.9 us: project(): pl.pallas_call(partial(project_kernel, pieces), out_shape=(jax.ShapeDtype...]
    ppermute x2, waiting for transfers between devices: 36.5 us -> 31.6 us  [from_partner(): return lax.switch(mask - 1, moves, block)]
    convert_element_type x0 -> x2, other arithmetic: none -> 3.1 us  [the longest x1 1.93 us: sum_over_tensor(): acts = total.astype(jnp.bfloat16)]
    all_to_all x1, starting transfers between devices: 4.77 us -> 6.94 us  [on_device(): lax.all_to_all(shipped_down, 'dp', split_axis=0, concat_axis=0, tiled=True)]
  transfers between devices with their start and end apart: 6 -> 18, of which waited for: 4 -> 7; matrix products, arithmetic and copies ran while one was open for 17% -> 11% of each run, Pallas kernels for 0% -> 12%
where the time goes in v3:
time: 146 us; the launch traced here: 145 us
  waiting for transfers between devices  49.3 us (34%)
  starting transfers between devices  37.9 us (26%)
  Pallas kernels  24.9 us (17%)
  local copies, waits for them, and re-layouts  13.4 us (9%)
  blocking collectives  13 us (9%)
  other arithmetic  5.15 us (4%)
    ppermute x2, waiting for transfers between devices, from_partner(): return lax.switch(mask - 1, moves, block)  31.6 us
    ppermute x4, waiting for transfers between devices, along_column(): lax.ppermute(block, 'tensor', [(source, (source + 2 * step) % size) for s...  14.2 us
    pallas_call x1, Pallas kernels, project(): pl.pallas_call(partial(project_kernel, pieces), out_shape=(jax.ShapeDtype...  13.9 us
    all_to_all x1, blocking collectives, on_device(): lax.all_to_all(wanted, 'dp', split_axis=0, concat_axis=0, tiled=True)  13 us
    ppermute x10, starting transfers between devices, across_tensor(): lax.ppermute(block, 'tensor', [(source, source ^ flip) for source in rang...  10.8 us
    ppermute x2, starting transfers between devices, from_partner(): return lax.switch(mask - 1, moves, block)  8.17 us
    ppermute x4, starting transfers between devices, along_column(): lax.ppermute(block, 'tensor', [(source, (source + 2 * step) % size) for s...  7.47 us
    gather x2, local copies, waits for them, and re-layouts, take_asked(): jnp.take(table, asked[:, :MOST_PER_INDEX].reshape(-1), axis=0, mode='clip')  7.03 us
  transfers between devices with their start and end apart: 18, of which 7 were waited for; matrix products, arithmetic and copies ran while one was open for 11% of the time, Pallas kernels for 12%

profile of v3, /device:TPU:1, one launch (start us, length us, event | category | flops | bytes accessed | tf_op | source)
XLA Modules:
  0.0 144.7 jit_solution(14038316134128852271)
XLA Ops:
  0.0 0.0 copy-start
  0.0 2.5 %collective-permute-start.57 = (bf16[512,1024]{1,0:T(8,128)(2,1)}, bf16[512,1024]{1,0:T(8,128)(2,1)S(1)}, u32[]{:S(2)}, u32[]{:S(2)}) collective-permute-start(bf16[512,1024]{1,0:T(8,128)(2,1)} %tokens_ref.1), channel_id=1, source_target_pairs={{0,2},{1,3},{2,4},{3,5},{4,6},{5,7},{6,0},{7,1},{8,10},{9,11},{10,... | collective-permute-start | bytes 3145736 | tf_op jit(solution)/shard_map/ppermute | solution.py:126
  2.5 2.2 %collective-permute-start.58 = (bf16[512,1024]{1,0:T(8,128)(2,1)}, bf16[512,1024]{1,0:T(8,128)(2,1)}, u32[]{:S(2)}, u32[]{:S(2)}) collective-permute-start(bf16[512,1024]{1,0:T(8,128)(2,1)} %tokens_ref.1), channel_id=1, source_target_pairs={{0,6},{1,7},{2,0},{3,1},{4,2},{5,3},{6,4},{7,5},{8,14},{9,15},{10,... | collective-permute-start | bytes 3145736 | tf_op jit(solution)/shard_map/ppermute | solution.py:126
  4.7 0.8 reshape.188
  5.4 0.2 and_reduce_fusion
  5.6 0.1 add_select_fusion
  5.7 0.1 select_reduce_fusion
  5.8 13.0 %all_to_all.22 = s32[16,1,128]{2,1,0:T(1,128)S(1)} all-to-all(s32[16,1,128]{2,1,0:T(1,128)S(1)} %bitcast.44), channel_id=1, replica_groups=mesh['dp'=16,'tensor'=8] {'dp'}, dimensions={0} | all-to-all | bytes 16384 | tf_op jit(solution)/shard_map/all_to_all | solution.py:309
  18.8 0.1 reshape.206
  18.9 5.0 %gather_fusion.1 = bf16[32,64,1024]{2,1,0:T(8,128)(2,1)} fusion(bf16[32,64,1024]{2,1,0:T(8,128)(2,1)} %param.59, s32[1024]{0:T(1024)S(1)} %pad_clamp_fusion), kind=kCustom, calls=%fused_computation.1 | custom fusion | bytes 8388736 | tf_op jit(solution)/shard_map/jit(_take)/gather | solution.py:35
  23.9 3.7 %collective-permute-done.57.refs_2_ = bf16[512,1024]{1,0:T(8,128)(2,1)S(1)} collective-permute-done((bf16[512,1024]{1,0:T(8,128)(2,1)}, bf16[512,1024]{1,0:T(8,128)(2,1)S(1)}, u32[]{:S(2)}, u32[]{:S(2)}) %collective-permute-start.57) | collective-permute-done | bytes 1048608 | tf_op jit(solution)/shard_map/ppermute | solution.py:126
  27.7 0.0 collective-permute-done.58.refs_4_
  27.7 1.0 copy-done.5
  28.7 6.9 %all-to-all-start.1 = ((bf16[16,2,64,1024]{3,2,1,0:T(8,128)(2,1)}), bf16[16,2,64,1024]{3,2,1,0:T(8,128)(2,1)}, u32[]{:S(2)}, u32[]{:S(2)}) async-start(bf16[16,2,64,1024]{3,2,1,0:T(8,128)(2,1)} %bitcast.40), calls=%async_computation.1 | async-start | bytes 8388608 | tf_op jit(solution)/shard_map/all_to_all | solution.py:313
  35.7 1.6 %collective-permute-start.59 = (bf16[512,1024]{1,0:T(8,128)(2,1)S(1)}, bf16[512,1024]{1,0:T(8,128)(2,1)}, u32[]{:S(2)}, u32[]{:S(2)}) collective-permute-start(bf16[512,1024]{1,0:T(8,128)(2,1)S(1)} %copy-done.1), channel_id=1, source_target_pairs={{0,1},{1,0},{2,3},{3,2},{4,5},{5,4},{6,7},{7,6},{8,9},{9,8},{10,11... | collective-permute-start | bytes 3145736 | tf_op jit(solution)/shard_map/ppermute | solution.py:121
  37.3 1.1 slice.37
  38.3 0.1 collective-permute-start.62
  38.5 1.1 slice.38
  39.5 2.7 %collective-permute-start.63 = (bf16[256,1024]{1,0:T(8,128)(2,1)S(1)}, bf16[256,1024]{1,0:T(8,128)(2,1)}, u32[]{:S(2)}, u32[]{:S(2)}) collective-permute-start(bf16[256,1024]{1,0:T(8,128)(2,1)S(1)} %slice.38), channel_id=1, source_target_pairs={{0,6},{1,7},{2,0},{3,1},{4,2},{5,3},{6,4},{7,5},{8,14},{9,15},{10,... | collective-permute-start | bytes 1572872 | tf_op jit(solution)/shard_map/ppermute | solution.py:126
  42.2 0.6 collective-permute-start.60
  42.8 0.0 collective-permute-start.61
  42.8 10.5 %collective-permute-done.62.refs_6_ = bf16[256,1024]{1,0:T(8,128)(2,1)} collective-permute-done((bf16[256,1024]{1,0:T(8,128)(2,1)S(1)}, bf16[256,1024]{1,0:T(8,128)(2,1)}, u32[]{:S(2)}, u32[]{:S(2)}) %collective-permute-start.62) | collective-permute-done | bytes 524320 | tf_op jit(solution)/shard_map/ppermute | solution.py:126
  53.3 0.8 collective-permute-start.64
  54.1 0.0 collective-permute-done.63.refs_7_
  54.1 0.3 collective-permute-start.65
  54.4 0.1 stack.44.order_ref
  54.5 2.0 %gather_fusion.2 = bf16[32,64,512]{2,1,0:T(8,128)(2,1)} fusion(bf16[32,64,512]{2,1,0:T(8,128)(2,1)S(1)} %copy-done, s32[1024]{0:T(1024)S(1)} %pad_clamp_fusion), kind=kCustom, calls=%fused_computation.2 | custom fusion | bytes 4194432 | tf_op jit(solution)/shard_map/jit(_take)/gather | solution.py:35
  56.5 0.0 collective-permute-done.59.refs_1_
  56.5 0.0 collective-permute-done.64.refs_8_
  56.5 0.2 collective-permute-done.65.refs_9_
  56.7 0.0 collective-permute-done.60.refs_3_
  56.7 0.0 collective-permute-done.61.refs_5_
  56.7 13.9 %project.1 = (f32[512,512]{1,0:T(8,128)S(1)}, bf16[2,512,128]{2,1,0:T(8,128)(2,1)S(1)}) custom-call(s32[8]{0:T(128)S(1)} %stack.44.order_ref, bf16[8192,512]{1,0:T(8,128)(2,1)} %query_weight_ref.1, bf16[2,8192,128]{2,1,0:T(8,128)(2,1)} %keyval_weight_ref.1, bf16[512,1024]{1,0:T(8,128)(2,1)} %tokens_ref.1, bf16[512,1024]{1,0:T(8,128)(2,1)} %collective-permute-done.59.refs_1_, ...), custom_call_target="tpu_custom_call" | custom-call | tf_op jit(solution)/shard_map/project/pallas_call | solution.py:89
  70.6 1.0 copy-done.3
  71.6 27.5 %conditional.4 = (bf16[2,256,128]{2,1,0:T(8,128)(2,1)}) conditional(s32[]{:T(128)} %bitcast.13, bf16[2,256,128]{2,1,0:T(8,128)(2,1)S(1)} %slice_bitcast_fusion.3, bf16[2,256,128]{2,1,0:T(8,128)(2,1)S(1)} %slice_bitcast_fusion.3, bf16[2,256,128]{2,1,0:T(8,128)(2,1)S(1)} %slice_bitcast_fusion.3, ...), branch_computations={%region_2.3_spmd, %region_3.4_spmd, %region_4.5_spmd, %region_5.6_... | conditional | bytes 524336 | solution.py:31
  71.6 5.3 %collective-permute-start.13 = (bf16[2,256,128]{2,1,0:T(8,128)(2,1)S(1)}, bf16[2,256,128]{2,1,0:T(8,128)(2,1)}, u32[]{:S(2)}, u32[]{:S(2)}) collective-permute-start(bf16[2,256,128]{2,1,0:T(8,128)(2,1)S(1)} %param.13), channel_id=1, source_target_pairs={{0,112},{8,120},{16,96},{24,104},{32,80},{40,88},{48,64},{56,72},{... | collective-permute-start | bytes 393224 | tf_op jit(solution)/shard_map/cond/branch_13_fun/ppermute | solution.py:31
  76.9 22.2 %collective-permute-done.13 = bf16[2,256,128]{2,1,0:T(8,128)(2,1)} collective-permute-done((bf16[2,256,128]{2,1,0:T(8,128)(2,1)S(1)}, bf16[2,256,128]{2,1,0:T(8,128)(2,1)}, u32[]{:S(2)}, u32[]{:S(2)}) %collective-permute-start.13) | collective-permute-done | bytes 131104 | tf_op jit(solution)/shard_map/cond/branch_13_fun/ppermute | solution.py:31
  99.1 0.0 all-to-all-done.1
  99.1 4.4 %all-to-all-start.2 = ((bf16[16,2,64,512]{3,2,1,0:T(8,128)(2,1)}), bf16[16,2,64,512]{3,2,1,0:T(8,128)(2,1)}, u32[]{:S(2)}, u32[]{:S(2)}) async-start(bf16[16,2,64,512]{3,2,1,0:T(8,128)(2,1)} %bitcast.41), calls=%async_computation.2 | async-start | bytes 4194304 | tf_op jit(solution)/shard_map/all_to_all | solution.py:323
  103.6 0.1 dynamic_slice.3.lens_ref
  103.7 0.7 iota_add_fusion
  104.4 0.6 gather_fusion
  105.0 0.0 copy-start.8
  105.0 4.0 %partial_rank_acts.1 = (f32[256,512]{1,0:T(8,128)}, f32[256,512]{1,0:T(8,128)}) custom-call(s32[16]{0:T(128)S(1)} %convert_add_fusion.slots_ref, s32[1]{0:T(128)} %bitcast.6.core_ref, bf16[512,1024]{1,0:T(8,128)(2,1)S(1)} %copy-done.2, bf16[32,64,1024]{2,1,0:T(8,128)(2,1)} %bitcast.24.refs_0_.refs_1_.refs_2_.refs_3_.refs_4_.refs_5_.refs_6_.refs_7_, ...), custom_call_target="tpu_custom_call" | custom-call | flops 536870912 | bytes 4194304 | tf_op jit(solution)/shard_map/partial_rank_acts/pallas_call | solution.py:199
  109.0 27.7 %conditional.5 = (bf16[256,512]{1,0:T(8,128)(2,1)}, bf16[256,512]{1,0:T(8,128)(2,1)}, bf16[2,256,128]{2,1,0:T(8,128)(2,1)}) conditional(s32[]{:T(128)} %bitcast.7, (s32[]{:T(128)}, f32[256,512]{1,0:T(8,128)}, f32[256,512]{1,0:T(8,128)}, s32[2]{0:T(128)S(1)}, bf16[2,256,128]{2,1,0:T(8,128)(2,1)S(1)}) %tuple.206, (f32[256,512]{1,0:T(8,128)}, ...), branch_computations={%region_17.33_spmd, %region_33.49_spmd} | conditional | flops 3145731 | bytes 45089164 | solution.py:342
  109.3 2.8 %collective-permute-start.52 = (f32[256,512]{1,0:T(8,128)}, f32[256,512]{1,0:T(8,128)S(1)}, u32[]{:S(2)}, u32[]{:S(2)}) collective-permute-start(f32[256,512]{1,0:T(8,128)} %get-tuple-element.122), channel_id=1, source_target_pairs={{0,1},{1,0},{2,3},{3,2},{4,5},{5,4},{6,7},{7,6},{8,9},{9,8},{10,11... | collective-permute-start | bytes 1572872 | tf_op jit(solution)/shard_map/cond/branch_1_fun/ppermute | solution.py:121
  112.1 1.7 %collective-permute-done.52 = f32[256,512]{1,0:T(8,128)S(1)} collective-permute-done((f32[256,512]{1,0:T(8,128)}, f32[256,512]{1,0:T(8,128)S(1)}, u32[]{:S(2)}, u32[]{:S(2)}) %collective-permute-start.52) | collective-permute-done | bytes 524320 | tf_op jit(solution)/shard_map/cond/branch_1_fun/ppermute | solution.py:121
  113.8 1.2 fusion
  115.0 0.1 collective-permute-start.53
  115.1 1.9 %collective-permute-start.54 = (bf16[256,512]{1,0:T(8,128)(2,1)S(1)}, bf16[256,512]{1,0:T(8,128)(2,1)}, u32[]{:S(2)}, u32[]{:S(2)}) collective-permute-start(bf16[256,512]{1,0:T(8,128)(2,1)S(1)} %get-tuple-element.158), channel_id=1, source_target_pairs={{0,4},{1,5},{2,6},{3,7},{4,0},{5,1},{6,2},{7,3},{8,12},{9,13},{10,... | collective-permute-start | bytes 786440 | tf_op jit(solution)/shard_map/cond/branch_1_fun/ppermute | solution.py:121
  117.0 2.0 %collective-permute-start.55 = (bf16[256,512]{1,0:T(8,128)(2,1)S(1)}, bf16[256,512]{1,0:T(8,128)(2,1)}, u32[]{:S(2)}, u32[]{:S(2)}) collective-permute-start(bf16[256,512]{1,0:T(8,128)(2,1)S(1)} %get-tuple-element.158), channel_id=1, source_target_pairs={{0,6},{1,7},{2,4},{3,5},{4,2},{5,3},{6,0},{7,1},{8,14},{9,15},{10,... | collective-permute-start | bytes 786440 | tf_op jit(solution)/shard_map/cond/branch_1_fun/ppermute | solution.py:121
  118.9 0.6 slice.26
  120.0 12.4 %conditional.1 = (bf16[2,256,128]{2,1,0:T(8,128)(2,1)}) conditional(s32[]{:T(128)} %bitcast.5, bf16[2,256,128]{2,1,0:T(8,128)(2,1)S(1)} %get-tuple-element.125, bf16[2,256,128]{2,1,0:T(8,128)(2,1)S(1)} %get-tuple-element.125, bf16[2,256,128]{2,1,0:T(8,128)(2,1)S(1)} %get-tuple-element.125, ...), branch_computations={%region_34.34_spmd, %region_35.35_spmd, %region_36.36_spmd, %regio... | conditional | bytes 524336 | solution.py:31
  120.1 2.9 %collective-permute-start.32 = (bf16[2,256,128]{2,1,0:T(8,128)(2,1)S(1)}, bf16[2,256,128]{2,1,0:T(8,128)(2,1)}, u32[]{:S(2)}, u32[]{:S(2)}) collective-permute-start(bf16[2,256,128]{2,1,0:T(8,128)(2,1)S(1)} %param.33), channel_id=1, source_target_pairs={{0,24},{8,16},{16,8},{24,0},{32,56},{40,48},{48,40},{56,32},{64,88... | collective-permute-start | bytes 393224 | tf_op jit(solution)/shard_map/cond/branch_1_fun/cond/branch_2_fun/ppermute | solution.py:31
  123.0 9.5 %collective-permute-done.32 = bf16[2,256,128]{2,1,0:T(8,128)(2,1)} collective-permute-done((bf16[2,256,128]{2,1,0:T(8,128)(2,1)S(1)}, bf16[2,256,128]{2,1,0:T(8,128)(2,1)}, u32[]{:S(2)}, u32[]{:S(2)}) %collective-permute-start.32) | collective-permute-done | bytes 131104 | tf_op jit(solution)/shard_map/cond/branch_1_fun/cond/branch_2_fun/ppermute | solution.py:31
  132.4 0.0 collective-permute-done.53
  132.4 0.0 collective-permute-done.54
  132.4 0.0 collective-permute-done.55
  132.4 1.9 %add_convert_fusion.1 = bf16[256,512]{1,0:T(8,128)(2,1)} fusion(bf16[256,512]{1,0:T(8,128)(2,1)} %collective-permute-done.55, bf16[256,512]{1,0:T(8,128)(2,1)} %collective-permute-done.54, f32[256,512]{1,0:T(8,128)S(1)} %get-tuple-element.159, bf16[256,512]{1,0:T(8,128)(2,1)S(1)} %collective-permute-done.53), kind=kLoop, calls=%fused_computation.9 | loop fusion | flops 917504 | bytes 1572864 | tf_op jit(solution)/shard_map/cond/branch_1_fun/convert_element_type | solution.py:157
  134.4 0.8 collective-permute-start.56
  135.2 1.5 %collective-permute-done.56 = bf16[256,512]{1,0:T(8,128)(2,1)} collective-permute-done((bf16[256,512]{1,0:T(8,128)(2,1)}, bf16[256,512]{1,0:T(8,128)(2,1)}, u32[]{:S(2)}, u32[]{:S(2)}) %collective-permute-start.56) | collective-permute-done | bytes 262176 | tf_op jit(solution)/shard_map/cond/branch_1_fun/ppermute | solution.py:121
  136.7 1.0 pad_maximum_fusion.1.mate_ref
  137.7 0.0 all-to-all-done.2
  137.7 7.0 %attend.1 = bf16[512,512]{1,0:T(8,128)(2,1)} custom-call(s32[16]{0:T(128)S(1)} %convert_add_fusion.slots_ref, s32[2]{0:T(128)S(1)} %dynamic_slice.3.lens_ref, s32[2]{0:T(128)S(1)} %compare_select_fusion.mates_ref, s32[1]{0:T(128)} %bitcast.6.core_ref, bf16[256,512]{1,0:T(8,128)(2,1)} %get-tuple-element.152.same_ref, ...), custom_call_target="tpu_custom_call" | custom-call | tf_op jit(solution)/shard_map/attend/pallas_call | solution.py:258
  (23 shorter events, 0.1 us)
Async XLA Ops:
  0.0 54.5 %copy-start = (bf16[32,64,512]{2,1,0:T(8,128)(2,1)S(1)}, bf16[32,64,512]{2,1,0:T(8,128)(2,1)}, u32[]{:S(2)}) copy-start(bf16[32,64,512]{2,1,0:T(8,128)(2,1)} %param.60) | copy-start | bytes 6291460
  0.0 27.7 %collective-permute-start.57 = (bf16[512,1024]{1,0:T(8,128)(2,1)}, bf16[512,1024]{1,0:T(8,128)(2,1)S(1)}, u32[]{:S(2)}, u32[]{:S(2)}) collective-permute-start(bf16[512,1024]{1,0:T(8,128)(2,1)} %tokens_ref.1), channel_id=1, source_target_pairs={{0,2},{1,3},{2,4},{3,5},{4,6},{5,7},{6,0},{7,1},{8,10},{9,11},{10,... | collective-permute-start | bytes 3145736 | tf_op jit(solution)/shard_map/ppermute | solution.py:126
  2.5 25.2 %collective-permute-start.58 = (bf16[512,1024]{1,0:T(8,128)(2,1)}, bf16[512,1024]{1,0:T(8,128)(2,1)}, u32[]{:S(2)}, u32[]{:S(2)}) collective-permute-start(bf16[512,1024]{1,0:T(8,128)(2,1)} %tokens_ref.1), channel_id=1, source_target_pairs={{0,6},{1,7},{2,0},{3,1},{4,2},{5,3},{6,4},{7,5},{8,14},{9,15},{10,... | collective-permute-start | bytes 3145736 | tf_op jit(solution)/shard_map/ppermute | solution.py:126
  27.7 1.0 copy-start.5
  28.7 7.0 %copy-start.1 = (bf16[512,1024]{1,0:T(8,128)(2,1)S(1)}, bf16[512,1024]{1,0:T(8,128)(2,1)}, u32[]{:S(2)}) copy-start(bf16[512,1024]{1,0:T(8,128)(2,1)} %tokens_ref.1) | copy-start | bytes 3145732
  28.7 25.7 %copy-start.7 = (s32[2]{0:T(128)S(1)}, s32[2]{0:T(128)}, u32[]{:S(2)}) copy-start(s32[2]{0:T(128)} %param.64) | copy-start | bytes 28
  28.7 70.4 %all-to-all-start.1 = ((bf16[16,2,64,1024]{3,2,1,0:T(8,128)(2,1)}), bf16[16,2,64,1024]{3,2,1,0:T(8,128)(2,1)}, u32[]{:S(2)}, u32[]{:S(2)}) async-start(bf16[16,2,64,1024]{3,2,1,0:T(8,128)(2,1)} %bitcast.40), calls=%async_computation.1 | async-start | bytes 8388608 | tf_op jit(solution)/shard_map/all_to_all | solution.py:313
  35.7 20.8 %collective-permute-start.59 = (bf16[512,1024]{1,0:T(8,128)(2,1)S(1)}, bf16[512,1024]{1,0:T(8,128)(2,1)}, u32[]{:S(2)}, u32[]{:S(2)}) collective-permute-start(bf16[512,1024]{1,0:T(8,128)(2,1)S(1)} %copy-done.1), channel_id=1, source_target_pairs={{0,1},{1,0},{2,3},{3,2},{4,5},{5,4},{6,7},{7,6},{8,9},{9,8},{10,11... | collective-permute-start | bytes 3145736 | tf_op jit(solution)/shard_map/ppermute | solution.py:121
  38.3 14.9 %collective-permute-start.62 = (bf16[256,1024]{1,0:T(8,128)(2,1)S(1)}, bf16[256,1024]{1,0:T(8,128)(2,1)}, u32[]{:S(2)}, u32[]{:S(2)}) collective-permute-start(bf16[256,1024]{1,0:T(8,128)(2,1)S(1)} %slice.37), channel_id=1, source_target_pairs={{0,2},{1,3},{2,4},{3,5},{4,6},{5,7},{6,0},{7,1},{8,10},{9,11},{10,... | collective-permute-start | bytes 1572872 | tf_op jit(solution)/shard_map/ppermute | solution.py:126
  39.5 14.5 %collective-permute-start.63 = (bf16[256,1024]{1,0:T(8,128)(2,1)S(1)}, bf16[256,1024]{1,0:T(8,128)(2,1)}, u32[]{:S(2)}, u32[]{:S(2)}) collective-permute-start(bf16[256,1024]{1,0:T(8,128)(2,1)S(1)} %slice.38), channel_id=1, source_target_pairs={{0,6},{1,7},{2,0},{3,1},{4,2},{5,3},{6,4},{7,5},{8,14},{9,15},{10,... | collective-permute-start | bytes 1572872 | tf_op jit(solution)/shard_map/ppermute | solution.py:126
  42.2 14.5 %collective-permute-start.60 = (bf16[512,1024]{1,0:T(8,128)(2,1)}, bf16[512,1024]{1,0:T(8,128)(2,1)}, u32[]{:S(2)}, u32[]{:S(2)}) collective-permute-start(bf16[512,1024]{1,0:T(8,128)(2,1)} %copy-done.5), channel_id=1, source_target_pairs={{0,1},{1,0},{2,3},{3,2},{4,5},{5,4},{6,7},{7,6},{8,9},{9,8},{10,11... | collective-permute-start | bytes 3145736 | tf_op jit(solution)/shard_map/ppermute | solution.py:121
  42.8 13.9 %collective-permute-start.61 = (bf16[512,1024]{1,0:T(8,128)(2,1)}, bf16[512,1024]{1,0:T(8,128)(2,1)}, u32[]{:S(2)}, u32[]{:S(2)}) collective-permute-start(bf16[512,1024]{1,0:T(8,128)(2,1)} %collective-permute-done.58.refs_4_), channel_id=1, source_target_pairs={{0,1},{1,0},{2,3},{3,2},{4,5},{5,4},{6,7},{7,6},{8,9},{9,8},{10,11... | collective-permute-start | bytes 3145736 | tf_op jit(solution)/shard_map/ppermute | solution.py:121
  53.3 3.2 %collective-permute-start.64 = (bf16[256,1024]{1,0:T(8,128)(2,1)}, bf16[256,1024]{1,0:T(8,128)(2,1)}, u32[]{:S(2)}, u32[]{:S(2)}) collective-permute-start(bf16[256,1024]{1,0:T(8,128)(2,1)} %collective-permute-done.62.refs_6_), channel_id=1, source_target_pairs={{0,1},{1,0},{2,3},{3,2},{4,5},{5,4},{6,7},{7,6},{8,9},{9,8},{10,11... | collective-permute-start | bytes 1572872 | tf_op jit(solution)/shard_map/ppermute | solution.py:121
  54.1 2.6 %collective-permute-start.65 = (bf16[256,1024]{1,0:T(8,128)(2,1)}, bf16[256,1024]{1,0:T(8,128)(2,1)}, u32[]{:S(2)}, u32[]{:S(2)}) collective-permute-start(bf16[256,1024]{1,0:T(8,128)(2,1)} %collective-permute-done.63.refs_7_), channel_id=1, source_target_pairs={{0,1},{1,0},{2,3},{3,2},{4,5},{5,4},{6,7},{7,6},{8,9},{9,8},{10,11... | collective-permute-start | bytes 1572872 | tf_op jit(solution)/shard_map/ppermute | solution.py:121
  70.6 1.0 copy-start.3
  71.6 32.0 %copy-start.4 = (s32[32]{0:T(128)S(1)}, s32[32]{0:T(128)}, u32[]{:S(2)}) copy-start(s32[32]{0:T(128)} %param.62) | copy-start | bytes 388
  71.6 33.4 %copy-start.6 = (s32[2]{0:T(128)S(1)}, s32[2]{0:T(128)}, u32[]{:S(2)}) copy-start(s32[2]{0:T(128)} %param.63) | copy-start | bytes 28
  71.6 33.4 %copy-start.2 = (bf16[512,1024]{1,0:T(8,128)(2,1)S(1)}, bf16[512,1024]{1,0:T(8,128)(2,1)}, u32[]{:S(2)}) copy-start(bf16[512,1024]{1,0:T(8,128)(2,1)} %tokens_ref.1) | copy-start | bytes 3145732
  71.6 27.4 %collective-permute-start.13 = (bf16[2,256,128]{2,1,0:T(8,128)(2,1)S(1)}, bf16[2,256,128]{2,1,0:T(8,128)(2,1)}, u32[]{:S(2)}, u32[]{:S(2)}) collective-permute-start(bf16[2,256,128]{2,1,0:T(8,128)(2,1)S(1)} %param.13), channel_id=1, source_target_pairs={{0,112},{8,120},{16,96},{24,104},{32,80},{40,88},{48,64},{56,72},{... | collective-permute-start | bytes 393224 | tf_op jit(solution)/shard_map/cond/branch_13_fun/ppermute | solution.py:31
  99.1 38.6 %all-to-all-start.2 = ((bf16[16,2,64,512]{3,2,1,0:T(8,128)(2,1)}), bf16[16,2,64,512]{3,2,1,0:T(8,128)(2,1)}, u32[]{:S(2)}, u32[]{:S(2)}) async-start(bf16[16,2,64,512]{3,2,1,0:T(8,128)(2,1)} %bitcast.41), calls=%async_computation.2 | async-start | bytes 4194304 | tf_op jit(solution)/shard_map/all_to_all | solution.py:323
  105.0 4.0 %copy-start.8 = (s32[2]{0:T(128)S(1)}, s32[2]{0:T(128)}, u32[]{:S(2)}) copy-start(s32[2]{0:T(128)} %param.64) | copy-start | bytes 28
  109.3 4.5 %collective-permute-start.52 = (f32[256,512]{1,0:T(8,128)}, f32[256,512]{1,0:T(8,128)S(1)}, u32[]{:S(2)}, u32[]{:S(2)}) collective-permute-start(f32[256,512]{1,0:T(8,128)} %get-tuple-element.122), channel_id=1, source_target_pairs={{0,1},{1,0},{2,3},{3,2},{4,5},{5,4},{6,7},{7,6},{8,9},{9,8},{10,11... | collective-permute-start | bytes 1572872 | tf_op jit(solution)/shard_map/cond/branch_1_fun/ppermute | solution.py:121
  115.0 17.4 %collective-permute-start.53 = (bf16[256,512]{1,0:T(8,128)(2,1)S(1)}, bf16[256,512]{1,0:T(8,128)(2,1)S(1)}, u32[]{:S(2)}, u32[]{:S(2)}) collective-permute-start(bf16[256,512]{1,0:T(8,128)(2,1)S(1)} %get-tuple-element.158), channel_id=1, source_target_pairs={{0,2},{1,3},{2,0},{3,1},{4,6},{5,7},{6,4},{7,5},{8,10},{9,11},{10,... | collective-permute-start | bytes 786440 | tf_op jit(solution)/shard_map/cond/branch_1_fun/ppermute | solution.py:121
  115.1 17.3 %collective-permute-start.54 = (bf16[256,512]{1,0:T(8,128)(2,1)S(1)}, bf16[256,512]{1,0:T(8,128)(2,1)}, u32[]{:S(2)}, u32[]{:S(2)}) collective-permute-start(bf16[256,512]{1,0:T(8,128)(2,1)S(1)} %get-tuple-element.158), channel_id=1, source_target_pairs={{0,4},{1,5},{2,6},{3,7},{4,0},{5,1},{6,2},{7,3},{8,12},{9,13},{10,... | collective-permute-start | bytes 786440 | tf_op jit(solution)/shard_map/cond/branch_1_fun/ppermute | solution.py:121
  117.0 15.4 %collective-permute-start.55 = (bf16[256,512]{1,0:T(8,128)(2,1)S(1)}, bf16[256,512]{1,0:T(8,128)(2,1)}, u32[]{:S(2)}, u32[]{:S(2)}) collective-permute-start(bf16[256,512]{1,0:T(8,128)(2,1)S(1)} %get-tuple-element.158), channel_id=1, source_target_pairs={{0,6},{1,7},{2,4},{3,5},{4,2},{5,3},{6,0},{7,1},{8,14},{9,15},{10,... | collective-permute-start | bytes 786440 | tf_op jit(solution)/shard_map/cond/branch_1_fun/ppermute | solution.py:121
  120.1 12.4 %collective-permute-start.32 = (bf16[2,256,128]{2,1,0:T(8,128)(2,1)S(1)}, bf16[2,256,128]{2,1,0:T(8,128)(2,1)}, u32[]{:S(2)}, u32[]{:S(2)}) collective-permute-start(bf16[2,256,128]{2,1,0:T(8,128)(2,1)S(1)} %param.33), channel_id=1, source_target_pairs={{0,24},{8,16},{16,8},{24,0},{32,56},{40,48},{48,40},{56,32},{64,88... | collective-permute-start | bytes 393224 | tf_op jit(solution)/shard_map/cond/branch_1_fun/cond/branch_2_fun/ppermute | solution.py:31
  134.4 2.3 %collective-permute-start.56 = (bf16[256,512]{1,0:T(8,128)(2,1)}, bf16[256,512]{1,0:T(8,128)(2,1)}, u32[]{:S(2)}, u32[]{:S(2)}) collective-permute-start(bf16[256,512]{1,0:T(8,128)(2,1)} %add_convert_fusion.1), channel_id=1, source_target_pairs={{0,1},{1,0},{2,3},{3,2},{4,5},{5,4},{6,7},{7,6},{8,9},{9,8},{10,11... | collective-permute-start | bytes 786440 | tf_op jit(solution)/shard_map/cond/branch_1_fun/ppermute | solution.py:121

commit v4 on v3

--- a/solution.py
+++ b/solution.py
@@ -35,7 +35,8 @@
     return jnp.take(table, asked[:, :MOST_PER_INDEX].reshape(-1), axis=0, mode="clip")
 
 
-def project_kernel(pieces, order_ref, query_weight_ref, keyval_weight_ref, *refs):
+def project_kernel(pieces, carried, order_ref, query_weight_ref, keyval_weight_ref, *refs):
+    sums, refs = refs[: 2 * carried], refs[2 * carried :]
     base_ref, keyval_ref, rows_ref, query_acc, keyval_acc, sems = refs[-6:]
     step = pl.program_id(0)
     last = len(pieces) - 1
@@ -54,8 +55,8 @@
     def _():
         for copy in fetches(0):
             copy.start()
-        query_acc[...] = jnp.zeros_like(query_acc)
-        keyval_acc[...] = jnp.zeros_like(keyval_acc)
+        query_acc[...] = sums[0][...] if carried else jnp.zeros_like(query_acc)
+        keyval_acc[...] = sums[1][...] if carried else jnp.zeros_like(keyval_acc)
 
     for i in range(len(pieces)):
 
@@ -74,24 +75,32 @@
 
     @pl.when(step == last)
     def _():
-        width = keyval_ref.shape[2]
         base_ref[...] = query_acc[...]
-        keyval_ref[0] = keyval_acc[:, :width].astype(keyval_ref.dtype)
-        keyval_ref[1] = keyval_acc[:, width:].astype(keyval_ref.dtype)
-
-
-def project(blocks, order, query_weight, keyval_weight):
-    rows, features = blocks[0][0].shape
+        if carried:
+            width = keyval_ref.shape[2]
+            keyval_ref[0] = keyval_acc[:, :width].astype(keyval_ref.dtype)
+            keyval_ref[1] = keyval_acc[:, width:].astype(keyval_ref.dtype)
+        else:
+            keyval_ref[...] = keyval_acc[...]
+
+
+def project(blocks, order, query_weight, keyval_weight, sums=()):
+    features = blocks[0][0].shape[1]
+    rows = sum(piece.shape[0] for piece in blocks[0])
     pieces = tuple(len(block) for block in blocks)
     arrays = [piece for block in blocks for piece in block]
     columns = query_weight.shape[1]
     width = keyval_weight.shape[2]
+    base = jax.ShapeDtypeStruct((rows, columns), jnp.float32)
+    keyval_sums = jax.ShapeDtypeStruct((rows, 2 * width), jnp.float32)
+    keyval = jax.ShapeDtypeStruct((2, rows, width), jnp.bfloat16) if sums else keyval_sums
+
+    def whole(shape):
+        return pl.BlockSpec(shape, lambda i, *_: (0,) * len(shape))
+
     return pl.pallas_call(
-        partial(project_kernel, pieces),
-        out_shape=(
-            jax.ShapeDtypeStruct((rows, columns), jnp.float32),
-            jax.ShapeDtypeStruct((2, rows, width), jnp.bfloat16),
-        ),
+        partial(project_kernel, pieces, bool(sums)),
+        out_shape=(pltpu.HBM(base.shape, base.dtype), pltpu.HBM(keyval.shape, keyval.dtype)),
         grid_spec=pltpu.PrefetchScalarGridSpec(
             num_scalar_prefetch=1,
             grid=(len(blocks),),
@@ -99,21 +108,29 @@
                 pl.BlockSpec((features, columns), lambda i, order_ref: (order_ref[i], 0)),
                 pl.BlockSpec((2, features, width), lambda i, order_ref: (0, order_ref[i], 0)),
             ]
+            + [whole(x.shape) for x in sums]
             + [pl.BlockSpec(memory_space=pl.ANY)] * len(arrays),
-            out_specs=(
-                pl.BlockSpec((rows, columns), lambda i, *_: (0, 0)),
-                pl.BlockSpec((2, rows, width), lambda i, *_: (0, 0, 0)),
-            ),
+            out_specs=(whole(base.shape), whole(keyval.shape)),
             scratch_shapes=[
                 pltpu.VMEM((2, rows, features), jnp.bfloat16),
-                pltpu.VMEM((rows, columns), jnp.float32),
-                pltpu.VMEM((rows, 2 * width), jnp.float32),
+                pltpu.VMEM(base.shape, jnp.float32),
+                pltpu.VMEM(keyval_sums.shape, jnp.float32),
                 pltpu.SemaphoreType.DMA((2, max(pieces))),
             ],
         ),
         compiler_params=pltpu.CompilerParams(vmem_limit_bytes=32 << 20),
+        cost_estimate=pl.CostEstimate(
+            flops=2 * len(blocks) * rows * features * (columns + 2 * width),
+            bytes_accessed=2 * len(blocks) * features * (rows + columns + 2 * width),
+            transcendentals=0,
+        ),
         name="project",
-    )(order, *[pltpu.with_memory_space_constraint(x, pltpu.HBM) for x in (query_weight, keyval_weight, *arrays)])
+    )(
+        order,
+        *[pltpu.with_memory_space_constraint(x, pltpu.HBM) for x in (query_weight, keyval_weight)],
+        *[pltpu.with_memory_space_constraint(x, pltpu.HBM) for x in sums],
+        *arrays,
+    )
 
 
 def across_tensor(block, flip):
@@ -130,14 +147,11 @@
     return along_column(tokens, 1), along_column(tokens, -1)
 
 
-def all_features(tokens, before, after):
+def paired(held, offsets):
     size = lax.axis_size("tensor")
     own = lax.axis_index("tensor")
-    half = tokens.shape[0] // 2
-    opposite = (along_column(before[:half], 1), along_column(after[half:], -1))
-    held = [(tokens,), (before,), (after,), opposite]
     blocks, order = [], []
-    for offset, pieces in zip((0, size - 2, 2, 4), held):
+    for offset, pieces in zip(offsets, held):
         index = (own + offset) % size
         blocks += [pieces, tuple(across_tensor(piece, 1) for piece in pieces)]
         order += [index, jnp.bitwise_xor(index, 1)]
@@ -213,18 +227,19 @@
 
 
 def attend_kernel(
-    slots_ref, lens_ref, mates_ref, core_ref, same_ref, other_ref, base_ref, own_ref, mate_ref, *refs
+    slots_ref, lens_ref, mates_ref, core_ref, same_ref, other_ref, base_ref, own_ref, *refs
 ):
-    ups, out_ref = refs[:-1], refs[-1]
+    mate_refs, ups, out_ref = refs[:2], refs[2:-1], refs[-1]
     j = pl.program_id(0)
+    mate = jnp.where(j == 0, mate_refs[0][...], mate_refs[1][...])
     acts = jnp.where(j == core_ref[0], same_ref[...], other_ref[...])
     up_rows = jnp.concatenate([u[0] for u in ups], axis=0)
     delta = jnp.dot(acts, up_rows, preferred_element_type=jnp.float32)
     queries = (base_ref[...] + delta).astype(jnp.bfloat16)
     rows, columns = queries.shape
     scale = math.log2(math.e) / math.sqrt(HEAD_SIZE)
-    keys = jnp.concatenate([own_ref[0], mate_ref[0]], axis=0)
-    values = jnp.concatenate([own_ref[1], mate_ref[1]], axis=0)
+    keys = jnp.concatenate([own_ref[0], mate[0]], axis=0)
+    values = jnp.concatenate([own_ref[1], mate[1]], axis=0)
     position = lax.broadcasted_iota(jnp.int32, (rows, 2 * rows), 0)
     key_at = lax.broadcasted_iota(jnp.int32, (rows, 2 * rows), 1)
     own_ok = (key_at <= position) & (key_at < lens_ref[j])
@@ -254,7 +269,7 @@
         return pl.BlockSpec((1, ranks, columns), lambda j, slots_ref, *_: (slots_ref[j * rubrics + s], 0, 0))
 
     acts_spec = pl.BlockSpec(acts[0].shape, lambda j, *_: (0, 0))
-    kv_spec = pl.BlockSpec((2, resp_len, HEAD_SIZE), lambda j, *_: (0, j, 0))
+    mate_spec = pl.BlockSpec((2, resp_len, HEAD_SIZE), lambda j, *_: (0, 0, 0))
     return pl.pallas_call(
         attend_kernel,
         out_shape=jax.ShapeDtypeStruct((rows, columns), jnp.bfloat16),
@@ -265,15 +280,16 @@
                 acts_spec,
                 acts_spec,
                 pl.BlockSpec((resp_len, columns), lambda j, *_: (j, 0)),
-                kv_spec,
-                kv_spec,
+                pl.BlockSpec((2, resp_len, HEAD_SIZE), lambda j, *_: (0, j, 0)),
+                mate_spec,
+                mate_spec,
             ]
             + [up_spec(s) for s in range(rubrics)],
             out_specs=pl.BlockSpec((resp_len, columns), lambda j, *_: (j, 0)),
         ),
         compiler_params=pltpu.CompilerParams(vmem_limit_bytes=40 << 20),
         name="attend",
-    )(slots, own_lens, mate_lens, core, *acts, pltpu.with_memory_space_constraint(base, pltpu.HBM), keyval, mate_keyvals, *([got_up] * rubrics))
+    )(slots, own_lens, mate_lens, core, *acts, pltpu.with_memory_space_constraint(base, pltpu.HBM), keyval, *mate_keyvals, *([got_up] * rubrics))
 
 
 def on_device(
@@ -309,12 +325,17 @@
     asked = lax.all_to_all(wanted, "dp", split_axis=0, concat_axis=0, tiled=True)
     shipped_down = take_asked(adapter_down_weight, asked)
     shipped_down = shipped_down.reshape(owner_groups, MOST_PER_INDEX, rank_extent, feature_shard)
-    shipped_down, before, after = lax.optimization_barrier((shipped_down, before, after))
     got_down = lax.all_to_all(shipped_down, "dp", split_axis=0, concat_axis=0, tiled=True)
     shipped_up = take_asked(adapter_up_weight, asked)
     shipped_up = shipped_up.reshape(owner_groups, MOST_PER_INDEX, rank_extent, head_columns)
-    blocks, order = all_features(tokens, before, after)
-    base, keyval = project(blocks, order, query_weight, key_value_weight)
+    before, after, shipped_up = lax.optimization_barrier((before, after, shipped_up))
+    half = tok_rows // 2
+    opposite = (along_column(before[:half], 1), along_column(after[half:], -1))
+    near, order = paired([(tokens,), (before,), (after,)], (0, -2, 2))
+    sums = project(near, order, query_weight, key_value_weight)
+    opposite, sums = lax.optimization_barrier((opposite, sums))
+    far, order = paired([opposite], (4,))
+    base, keyval = project(far, order, query_weight, key_value_weight, sums)
     own_keyval = keyval.reshape(2, resp_dev, resp_len, kv_cols)
     mate_first = from_partner(own_keyval[:, 0], partner_xor_mask[0])
     got_down, shipped_up, mate_first, own_keyval = lax.optimization_barrier(
@@ -342,13 +363,12 @@
     same, other, mate_second = lax.cond(
         lengths[0] >= 1, split_sum, plain_sum, (keep, send, own_keyval[:, 1])
     )
-    mate_keyval = jnp.concatenate([mate_first, mate_second], axis=1)
     own_lens = lax.dynamic_slice_in_dim(lengths, own_index * resp_dev, resp_dev)
     mate_index = partner_dev * resp_dev + jnp.arange(resp_dev, dtype=jnp.int32)
     mate_lens = jnp.take(lengths, mate_index, axis=0, mode="clip")
     mate_lens = jnp.where(partner_attend_mask == 1, mate_lens, 0)
     return attend(
-        (same, other), base, keyval, mate_keyval, got_up.reshape(-1, rank_extent, head_columns),
+        (same, other), base, keyval, (mate_first, mate_second), got_up.reshape(-1, rank_extent, head_columns),
         buffer_slot, own_lens, mate_lens, core.reshape(1), rubrics,
     )
 

time: 146 us -> 139 us (0.952); the launches traced: 145 us -> 140 us
  waiting for transfers between devices: 49.3 us -> 38.5 us
  Pallas kernels: 24.9 us -> 29.3 us
  starting transfers between devices: 37.9 us -> 39.7 us
  other arithmetic: 5.15 us -> 3.58 us
    ppermute x2, waiting for transfers between devices: 31.6 us -> 15.1 us  [from_partner(): return lax.switch(mask - 1, moves, block)]
    pallas_call x1 -> x2, Pallas kernels: 13.9 us -> 18.2 us  [project(): pl.pallas_call(partial(project_kernel, pieces, bool(sums)), out_shape=(pl...]
    ppermute x10, starting transfers between devices: 10.8 us -> 14.6 us  [across_tensor(): lax.ppermute(block, 'tensor', [(source, source ^ flip) for source in rang...]
    ppermute x4, waiting for transfers between devices: 14.2 us -> 17.6 us  [along_column(): lax.ppermute(block, 'tensor', [(source, (source + 2 * step) % size) for s...]
    ppermute x10, waiting for transfers between devices: 3.46 us -> 5.77 us  [across_tensor(): lax.ppermute(block, 'tensor', [(source, source ^ flip) for source in rang...]
    all_to_all x1, starting transfers between devices: 6.94 us -> 4.68 us  [on_device(): lax.all_to_all(shipped_down, 'dp', split_axis=0, concat_axis=0, tiled=True)]
    unnamed x18 -> x12, local copies, waits for them, and re-layouts: 2.04 us -> 0.03 us
    all_to_all x1, starting transfers between devices: 4.44 us -> 6.25 us  [on_device(): lax.all_to_all(shipped_up, 'dp', split_axis=0, concat_axis=0, tiled=True)]
  transfers between devices with their start and end apart: 18 -> 18, of which waited for: 7 -> 8; matrix products, arithmetic and copies ran while one was open for 11% -> 8% of each run, Pallas kernels for 12% -> 16%
where the time goes in v4:
time: 139 us; the launch traced here: 140 us
  starting transfers between devices  39.7 us (29%)
  waiting for transfers between devices  38.5 us (28%)
  Pallas kernels  29.3 us (21%)
  local copies, waits for them, and re-layouts  14.1 us (10%)
  blocking collectives  13.8 us (10%)
  other arithmetic  3.58 us (3%)
    pallas_call x2, Pallas kernels, project(): pl.pallas_call(partial(project_kernel, pieces, bool(sums)), out_shape=(pl...  18.2 us
    ppermute x4, waiting for transfers between devices, along_column(): lax.ppermute(block, 'tensor', [(source, (source + 2 * step) % size) for s...  17.6 us
    ppermute x2, waiting for transfers between devices, from_partner(): return lax.switch(mask - 1, moves, block)  15.1 us
    ppermute x10, starting transfers between devices, across_tensor(): lax.ppermute(block, 'tensor', [(source, source ^ flip) for source in rang...  14.6 us
    all_to_all x1, blocking collectives, on_device(): lax.all_to_all(wanted, 'dp', split_axis=0, concat_axis=0, tiled=True)  13.8 us
    ppermute x2, starting transfers between devices, from_partner(): return lax.switch(mask - 1, moves, block)  7.5 us
    pallas_call x1, Pallas kernels, attend(): pl.pallas_call(attend_kernel, out_shape=jax.ShapeDtypeStruct((rows, colum...  7.08 us
    gather x2, local copies, waits for them, and re-layouts, take_asked(): jnp.take(table, asked[:, :MOST_PER_INDEX].reshape(-1), axis=0, mode='clip')  7.02 us
  transfers between devices with their start and end apart: 18, of which 8 were waited for; matrix products, arithmetic and copies ran while one was open for 8% of the time, Pallas kernels for 16%

profile of v4, /device:TPU:1, one launch (start us, length us, event | category | flops | bytes accessed | tf_op | source)
XLA Modules:
  0.0 140.0 jit_solution(4913703604923468574)
XLA Ops:
  0.0 0.0 copy-start
  0.0 0.9 reshape.188
  0.9 0.2 and_reduce_fusion
  1.1 0.1 add_select_fusion
  1.2 0.1 select_reduce_fusion
  1.3 13.8 %all_to_all.22 = s32[16,1,128]{2,1,0:T(1,128)S(1)} all-to-all(s32[16,1,128]{2,1,0:T(1,128)S(1)} %bitcast.44), channel_id=1, replica_groups=mesh['dp'=16,'tensor'=8] {'dp'}, dimensions={0} | all-to-all | bytes 16384 | tf_op jit(solution)/shard_map/all_to_all | solution.py:325
  15.1 0.1 reshape.206
  15.2 5.0 %gather_fusion.1 = bf16[32,64,1024]{2,1,0:T(8,128)(2,1)} fusion(bf16[32,64,1024]{2,1,0:T(8,128)(2,1)} %param.59, s32[1024]{0:T(1024)S(1)} %pad_clamp_fusion), kind=kCustom, calls=%fused_computation.1 | custom fusion | bytes 8388736 | tf_op jit(solution)/shard_map/jit(_take)/gather | solution.py:35
  20.2 4.7 %all-to-all-start.1 = ((bf16[16,2,64,1024]{3,2,1,0:T(8,128)(2,1)}), bf16[16,2,64,1024]{3,2,1,0:T(8,128)(2,1)}, u32[]{:S(2)}, u32[]{:S(2)}) async-start(bf16[16,2,64,1024]{3,2,1,0:T(8,128)(2,1)} %bitcast.40), calls=%async_computation.1 | async-start | bytes 8388608 | tf_op jit(solution)/shard_map/all_to_all | solution.py:328
  24.9 1.7 %collective-permute-start.57 = (bf16[512,1024]{1,0:T(8,128)(2,1)S(1)}, bf16[512,1024]{1,0:T(8,128)(2,1)}, u32[]{:S(2)}, u32[]{:S(2)}) collective-permute-start(bf16[512,1024]{1,0:T(8,128)(2,1)S(1)} %copy-done.1), channel_id=1, source_target_pairs={{0,2},{1,3},{2,4},{3,5},{4,6},{5,7},{6,0},{7,1},{8,10},{9,11},{10,... | collective-permute-start | bytes 3145736 | tf_op jit(solution)/shard_map/ppermute | solution.py:143
  26.6 2.2 %collective-permute-start.58 = (bf16[512,1024]{1,0:T(8,128)(2,1)S(1)}, bf16[512,1024]{1,0:T(8,128)(2,1)}, u32[]{:S(2)}, u32[]{:S(2)}) collective-permute-start(bf16[512,1024]{1,0:T(8,128)(2,1)S(1)} %copy-done.1), channel_id=1, source_target_pairs={{0,6},{1,7},{2,0},{3,1},{4,2},{5,3},{6,4},{7,5},{8,14},{9,15},{10,... | collective-permute-start | bytes 3145736 | tf_op jit(solution)/shard_map/ppermute | solution.py:143
  28.8 2.4 %collective-permute-start.61 = (bf16[512,1024]{1,0:T(8,128)(2,1)S(1)}, bf16[512,1024]{1,0:T(8,128)(2,1)}, u32[]{:S(2)}, u32[]{:S(2)}) collective-permute-start(bf16[512,1024]{1,0:T(8,128)(2,1)S(1)} %copy-done.1), channel_id=1, source_target_pairs={{0,1},{1,0},{2,3},{3,2},{4,5},{5,4},{6,7},{7,6},{8,9},{9,8},{10,11... | collective-permute-start | bytes 3145736 | tf_op jit(solution)/shard_map/ppermute | solution.py:138
  31.2 2.0 %gather_fusion.2 = bf16[32,64,512]{2,1,0:T(8,128)(2,1)} fusion(bf16[32,64,512]{2,1,0:T(8,128)(2,1)S(1)} %copy-done, s32[1024]{0:T(1024)S(1)} %pad_clamp_fusion), kind=kCustom, calls=%fused_computation.2 | custom fusion | bytes 4194432 | tf_op jit(solution)/shard_map/jit(_take)/gather | solution.py:35
  33.2 17.0 %collective-permute-done.57.refs_2_ = bf16[512,1024]{1,0:T(8,128)(2,1)} collective-permute-done((bf16[512,1024]{1,0:T(8,128)(2,1)S(1)}, bf16[512,1024]{1,0:T(8,128)(2,1)}, u32[]{:S(2)}, u32[]{:S(2)}) %collective-permute-start.57) | collective-permute-done | bytes 1048608 | tf_op jit(solution)/shard_map/ppermute | solution.py:143
  50.2 0.0 collective-permute-done.58.refs_4_
  50.2 2.7 %collective-permute-start.62 = (bf16[512,1024]{1,0:T(8,128)(2,1)}, bf16[512,1024]{1,0:T(8,128)(2,1)}, u32[]{:S(2)}, u32[]{:S(2)}) collective-permute-start(bf16[512,1024]{1,0:T(8,128)(2,1)} %collective-permute-done.57.refs_2_), channel_id=1, source_target_pairs={{0,1},{1,0},{2,3},{3,2},{4,5},{5,4},{6,7},{7,6},{8,9},{9,8},{10,11... | collective-permute-start | bytes 3145736 | tf_op jit(solution)/shard_map/ppermute | solution.py:138
  53.0 0.0 collective-permute-start.63
  53.0 1.9 %slice.37 = bf16[256,1024]{1,0:T(8,128)(2,1)} slice(bf16[512,1024]{1,0:T(8,128)(2,1)} %collective-permute-done.57.refs_2_), slice={[0:256], [0:1024]} | slice | bytes 1048576 | tf_op jit(solution)/shard_map/slice | solution.py:333
  54.9 1.9 %slice.38 = bf16[256,1024]{1,0:T(8,128)(2,1)} slice(bf16[512,1024]{1,0:T(8,128)(2,1)} %collective-permute-done.58.refs_4_), slice={[256:512], [0:1024]} | slice | bytes 1048576 | tf_op jit(solution)/shard_map/slice | solution.py:333
  56.7 1.0 collective-permute-start.59
  57.7 1.8 %collective-permute-start.60 = (bf16[256,1024]{1,0:T(8,128)(2,1)}, bf16[256,1024]{1,0:T(8,128)(2,1)}, u32[]{:S(2)}, u32[]{:S(2)}) collective-permute-start(bf16[256,1024]{1,0:T(8,128)(2,1)} %slice.38), channel_id=1, source_target_pairs={{0,6},{1,7},{2,0},{3,1},{4,2},{5,3},{6,4},{7,5},{8,14},{9,15},{10,... | collective-permute-start | bytes 1572872 | tf_op jit(solution)/shard_map/ppermute | solution.py:143
  59.5 0.1 stack.48.order_ref
  59.6 0.0 collective-permute-done.61.refs_1_
  59.6 0.0 collective-permute-done.62.refs_3_
  59.6 0.0 collective-permute-done.63.refs_5_
  59.6 11.2 %project.2 = (f32[512,512]{1,0:T(8,128)}, f32[512,256]{1,0:T(8,128)}) custom-call(s32[6]{0:T(128)S(1)} %stack.48.order_ref, bf16[8192,512]{1,0:T(8,128)(2,1)} %query_weight_ref.3, bf16[2,8192,128]{2,1,0:T(8,128)(2,1)} %keyval_weight_ref.3, bf16[512,1024]{1,0:T(8,128)(2,1)S(1)} %copy-done.1, bf16[512,1024]{1,0:T(8,128)(2,1)} %collective-permute-done.61.refs_1_, ...), custom_call_target="tpu_custom_call" | custom-call | flops 4831838208 | bytes 15728640 | tf_op jit(solution)/shard_map/project/pallas_call | solution.py:101
  70.8 0.6 collective-permute-done.59.refs_2_
  71.4 0.0 collective-permute-done.60.refs_3_
  71.4 1.3 collective-permute-start.64
  72.7 0.0 collective-permute-start.65
  72.7 0.1 pad_add_fusion.order_ref
  72.8 1.8 %collective-permute-done.64.refs_4_ = bf16[256,1024]{1,0:T(8,128)(2,1)} collective-permute-done((bf16[256,1024]{1,0:T(8,128)(2,1)}, bf16[256,1024]{1,0:T(8,128)(2,1)}, u32[]{:S(2)}, u32[]{:S(2)}) %collective-permute-start.64) | collective-permute-done | bytes 524320 | tf_op jit(solution)/shard_map/ppermute | solution.py:138
  74.6 0.7 collective-permute-done.65.refs_5_
  75.3 7.0 %project.3 = (f32[512,512]{1,0:T(8,128)}, bf16[2,512,128]{2,1,0:T(8,128)(2,1)}) custom-call(s32[2]{0:T(128)S(1)} %pad_add_fusion.order_ref, bf16[8192,512]{1,0:T(8,128)(2,1)} %query_weight_ref.3, bf16[2,8192,128]{2,1,0:T(8,128)(2,1)} %keyval_weight_ref.3, f32[512,512]{1,0:T(8,128)} %get-tuple-element.155.refs_0_, f32[512,256]{1,0:T(8,128)} %get-tuple-element.156.refs_1_, ...), custom_call_target="tpu_custom_call" | custom-call | flops 1610612736 | bytes 5242880 | tf_op jit(solution)/shard_map/project/pallas_call | solution.py:101
  82.3 0.0 copy-start.3
  82.3 0.0 copy-start.4
  82.3 0.9 slice_bitcast_fusion.3
  83.3 8.6 %conditional.4 = (bf16[2,256,128]{2,1,0:T(8,128)(2,1)}) conditional(s32[]{:T(128)} %bitcast.13, bf16[2,256,128]{2,1,0:T(8,128)(2,1)S(1)} %slice_bitcast_fusion.3, bf16[2,256,128]{2,1,0:T(8,128)(2,1)S(1)} %slice_bitcast_fusion.3, bf16[2,256,128]{2,1,0:T(8,128)(2,1)S(1)} %slice_bitcast_fusion.3, ...), branch_computations={%region_2.3_spmd, %region_3.4_spmd, %region_4.5_spmd, %region_5.6_... | conditional | bytes 524336 | solution.py:31
  83.3 4.9 %collective-permute-start.10 = (bf16[2,256,128]{2,1,0:T(8,128)(2,1)S(1)}, bf16[2,256,128]{2,1,0:T(8,128)(2,1)}, u32[]{:S(2)}, u32[]{:S(2)}) collective-permute-start(bf16[2,256,128]{2,1,0:T(8,128)(2,1)S(1)} %param.10), channel_id=1, source_target_pairs={{0,88},{8,80},{16,72},{24,64},{32,120},{40,112},{48,104},{56,96},{... | collective-permute-start | bytes 393224 | tf_op jit(solution)/shard_map/cond/branch_10_fun/ppermute | solution.py:31
  88.2 3.6 %collective-permute-done.10 = bf16[2,256,128]{2,1,0:T(8,128)(2,1)} collective-permute-done((bf16[2,256,128]{2,1,0:T(8,128)(2,1)S(1)}, bf16[2,256,128]{2,1,0:T(8,128)(2,1)}, u32[]{:S(2)}, u32[]{:S(2)}) %collective-permute-start.10) | collective-permute-done | bytes 131104 | tf_op jit(solution)/shard_map/cond/branch_10_fun/ppermute | solution.py:31
  91.8 0.0 all-to-all-done.1
  91.8 6.2 %all-to-all-start.2 = ((bf16[16,2,64,512]{3,2,1,0:T(8,128)(2,1)}), bf16[16,2,64,512]{3,2,1,0:T(8,128)(2,1)}, u32[]{:S(2)}, u32[]{:S(2)}) async-start(bf16[16,2,64,512]{3,2,1,0:T(8,128)(2,1)} %bitcast.41), calls=%async_computation.2 | async-start | bytes 4194304 | tf_op jit(solution)/shard_map/all_to_all | solution.py:344
  98.1 0.1 dynamic_slice.3.lens_ref
  98.2 0.6 gather_fusion
  98.9 4.0 %partial_rank_acts.1 = (f32[256,512]{1,0:T(8,128)}, f32[256,512]{1,0:T(8,128)}) custom-call(s32[16]{0:T(128)S(1)} %convert_add_fusion.slots_ref, s32[1]{0:T(128)} %bitcast.6.core_ref, bf16[512,1024]{1,0:T(8,128)(2,1)S(1)} %copy-done.1, bf16[32,64,1024]{2,1,0:T(8,128)(2,1)} %bitcast.24.refs_0_.refs_1_.refs_2_.refs_3_.refs_4_.refs_5_.refs_6_.refs_7_, ...), custom_call_target="tpu_custom_call" | custom-call | flops 536870912 | bytes 4194304 | tf_op jit(solution)/shard_map/partial_rank_acts/pallas_call | solution.py:213
  102.9 30.0 %conditional.5 = (bf16[256,512]{1,0:T(8,128)(2,1)}, bf16[256,512]{1,0:T(8,128)(2,1)}, bf16[2,256,128]{2,1,0:T(8,128)(2,1)}) conditional(s32[]{:T(128)} %bitcast.7, (s32[]{:T(128)}, f32[256,512]{1,0:T(8,128)}, f32[256,512]{1,0:T(8,128)}, s32[2]{0:T(128)S(1)}, bf16[2,256,128]{2,1,0:T(8,128)(2,1)S(1)}) %tuple.208, (f32[256,512]{1,0:T(8,128)}, ...), branch_computations={%region_17.33_spmd, %region_33.49_spmd} | conditional | flops 3145731 | bytes 45089164 | solution.py:363
  103.2 1.6 %collective-permute-start.52 = (f32[256,512]{1,0:T(8,128)}, f32[256,512]{1,0:T(8,128)S(1)}, u32[]{:S(2)}, u32[]{:S(2)}) collective-permute-start(f32[256,512]{1,0:T(8,128)} %get-tuple-element.122), channel_id=1, source_target_pairs={{0,1},{1,0},{2,3},{3,2},{4,5},{5,4},{6,7},{7,6},{8,9},{9,8},{10,11... | collective-permute-start | bytes 1572872 | tf_op jit(solution)/shard_map/cond/branch_1_fun/ppermute | solution.py:138
  104.7 1.7 %collective-permute-done.52 = f32[256,512]{1,0:T(8,128)S(1)} collective-permute-done((f32[256,512]{1,0:T(8,128)}, f32[256,512]{1,0:T(8,128)S(1)}, u32[]{:S(2)}, u32[]{:S(2)}) %collective-permute-start.52) | collective-permute-done | bytes 524320 | tf_op jit(solution)/shard_map/cond/branch_1_fun/ppermute | solution.py:138
  106.5 1.2 fusion
  107.6 1.1 collective-permute-start.53
  108.8 2.8 %collective-permute-start.54 = (bf16[256,512]{1,0:T(8,128)(2,1)S(1)}, bf16[256,512]{1,0:T(8,128)(2,1)}, u32[]{:S(2)}, u32[]{:S(2)}) collective-permute-start(bf16[256,512]{1,0:T(8,128)(2,1)S(1)} %get-tuple-element.170), channel_id=1, source_target_pairs={{0,4},{1,5},{2,6},{3,7},{4,0},{5,1},{6,2},{7,3},{8,12},{9,13},{10,... | collective-permute-start | bytes 786440 | tf_op jit(solution)/shard_map/cond/branch_1_fun/ppermute | solution.py:138
  111.6 0.0 collective-permute-start.55
  111.6 0.6 slice.26
  112.7 14.1 %conditional.1 = (bf16[2,256,128]{2,1,0:T(8,128)(2,1)}) conditional(s32[]{:T(128)} %bitcast.5, bf16[2,256,128]{2,1,0:T(8,128)(2,1)S(1)} %get-tuple-element.125, bf16[2,256,128]{2,1,0:T(8,128)(2,1)S(1)} %get-tuple-element.125, bf16[2,256,128]{2,1,0:T(8,128)(2,1)S(1)} %get-tuple-element.125, ...), branch_computations={%region_34.34_spmd, %region_35.35_spmd, %region_36.36_spmd, %regio... | conditional | bytes 524336 | solution.py:31
  112.8 2.6 %collective-permute-start.34 = (bf16[2,256,128]{2,1,0:T(8,128)(2,1)S(1)}, bf16[2,256,128]{2,1,0:T(8,128)(2,1)}, u32[]{:S(2)}, u32[]{:S(2)}) collective-permute-start(bf16[2,256,128]{2,1,0:T(8,128)(2,1)S(1)} %param.35), channel_id=1, source_target_pairs={{0,40},{8,32},{16,56},{24,48},{32,8},{40,0},{48,24},{56,16},{64,10... | collective-permute-start | bytes 393224 | tf_op jit(solution)/shard_map/cond/branch_1_fun/cond/branch_4_fun/ppermute | solution.py:31
  115.3 11.5 %collective-permute-done.34 = bf16[2,256,128]{2,1,0:T(8,128)(2,1)} collective-permute-done((bf16[2,256,128]{2,1,0:T(8,128)(2,1)S(1)}, bf16[2,256,128]{2,1,0:T(8,128)(2,1)}, u32[]{:S(2)}, u32[]{:S(2)}) %collective-permute-start.34) | collective-permute-done | bytes 131104 | tf_op jit(solution)/shard_map/cond/branch_1_fun/cond/branch_4_fun/ppermute | solution.py:31
  126.9 0.0 collective-permute-done.53
  126.9 0.0 collective-permute-done.54
  126.9 0.0 collective-permute-done.55
  126.9 1.9 %add_convert_fusion.1 = bf16[256,512]{1,0:T(8,128)(2,1)} fusion(bf16[256,512]{1,0:T(8,128)(2,1)} %collective-permute-done.55, bf16[256,512]{1,0:T(8,128)(2,1)} %collective-permute-done.54, f32[256,512]{1,0:T(8,128)S(1)} %get-tuple-element.171, bf16[256,512]{1,0:T(8,128)(2,1)S(1)} %collective-permute-done.53), kind=kLoop, calls=%fused_computation.9 | loop fusion | flops 917504 | bytes 1572864 | tf_op jit(solution)/shard_map/cond/branch_1_fun/convert_element_type | solution.py:171
  128.8 2.7 %collective-permute-start.56 = (bf16[256,512]{1,0:T(8,128)(2,1)}, bf16[256,512]{1,0:T(8,128)(2,1)}, u32[]{:S(2)}, u32[]{:S(2)}) collective-permute-start(bf16[256,512]{1,0:T(8,128)(2,1)} %add_convert_fusion.1), channel_id=1, source_target_pairs={{0,1},{1,0},{2,3},{3,2},{4,5},{5,4},{6,7},{7,6},{8,9},{9,8},{10,11... | collective-permute-start | bytes 786440 | tf_op jit(solution)/shard_map/cond/branch_1_fun/ppermute | solution.py:138
  131.4 1.5 %collective-permute-done.56 = bf16[256,512]{1,0:T(8,128)(2,1)} collective-permute-done((bf16[256,512]{1,0:T(8,128)(2,1)}, bf16[256,512]{1,0:T(8,128)(2,1)}, u32[]{:S(2)}, u32[]{:S(2)}) %collective-permute-start.56) | collective-permute-done | bytes 262176 | tf_op jit(solution)/shard_map/cond/branch_1_fun/ppermute | solution.py:138
  133.0 0.0 all-to-all-done.2
  133.0 7.1 %attend.1 = bf16[512,512]{1,0:T(8,128)(2,1)} custom-call(s32[16]{0:T(128)S(1)} %convert_add_fusion.slots_ref, s32[2]{0:T(128)S(1)} %dynamic_slice.3.lens_ref, s32[2]{0:T(128)S(1)} %compare_select_fusion.mates_ref, s32[1]{0:T(128)} %bitcast.6.core_ref, bf16[256,512]{1,0:T(8,128)(2,1)} %get-tuple-element.164.same_ref, ...), custom_call_target="tpu_custom_call" | custom-call | tf_op jit(solution)/shard_map/attend/pallas_call | solution.py:273
  (18 shorter events, 0.1 us)
Async XLA Ops:
  0.0 31.2 %copy-start = (bf16[32,64,512]{2,1,0:T(8,128)(2,1)S(1)}, bf16[32,64,512]{2,1,0:T(8,128)(2,1)}, u32[]{:S(2)}) copy-start(bf16[32,64,512]{2,1,0:T(8,128)(2,1)} %param.60) | copy-start | bytes 6291460
  20.2 4.7 %copy-start.1 = (bf16[512,1024]{1,0:T(8,128)(2,1)S(1)}, bf16[512,1024]{1,0:T(8,128)(2,1)}, u32[]{:S(2)}) copy-start(bf16[512,1024]{1,0:T(8,128)(2,1)} %tokens_ref.1) | copy-start | bytes 3145732
  20.2 71.6 %all-to-all-start.1 = ((bf16[16,2,64,1024]{3,2,1,0:T(8,128)(2,1)}), bf16[16,2,64,1024]{3,2,1,0:T(8,128)(2,1)}, u32[]{:S(2)}, u32[]{:S(2)}) async-start(bf16[16,2,64,1024]{3,2,1,0:T(8,128)(2,1)} %bitcast.40), calls=%async_computation.1 | async-start | bytes 8388608 | tf_op jit(solution)/shard_map/all_to_all | solution.py:328
  24.9 25.3 %collective-permute-start.57 = (bf16[512,1024]{1,0:T(8,128)(2,1)S(1)}, bf16[512,1024]{1,0:T(8,128)(2,1)}, u32[]{:S(2)}, u32[]{:S(2)}) collective-permute-start(bf16[512,1024]{1,0:T(8,128)(2,1)S(1)} %copy-done.1), channel_id=1, source_target_pairs={{0,2},{1,3},{2,4},{3,5},{4,6},{5,7},{6,0},{7,1},{8,10},{9,11},{10,... | collective-permute-start | bytes 3145736 | tf_op jit(solution)/shard_map/ppermute | solution.py:143
  26.6 23.6 %collective-permute-start.58 = (bf16[512,1024]{1,0:T(8,128)(2,1)S(1)}, bf16[512,1024]{1,0:T(8,128)(2,1)}, u32[]{:S(2)}, u32[]{:S(2)}) collective-permute-start(bf16[512,1024]{1,0:T(8,128)(2,1)S(1)} %copy-done.1), channel_id=1, source_target_pairs={{0,6},{1,7},{2,0},{3,1},{4,2},{5,3},{6,4},{7,5},{8,14},{9,15},{10,... | collective-permute-start | bytes 3145736 | tf_op jit(solution)/shard_map/ppermute | solution.py:143
  28.8 30.7 %collective-permute-start.61 = (bf16[512,1024]{1,0:T(8,128)(2,1)S(1)}, bf16[512,1024]{1,0:T(8,128)(2,1)}, u32[]{:S(2)}, u32[]{:S(2)}) collective-permute-start(bf16[512,1024]{1,0:T(8,128)(2,1)S(1)} %copy-done.1), channel_id=1, source_target_pairs={{0,1},{1,0},{2,3},{3,2},{4,5},{5,4},{6,7},{7,6},{8,9},{9,8},{10,11... | collective-permute-start | bytes 3145736 | tf_op jit(solution)/shard_map/ppermute | solution.py:138
  50.2 9.4 %collective-permute-start.62 = (bf16[512,1024]{1,0:T(8,128)(2,1)}, bf16[512,1024]{1,0:T(8,128)(2,1)}, u32[]{:S(2)}, u32[]{:S(2)}) collective-permute-start(bf16[512,1024]{1,0:T(8,128)(2,1)} %collective-permute-done.57.refs_2_), channel_id=1, source_target_pairs={{0,1},{1,0},{2,3},{3,2},{4,5},{5,4},{6,7},{7,6},{8,9},{9,8},{10,11... | collective-permute-start | bytes 3145736 | tf_op jit(solution)/shard_map/ppermute | solution.py:138
  53.0 6.6 %collective-permute-start.63 = (bf16[512,1024]{1,0:T(8,128)(2,1)}, bf16[512,1024]{1,0:T(8,128)(2,1)}, u32[]{:S(2)}, u32[]{:S(2)}) collective-permute-start(bf16[512,1024]{1,0:T(8,128)(2,1)} %collective-permute-done.58.refs_4_), channel_id=1, source_target_pairs={{0,1},{1,0},{2,3},{3,2},{4,5},{5,4},{6,7},{7,6},{8,9},{9,8},{10,11... | collective-permute-start | bytes 3145736 | tf_op jit(solution)/shard_map/ppermute | solution.py:138
  56.7 14.7 %collective-permute-start.59 = (bf16[256,1024]{1,0:T(8,128)(2,1)}, bf16[256,1024]{1,0:T(8,128)(2,1)}, u32[]{:S(2)}, u32[]{:S(2)}) collective-permute-start(bf16[256,1024]{1,0:T(8,128)(2,1)} %slice.37), channel_id=1, source_target_pairs={{0,2},{1,3},{2,4},{3,5},{4,6},{5,7},{6,0},{7,1},{8,10},{9,11},{10,... | collective-permute-start | bytes 1572872 | tf_op jit(solution)/shard_map/ppermute | solution.py:143
  57.7 13.7 %collective-permute-start.60 = (bf16[256,1024]{1,0:T(8,128)(2,1)}, bf16[256,1024]{1,0:T(8,128)(2,1)}, u32[]{:S(2)}, u32[]{:S(2)}) collective-permute-start(bf16[256,1024]{1,0:T(8,128)(2,1)} %slice.38), channel_id=1, source_target_pairs={{0,6},{1,7},{2,0},{3,1},{4,2},{5,3},{6,4},{7,5},{8,14},{9,15},{10,... | collective-permute-start | bytes 1572872 | tf_op jit(solution)/shard_map/ppermute | solution.py:143
  59.6 13.1 %copy-start.5 = (s32[2]{0:T(128)S(1)}, s32[2]{0:T(128)}, u32[]{:S(2)}) copy-start(s32[2]{0:T(128)} %param.64) | copy-start | bytes 28
  71.4 3.2 %collective-permute-start.64 = (bf16[256,1024]{1,0:T(8,128)(2,1)}, bf16[256,1024]{1,0:T(8,128)(2,1)}, u32[]{:S(2)}, u32[]{:S(2)}) collective-permute-start(bf16[256,1024]{1,0:T(8,128)(2,1)} %collective-permute-done.59.refs_2_), channel_id=1, source_target_pairs={{0,1},{1,0},{2,3},{3,2},{4,5},{5,4},{6,7},{7,6},{8,9},{9,8},{10,11... | collective-permute-start | bytes 1572872 | tf_op jit(solution)/shard_map/ppermute | solution.py:138
  72.7 2.6 %collective-permute-start.65 = (bf16[256,1024]{1,0:T(8,128)(2,1)}, bf16[256,1024]{1,0:T(8,128)(2,1)}, u32[]{:S(2)}, u32[]{:S(2)}) collective-permute-start(bf16[256,1024]{1,0:T(8,128)(2,1)} %collective-permute-done.60.refs_3_), channel_id=1, source_target_pairs={{0,1},{1,0},{2,3},{3,2},{4,5},{5,4},{6,7},{7,6},{8,9},{9,8},{10,11... | collective-permute-start | bytes 1572872 | tf_op jit(solution)/shard_map/ppermute | solution.py:138
  82.3 15.8 %copy-start.3 = (s32[32]{0:T(128)S(1)}, s32[32]{0:T(128)}, u32[]{:S(2)}) copy-start(s32[32]{0:T(128)} %param.62) | copy-start | bytes 388
  82.3 16.5 %copy-start.4 = (s32[2]{0:T(128)S(1)}, s32[2]{0:T(128)}, u32[]{:S(2)}) copy-start(s32[2]{0:T(128)} %param.63) | copy-start | bytes 28
  83.3 8.5 %collective-permute-start.10 = (bf16[2,256,128]{2,1,0:T(8,128)(2,1)S(1)}, bf16[2,256,128]{2,1,0:T(8,128)(2,1)}, u32[]{:S(2)}, u32[]{:S(2)}) collective-permute-start(bf16[2,256,128]{2,1,0:T(8,128)(2,1)S(1)} %param.10), channel_id=1, source_target_pairs={{0,88},{8,80},{16,72},{24,64},{32,120},{40,112},{48,104},{56,96},{... | collective-permute-start | bytes 393224 | tf_op jit(solution)/shard_map/cond/branch_10_fun/ppermute | solution.py:31
  91.8 41.1 %all-to-all-start.2 = ((bf16[16,2,64,512]{3,2,1,0:T(8,128)(2,1)}), bf16[16,2,64,512]{3,2,1,0:T(8,128)(2,1)}, u32[]{:S(2)}, u32[]{:S(2)}) async-start(bf16[16,2,64,512]{3,2,1,0:T(8,128)(2,1)} %bitcast.41), calls=%async_computation.2 | async-start | bytes 4194304 | tf_op jit(solution)/shard_map/all_to_all | solution.py:344
  98.9 4.0 %copy-start.2 = (bf16[2,512,128]{2,1,0:T(8,128)(2,1)S(1)}, bf16[2,512,128]{2,1,0:T(8,128)(2,1)}, u32[]{:S(2)}) copy-start(bf16[2,512,128]{2,1,0:T(8,128)(2,1)} %get-tuple-element.159.own_ref) | copy-start | bytes 786436
  103.2 3.3 %collective-permute-start.52 = (f32[256,512]{1,0:T(8,128)}, f32[256,512]{1,0:T(8,128)S(1)}, u32[]{:S(2)}, u32[]{:S(2)}) collective-permute-start(f32[256,512]{1,0:T(8,128)} %get-tuple-element.122), channel_id=1, source_target_pairs={{0,1},{1,0},{2,3},{3,2},{4,5},{5,4},{6,7},{7,6},{8,9},{9,8},{10,11... | collective-permute-start | bytes 1572872 | tf_op jit(solution)/shard_map/cond/branch_1_fun/ppermute | solution.py:138
  107.6 19.2 %collective-permute-start.53 = (bf16[256,512]{1,0:T(8,128)(2,1)S(1)}, bf16[256,512]{1,0:T(8,128)(2,1)S(1)}, u32[]{:S(2)}, u32[]{:S(2)}) collective-permute-start(bf16[256,512]{1,0:T(8,128)(2,1)S(1)} %get-tuple-element.170), channel_id=1, source_target_pairs={{0,2},{1,3},{2,0},{3,1},{4,6},{5,7},{6,4},{7,5},{8,10},{9,11},{10,... | collective-permute-start | bytes 786440 | tf_op jit(solution)/shard_map/cond/branch_1_fun/ppermute | solution.py:138
  108.8 18.1 %collective-permute-start.54 = (bf16[256,512]{1,0:T(8,128)(2,1)S(1)}, bf16[256,512]{1,0:T(8,128)(2,1)}, u32[]{:S(2)}, u32[]{:S(2)}) collective-permute-start(bf16[256,512]{1,0:T(8,128)(2,1)S(1)} %get-tuple-element.170), channel_id=1, source_target_pairs={{0,4},{1,5},{2,6},{3,7},{4,0},{5,1},{6,2},{7,3},{8,12},{9,13},{10,... | collective-permute-start | bytes 786440 | tf_op jit(solution)/shard_map/cond/branch_1_fun/ppermute | solution.py:138
  111.6 15.3 %collective-permute-start.55 = (bf16[256,512]{1,0:T(8,128)(2,1)S(1)}, bf16[256,512]{1,0:T(8,128)(2,1)}, u32[]{:S(2)}, u32[]{:S(2)}) collective-permute-start(bf16[256,512]{1,0:T(8,128)(2,1)S(1)} %get-tuple-element.170), channel_id=1, source_target_pairs={{0,6},{1,7},{2,4},{3,5},{4,2},{5,3},{6,0},{7,1},{8,14},{9,15},{10,... | collective-permute-start | bytes 786440 | tf_op jit(solution)/shard_map/cond/branch_1_fun/ppermute | solution.py:138
  112.8 14.1 %collective-permute-start.34 = (bf16[2,256,128]{2,1,0:T(8,128)(2,1)S(1)}, bf16[2,256,128]{2,1,0:T(8,128)(2,1)}, u32[]{:S(2)}, u32[]{:S(2)}) collective-permute-start(bf16[2,256,128]{2,1,0:T(8,128)(2,1)S(1)} %param.35), channel_id=1, source_target_pairs={{0,40},{8,32},{16,56},{24,48},{32,8},{40,0},{48,24},{56,16},{64,10... | collective-permute-start | bytes 393224 | tf_op jit(solution)/shard_map/cond/branch_1_fun/cond/branch_4_fun/ppermute | solution.py:31
  128.8 4.2 %collective-permute-start.56 = (bf16[256,512]{1,0:T(8,128)(2,1)}, bf16[256,512]{1,0:T(8,128)(2,1)}, u32[]{:S(2)}, u32[]{:S(2)}) collective-permute-start(bf16[256,512]{1,0:T(8,128)(2,1)} %add_convert_fusion.1), channel_id=1, source_target_pairs={{0,1},{1,0},{2,3},{3,2},{4,5},{5,4},{6,7},{7,6},{8,9},{9,8},{10,11... | collective-permute-start | bytes 786440 | tf_op jit(solution)/shard_map/cond/branch_1_fun/ppermute | solution.py:138

commit v5 on v4

--- a/solution.py
+++ b/solution.py
@@ -31,8 +31,51 @@
     return lax.switch(mask - 1, moves, block)
 
 
+def take_kernel(asked_ref, table_ref, out_ref, rows_ref, in_sems, out_sems):
+    count = out_ref.shape[0]
+
+    def fetch(i):
+        index = asked_ref[i // MOST_PER_INDEX, i % MOST_PER_INDEX]
+        return pltpu.make_async_copy(table_ref.at[jnp.maximum(index, 0)], rows_ref.at[i], in_sems.at[i])
+
+    def store(i):
+        return pltpu.make_async_copy(rows_ref.at[i], out_ref.at[i], out_sems.at[i])
+
+    def for_asked(step):
+        for i in range(count):
+
+            @pl.when(asked_ref[i // MOST_PER_INDEX, i % MOST_PER_INDEX] >= 0)
+            def _(i=i):
+                step(i)
+
+    def pass_on(i):
+        fetch(i).wait()
+        store(i).start()
+
+    for_asked(lambda i: fetch(i).start())
+    for_asked(pass_on)
+    for_asked(lambda i: store(i).wait())
+
+
 def take_asked(table, asked):
-    return jnp.take(table, asked[:, :MOST_PER_INDEX].reshape(-1), axis=0, mode="clip")
+    count = asked.shape[0] * MOST_PER_INDEX
+    shape = (count,) + table.shape[1:]
+    return pl.pallas_call(
+        take_kernel,
+        out_shape=jax.ShapeDtypeStruct(shape, table.dtype),
+        grid_spec=pltpu.PrefetchScalarGridSpec(
+            num_scalar_prefetch=1,
+            grid=(1,),
+            in_specs=[pl.BlockSpec(memory_space=pl.ANY)],
+            out_specs=pl.BlockSpec(memory_space=pl.ANY),
+            scratch_shapes=[
+                pltpu.VMEM(shape, table.dtype),
+                pltpu.SemaphoreType.DMA((count,)),
+                pltpu.SemaphoreType.DMA((count,)),
+            ],
+        ),
+        name="take_asked",
+    )(asked, table)
 
 
 def project_kernel(pieces, carried, order_ref, query_weight_ref, keyval_weight_ref, *refs):
@@ -183,47 +226,57 @@
     return total[0], total[1], extra
 
 
-def partial_kernel(slots_ref, core_ref, tokens_ref, *refs):
-    downs, keep_ref, send_ref = refs[:-2], refs[-2], refs[-1]
-    rows = jnp.concatenate([d[0] for d in downs], axis=0)
-    acts = lax.dot_general(
-        tokens_ref[...], rows, (((1,), (1,)), ((), ())), preferred_element_type=jnp.float32
-    )
-    kept = pl.program_id(0) == core_ref[0]
-
-    @pl.when(kept)
-    def _():
-        keep_ref[...] = acts
-
-    @pl.when(jnp.logical_not(kept))
-    def _():
-        send_ref[...] = acts
+def block_copies(slots_ref, source_ref, rows_ref, sems, rubrics, first, count):
+    ranks = source_ref.shape[1]
+    return [
+        pltpu.make_async_copy(
+            source_ref.at[slots_ref[j * rubrics + s]],
+            rows_ref.at[j, pl.ds(s * ranks, ranks)],
+            sems.at[j * rubrics + s],
+        )
+        for j in range(first, first + count)
+        for s in range(rubrics)
+    ]
+
+
+def partial_kernel(rubrics, slots_ref, core_ref, tokens_ref, down_ref, keep_ref, send_ref, rows_ref, sems):
+    copies = block_copies(slots_ref, down_ref, rows_ref, sems, rubrics, 0, 2)
+    for copy in copies:
+        copy.start()
+    for copy in copies:
+        copy.wait()
+    resp_len = keep_ref.shape[0]
+    for out_ref, j in ((send_ref, 1 - core_ref[0]), (keep_ref, core_ref[0])):
+        out_ref[...] = lax.dot_general(
+            tokens_ref[pl.ds(j * resp_len, resp_len), :], rows_ref[j], (((1,), (1,)), ((), ())),
+            preferred_element_type=jnp.float32,
+        )
 
 
 def partial_rank_acts(tokens, got_down, slots, core, rubrics):
     rows, features = tokens.shape
     ranks = got_down.shape[1]
-    resp_len = rows // 2
-
-    def down_spec(s):
-        return pl.BlockSpec((1, ranks, features), lambda j, slots_ref, _: (slots_ref[j * rubrics + s], 0, 0))
-
-    half = jax.ShapeDtypeStruct((resp_len, rubrics * ranks), jnp.float32)
-    half_spec = pl.BlockSpec(half.shape, lambda j, *_: (0, 0))
+    half = jax.ShapeDtypeStruct((rows // 2, rubrics * ranks), jnp.float32)
+    half_spec = pl.BlockSpec(half.shape, lambda i, *_: (0, 0))
     return pl.pallas_call(
-        partial_kernel,
+        partial(partial_kernel, rubrics),
         out_shape=(half, half),
         grid_spec=pltpu.PrefetchScalarGridSpec(
             num_scalar_prefetch=2,
-            grid=(2,),
-            in_specs=[pl.BlockSpec((resp_len, features), lambda j, *_: (j, 0))]
-            + [down_spec(s) for s in range(rubrics)],
+            grid=(1,),
+            in_specs=[
+                pl.BlockSpec((rows, features), lambda i, *_: (0, 0)),
+                pl.BlockSpec(memory_space=pl.ANY),
+            ],
             out_specs=(half_spec, half_spec),
+            scratch_shapes=[
+                pltpu.VMEM((2, rubrics * ranks, features), jnp.bfloat16),
+                pltpu.SemaphoreType.DMA((2 * rubrics,)),
+            ],
         ),
         compiler_params=pltpu.CompilerParams(vmem_limit_bytes=32 << 20),
-        cost_estimate=pl.CostEstimate(flops=2 * rows * features * ranks * rubrics, bytes_accessed=4 << 20, transcendentals=0),
         name="partial_rank_acts",
-    )(slots, core, tokens, *([got_down] * rubrics))
+    )(slots, core, tokens, got_down)
 
 
 def attend_kernel(
@@ -320,7 +373,7 @@
     lane = lax.broadcasted_iota(jnp.int32, (owner_groups, LANES), 1)
     cells = jnp.where(lane < MOST_PER_INDEX, cells + lane, -1)
     wanted = jnp.max(
-        jnp.where(buffer_slot[:, None, None] == cells[None], local_ids[:, None, None], 0), axis=0
+        jnp.where(buffer_slot[:, None, None] == cells[None], local_ids[:, None, None], -1), axis=0
     )
     asked = lax.all_to_all(wanted, "dp", split_axis=0, concat_axis=0, tiled=True)
     shipped_down = take_asked(adapter_down_weight, asked)
@@ -328,7 +381,13 @@
     got_down = lax.all_to_all(shipped_down, "dp", split_axis=0, concat_axis=0, tiled=True)
     shipped_up = take_asked(adapter_up_weight, asked)
     shipped_up = shipped_up.reshape(owner_groups, MOST_PER_INDEX, rank_extent, head_columns)
-    before, after, shipped_up = lax.optimization_barrier((before, after, shipped_up))
+    own_lens = lax.dynamic_slice_in_dim(lengths, own_index * resp_dev, resp_dev)
+    mate_index = partner_dev * resp_dev + jnp.arange(resp_dev, dtype=jnp.int32)
+    mate_lens = jnp.take(lengths, mate_index, axis=0, mode="clip")
+    mate_lens = jnp.where(partner_attend_mask == 1, mate_lens, 0)
+    before, after, shipped_up, own_lens, mate_lens = lax.optimization_barrier(
+        (before, after, shipped_up, own_lens, mate_lens)
+    )
     half = tok_rows // 2
     opposite = (along_column(before[:half], 1), along_column(after[half:], -1))
     near, order = paired([(tokens,), (before,), (after,)], (0, -2, 2))
@@ -363,10 +422,6 @@
     same, other, mate_second = lax.cond(
         lengths[0] >= 1, split_sum, plain_sum, (keep, send, own_keyval[:, 1])
     )
-    own_lens = lax.dynamic_slice_in_dim(lengths, own_index * resp_dev, resp_dev)
-    mate_index = partner_dev * resp_dev + jnp.arange(resp_dev, dtype=jnp.int32)
-    mate_lens = jnp.take(lengths, mate_index, axis=0, mode="clip")
-    mate_lens = jnp.where(partner_attend_mask == 1, mate_lens, 0)
     return attend(
         (same, other), base, keyval, (mate_first, mate_second), got_up.reshape(-1, rank_extent, head_columns),
         buffer_slot, own_lens, mate_lens, core.reshape(1), rubrics,

time: 139 us -> 137 us (0.986)
  local copies, waits for them, and re-layouts: 14.1 us -> 4.85 us
  Pallas kernels: 29.3 us -> 34.8 us
  waiting for transfers between devices: 38.5 us -> 42 us
    gather x2 -> x0, local copies, waits for them, and re-layouts: 7.02 us -> none  [take_asked(): jnp.take(table, asked[:, :MOST_PER_INDEX].reshape(-1), axis=0, mode='clip')]
    pallas_call x1 -> x3, Pallas kernels: 4.01 us -> 9.95 us  [the longest x2 6.93 us: take_asked(): pl.pallas_call(take_kernel, out_shape=jax.ShapeDtypeStruct(shape, table.d...]
    ppermute x2, waiting for transfers between devices: 15.1 us -> 20.5 us  [from_partner(): return lax.switch(mask - 1, moves, block)]
    slice x2, local copies, waits for them, and re-layouts: 3.75 us -> 1.67 us  [on_device(): opposite = (along_column(before[:half], 1), along_column(after[half:], -1))]
    all_to_all x1, starting transfers between devices: 6.25 us -> 4.53 us  [on_device(): lax.all_to_all(shipped_up, 'dp', split_axis=0, concat_axis=0, tiled=True)]
    ppermute x4, waiting for transfers between devices: 17.6 us -> 16.1 us  [along_column(): lax.ppermute(block, 'tensor', [(source, (source + 2 * step) % size) for s...]
  transfers between devices with their start and end apart: 18 -> 18, of which waited for: 8 -> 8; matrix products, arithmetic and copies ran while one was open for 8% -> 4% of each run, Pallas kernels for 16% -> 18%
where the time goes in v5:
time: 137 us; the launch traced here: 138 us
  waiting for transfers between devices  42 us (31%)
  starting transfers between devices  38.5 us (28%)
  Pallas kernels  34.8 us (25%)
  blocking collectives  13.9 us (10%)
  local copies, waits for them, and re-layouts  4.85 us (4%)
  other arithmetic  2.47 us (2%)
    ppermute x2, waiting for transfers between devices, from_partner(): return lax.switch(mask - 1, moves, block)  20.5 us
    pallas_call x2, Pallas kernels, project(): pl.pallas_call(partial(project_kernel, pieces, bool(sums)), out_shape=(pl...  18.1 us
    ppermute x4, waiting for transfers between devices, along_column(): lax.ppermute(block, 'tensor', [(source, (source + 2 * step) % size) for s...  16.1 us
    ppermute x10, starting transfers between devices, across_tensor(): lax.ppermute(block, 'tensor', [(source, source ^ flip) for source in rang...  14.5 us
    all_to_all x1, blocking collectives, on_device(): lax.all_to_all(wanted, 'dp', split_axis=0, concat_axis=0, tiled=True)  13.9 us
    ppermute x2, starting transfers between devices, from_partner(): return lax.switch(mask - 1, moves, block)  8.12 us
    pallas_call x2, Pallas kernels, take_asked(): pl.pallas_call(take_kernel, out_shape=jax.ShapeDtypeStruct(shape, table.d...  6.93 us
    pallas_call x1, Pallas kernels, attend(): pl.pallas_call(attend_kernel, out_shape=jax.ShapeDtypeStruct((rows, colum...  6.72 us
  transfers between devices with their start and end apart: 18, of which 8 were waited for; matrix products, arithmetic and copies ran while one was open for 4% of the time, Pallas kernels for 18%

profile of v5, /device:TPU:1, one launch (start us, length us, event | category | flops | bytes accessed | tf_op | source)
XLA Modules:
  0.0 137.7 jit_solution(5296305603532035423)
XLA Ops:
  0.0 0.8 reshape.185
  0.8 0.2 and_reduce_fusion
  1.0 0.1 add_select_fusion
  1.1 0.1 select_reduce_fusion
  1.2 13.9 %all_to_all.21 = s32[16,1,128]{2,1,0:T(1,128)} all-to-all(s32[16,1,128]{2,1,0:T(1,128)S(1)} %bitcast.53), channel_id=1, replica_groups=mesh['dp'=16,'tensor'=8] {'dp'}, dimensions={0} | all-to-all | bytes 16384 | tf_op jit(solution)/shard_map/all_to_all | solution.py:378
  15.1 3.7 %take_asked.3 = bf16[32,64,1024]{2,1,0:T(8,128)(2,1)} custom-call(s32[16,128]{1,0:T(8,128)} %bitcast.51, bf16[32,64,1024]{2,1,0:T(8,128)(2,1)} %table_ref.3), custom_call_target="tpu_custom_call" | custom-call | tf_op jit(solution)/shard_map/take_asked/pallas_call | solution.py:63
  18.8 0.0 copy-start
  18.8 0.0 copy-start.2
  18.8 0.0 copy-start.4
  18.8 0.0 copy-start.3
  18.8 4.7 %all-to-all-start.1 = ((bf16[16,2,64,1024]{3,2,1,0:T(8,128)(2,1)}), bf16[16,2,64,1024]{3,2,1,0:T(8,128)(2,1)}, u32[]{:S(2)}, u32[]{:S(2)}) async-start(bf16[16,2,64,1024]{3,2,1,0:T(8,128)(2,1)} %bitcast.47), calls=%async_computation.1 | async-start | bytes 8388608 | tf_op jit(solution)/shard_map/all_to_all | solution.py:381
  23.5 1.7 %collective-permute-start.57 = (bf16[512,1024]{1,0:T(8,128)(2,1)S(1)}, bf16[512,1024]{1,0:T(8,128)(2,1)S(1)}, u32[]{:S(2)}, u32[]{:S(2)}) collective-permute-start(bf16[512,1024]{1,0:T(8,128)(2,1)S(1)} %copy-done), channel_id=1, source_target_pairs={{0,2},{1,3},{2,4},{3,5},{4,6},{5,7},{6,0},{7,1},{8,10},{9,11},{10,... | collective-permute-start | bytes 3145736 | tf_op jit(solution)/shard_map/ppermute | solution.py:186
  25.2 2.2 %collective-permute-start.58 = (bf16[512,1024]{1,0:T(8,128)(2,1)S(1)}, bf16[512,1024]{1,0:T(8,128)(2,1)S(1)}, u32[]{:S(2)}, u32[]{:S(2)}) collective-permute-start(bf16[512,1024]{1,0:T(8,128)(2,1)S(1)} %copy-done), channel_id=1, source_target_pairs={{0,6},{1,7},{2,0},{3,1},{4,2},{5,3},{6,4},{7,5},{8,14},{9,15},{10,... | collective-permute-start | bytes 3145736 | tf_op jit(solution)/shard_map/ppermute | solution.py:186
  27.4 2.2 %collective-permute-start.61 = (bf16[512,1024]{1,0:T(8,128)(2,1)S(1)}, bf16[512,1024]{1,0:T(8,128)(2,1)}, u32[]{:S(2)}, u32[]{:S(2)}) collective-permute-start(bf16[512,1024]{1,0:T(8,128)(2,1)S(1)} %copy-done), channel_id=1, source_target_pairs={{0,1},{1,0},{2,3},{3,2},{4,5},{5,4},{6,7},{7,6},{8,9},{9,8},{10,11... | collective-permute-start | bytes 3145736 | tf_op jit(solution)/shard_map/ppermute | solution.py:181
  29.7 0.1 dynamic_slice.3.lens_ref
  29.8 0.6 gather_fusion
  30.4 3.2 %take_asked.2 = bf16[32,64,512]{2,1,0:T(8,128)(2,1)} custom-call(s32[16,128]{1,0:T(8,128)} %bitcast.52, bf16[32,64,512]{2,1,0:T(8,128)(2,1)} %table_ref.2), custom_call_target="tpu_custom_call" | custom-call | tf_op jit(solution)/shard_map/take_asked/pallas_call | solution.py:63
  33.7 15.3 %collective-permute-done.57.refs_2_ = bf16[512,1024]{1,0:T(8,128)(2,1)S(1)} collective-permute-done((bf16[512,1024]{1,0:T(8,128)(2,1)S(1)}, bf16[512,1024]{1,0:T(8,128)(2,1)S(1)}, u32[]{:S(2)}, u32[]{:S(2)}) %collective-permute-start.57) | collective-permute-done | bytes 1048608 | tf_op jit(solution)/shard_map/ppermute | solution.py:186
  49.0 0.0 collective-permute-done.58.refs_4_
  49.0 2.5 %collective-permute-start.62 = (bf16[512,1024]{1,0:T(8,128)(2,1)S(1)}, bf16[512,1024]{1,0:T(8,128)(2,1)}, u32[]{:S(2)}, u32[]{:S(2)}) collective-permute-start(bf16[512,1024]{1,0:T(8,128)(2,1)S(1)} %collective-permute-done.57.refs_2_), channel_id=1, source_target_pairs={{0,1},{1,0},{2,3},{3,2},{4,5},{5,4},{6,7},{7,6},{8,9},{9,8},{10,11... | collective-permute-start | bytes 3145736 | tf_op jit(solution)/shard_map/ppermute | solution.py:181
  51.5 0.0 collective-permute-start.63
  51.5 0.8 slice.32
  52.3 0.8 slice.33
  53.1 1.0 collective-permute-start.59
  54.1 1.8 %collective-permute-start.60 = (bf16[256,1024]{1,0:T(8,128)(2,1)}, bf16[256,1024]{1,0:T(8,128)(2,1)}, u32[]{:S(2)}, u32[]{:S(2)}) collective-permute-start(bf16[256,1024]{1,0:T(8,128)(2,1)} %slice.33), channel_id=1, source_target_pairs={{0,6},{1,7},{2,0},{3,1},{4,2},{5,3},{6,4},{7,5},{8,14},{9,15},{10,... | collective-permute-start | bytes 1572872 | tf_op jit(solution)/shard_map/ppermute | solution.py:186
  55.9 0.1 stack.48.order_ref
  56.0 0.0 collective-permute-done.61.refs_1_
  56.0 0.0 collective-permute-done.62.refs_3_
  56.0 0.0 collective-permute-done.63.refs_5_
  56.0 11.1 %project.2 = (f32[512,512]{1,0:T(8,128)}, f32[512,256]{1,0:T(8,128)}) custom-call(s32[6]{0:T(128)S(1)} %stack.48.order_ref, bf16[8192,512]{1,0:T(8,128)(2,1)} %query_weight_ref.3, bf16[2,8192,128]{2,1,0:T(8,128)(2,1)} %keyval_weight_ref.3, bf16[512,1024]{1,0:T(8,128)(2,1)S(1)} %copy-done, bf16[512,1024]{1,0:T(8,128)(2,1)} %collective-permute-done.61.refs_1_, ...), custom_call_target="tpu_custom_call" | custom-call | flops 4831838208 | bytes 15728640 | tf_op jit(solution)/shard_map/project/pallas_call | solution.py:144
  67.1 0.8 collective-permute-done.59.refs_2_
  67.8 0.0 collective-permute-done.60.refs_3_
  67.8 1.3 collective-permute-start.64
  69.1 0.0 collective-permute-start.65
  69.1 0.1 pad_add_fusion.order_ref
  69.2 1.6 %collective-permute-done.64.refs_4_ = bf16[256,1024]{1,0:T(8,128)(2,1)S(1)} collective-permute-done((bf16[256,1024]{1,0:T(8,128)(2,1)}, bf16[256,1024]{1,0:T(8,128)(2,1)S(1)}, u32[]{:S(2)}, u32[]{:S(2)}) %collective-permute-start.64) | collective-permute-done | bytes 524320 | tf_op jit(solution)/shard_map/ppermute | solution.py:181
  70.8 0.7 collective-permute-done.65.refs_5_
  71.6 7.0 %project.3 = (f32[512,512]{1,0:T(8,128)}, bf16[2,512,128]{2,1,0:T(8,128)(2,1)}) custom-call(s32[2]{0:T(128)S(1)} %pad_add_fusion.order_ref, bf16[8192,512]{1,0:T(8,128)(2,1)} %query_weight_ref.3, bf16[2,8192,128]{2,1,0:T(8,128)(2,1)} %keyval_weight_ref.3, f32[512,512]{1,0:T(8,128)} %get-tuple-element.159.refs_0_, f32[512,256]{1,0:T(8,128)} %get-tuple-element.160.refs_1_, ...), custom_call_target="tpu_custom_call" | custom-call | flops 1610612736 | bytes 5242880 | tf_op jit(solution)/shard_map/project/pallas_call | solution.py:144
  78.6 0.9 slice_bitcast_fusion.3
  79.6 8.0 %conditional.4 = (bf16[2,256,128]{2,1,0:T(8,128)(2,1)}) conditional(s32[]{:T(128)} %bitcast.13, bf16[2,256,128]{2,1,0:T(8,128)(2,1)S(1)} %slice_bitcast_fusion.3, bf16[2,256,128]{2,1,0:T(8,128)(2,1)S(1)} %slice_bitcast_fusion.3, bf16[2,256,128]{2,1,0:T(8,128)(2,1)S(1)} %slice_bitcast_fusion.3, ...), branch_computations={%region_2.3_spmd, %region_3.4_spmd, %region_4.5_spmd, %region_5.6_... | conditional | bytes 524336 | solution.py:31
  79.6 2.5 %collective-permute-start.2 = (bf16[2,256,128]{2,1,0:T(8,128)(2,1)S(1)}, bf16[2,256,128]{2,1,0:T(8,128)(2,1)}, u32[]{:S(2)}, u32[]{:S(2)}) collective-permute-start(bf16[2,256,128]{2,1,0:T(8,128)(2,1)S(1)} %param.2), channel_id=1, source_target_pairs={{0,24},{8,16},{16,8},{24,0},{32,56},{40,48},{48,40},{56,32},{64,88... | collective-permute-start | bytes 393224 | tf_op jit(solution)/shard_map/cond/branch_2_fun/ppermute | solution.py:31
  82.1 5.5 %collective-permute-done.2 = bf16[2,256,128]{2,1,0:T(8,128)(2,1)} collective-permute-done((bf16[2,256,128]{2,1,0:T(8,128)(2,1)S(1)}, bf16[2,256,128]{2,1,0:T(8,128)(2,1)}, u32[]{:S(2)}, u32[]{:S(2)}) %collective-permute-start.2) | collective-permute-done | bytes 131104 | tf_op jit(solution)/shard_map/cond/branch_2_fun/ppermute | solution.py:31
  87.5 0.0 all-to-all-done.1
  87.5 4.5 %all-to-all-start.2 = ((bf16[16,2,64,512]{3,2,1,0:T(8,128)(2,1)}), bf16[16,2,64,512]{3,2,1,0:T(8,128)(2,1)S(1)}, u32[]{:S(2)}, u32[]{:S(2)}) async-start(bf16[16,2,64,512]{3,2,1,0:T(8,128)(2,1)} %bitcast.48), calls=%async_computation.2 | async-start | bytes 4194304 | tf_op jit(solution)/shard_map/all_to_all | solution.py:403
  92.1 3.0 %partial_rank_acts.1 = (f32[256,512]{1,0:T(8,128)S(1)}, f32[256,512]{1,0:T(8,128)S(1)}) custom-call(s32[16]{0:T(128)S(1)} %convert_add_fusion.slots_ref, s32[1]{0:T(128)} %bitcast.10.core_ref, bf16[512,1024]{1,0:T(8,128)(2,1)S(1)} %copy-done, bf16[32,64,1024]{2,1,0:T(8,128)(2,1)} %bitcast.24.down_ref), custom_call_target="tpu_custom_call" | custom-call | tf_op jit(solution)/shard_map/partial_rank_acts/pallas_call | solution.py:261
  95.2 35.8 %conditional.5 = (bf16[256,512]{1,0:T(8,128)(2,1)}, bf16[256,512]{1,0:T(8,128)(2,1)}, bf16[2,256,128]{2,1,0:T(8,128)(2,1)}) conditional(s32[]{:T(128)} %bitcast.11, (s32[]{:T(128)}, f32[256,512]{1,0:T(8,128)S(1)}, f32[256,512]{1,0:T(8,128)S(1)}, s32[2]{0:T(128)S(1)}, bf16[2,256,128]{2,1,0:T(8,128)(2,1)S(1)}) %tuple.208, ...), branch_computations={%region_17.33_spmd, %region_33.49_spmd} | conditional | flops 3145731 | bytes 45089164 | solution.py:422
  95.4 1.6 %collective-permute-start.52 = (f32[256,512]{1,0:T(8,128)S(1)}, f32[256,512]{1,0:T(8,128)S(1)}, u32[]{:S(2)}, u32[]{:S(2)}) collective-permute-start(f32[256,512]{1,0:T(8,128)S(1)} %get-tuple-element.122), channel_id=1, source_target_pairs={{0,1},{1,0},{2,3},{3,2},{4,5},{5,4},{6,7},{7,6},{8,9},{9,8},{10,11... | collective-permute-start | bytes 1572872 | tf_op jit(solution)/shard_map/cond/branch_1_fun/ppermute | solution.py:181
  97.0 1.5 %collective-permute-done.52 = f32[256,512]{1,0:T(8,128)S(1)} collective-permute-done((f32[256,512]{1,0:T(8,128)S(1)}, f32[256,512]{1,0:T(8,128)S(1)}, u32[]{:S(2)}, u32[]{:S(2)}) %collective-permute-start.52) | collective-permute-done | bytes 524320 | tf_op jit(solution)/shard_map/cond/branch_1_fun/ppermute | solution.py:181
  98.5 0.1 fusion
  98.6 1.1 collective-permute-start.53
  99.7 3.3 %collective-permute-start.54 = (bf16[256,512]{1,0:T(8,128)(2,1)S(1)}, bf16[256,512]{1,0:T(8,128)(2,1)}, u32[]{:S(2)}, u32[]{:S(2)}) collective-permute-start(bf16[256,512]{1,0:T(8,128)(2,1)S(1)} %get-tuple-element.174), channel_id=1, source_target_pairs={{0,4},{1,5},{2,6},{3,7},{4,0},{5,1},{6,2},{7,3},{8,12},{9,13},{10,... | collective-permute-start | bytes 786440 | tf_op jit(solution)/shard_map/cond/branch_1_fun/ppermute | solution.py:181
  103.0 0.0 collective-permute-start.55
  103.0 0.7 slice.23
  104.3 20.7 %conditional.1 = (bf16[2,256,128]{2,1,0:T(8,128)(2,1)}) conditional(s32[]{:T(128)} %bitcast.5, bf16[2,256,128]{2,1,0:T(8,128)(2,1)S(1)} %get-tuple-element.125, bf16[2,256,128]{2,1,0:T(8,128)(2,1)S(1)} %get-tuple-element.125, bf16[2,256,128]{2,1,0:T(8,128)(2,1)S(1)} %get-tuple-element.125, ...), branch_computations={%region_34.34_spmd, %region_35.35_spmd, %region_36.36_spmd, %regio... | conditional | bytes 524336 | solution.py:31
  104.4 5.6 %collective-permute-start.39 = (bf16[2,256,128]{2,1,0:T(8,128)(2,1)S(1)}, bf16[2,256,128]{2,1,0:T(8,128)(2,1)}, u32[]{:S(2)}, u32[]{:S(2)}) collective-permute-start(bf16[2,256,128]{2,1,0:T(8,128)(2,1)S(1)} %param.40), channel_id=1, source_target_pairs={{0,80},{8,88},{16,64},{24,72},{32,112},{40,120},{48,96},{56,104},{... | collective-permute-start | bytes 393224 | tf_op jit(solution)/shard_map/cond/branch_1_fun/cond/branch_9_fun/ppermute | solution.py:31
  110.0 15.0 %collective-permute-done.39 = bf16[2,256,128]{2,1,0:T(8,128)(2,1)} collective-permute-done((bf16[2,256,128]{2,1,0:T(8,128)(2,1)S(1)}, bf16[2,256,128]{2,1,0:T(8,128)(2,1)}, u32[]{:S(2)}, u32[]{:S(2)}) %collective-permute-start.39) | collective-permute-done | bytes 131104 | tf_op jit(solution)/shard_map/cond/branch_1_fun/cond/branch_9_fun/ppermute | solution.py:31
  125.0 0.0 collective-permute-done.53
  125.0 0.0 collective-permute-done.54
  125.0 0.0 collective-permute-done.55
  125.0 1.9 %add_convert_fusion.1 = bf16[256,512]{1,0:T(8,128)(2,1)} fusion(bf16[256,512]{1,0:T(8,128)(2,1)} %collective-permute-done.55, bf16[256,512]{1,0:T(8,128)(2,1)} %collective-permute-done.54, f32[256,512]{1,0:T(8,128)S(1)} %get-tuple-element.175, bf16[256,512]{1,0:T(8,128)(2,1)S(1)} %collective-permute-done.53), kind=kLoop, calls=%fused_computation.7 | loop fusion | flops 917504 | bytes 1572864 | tf_op jit(solution)/shard_map/cond/branch_1_fun/convert_element_type | solution.py:214
  126.9 2.5 %collective-permute-start.56 = (bf16[256,512]{1,0:T(8,128)(2,1)}, bf16[256,512]{1,0:T(8,128)(2,1)}, u32[]{:S(2)}, u32[]{:S(2)}) collective-permute-start(bf16[256,512]{1,0:T(8,128)(2,1)} %add_convert_fusion.1), channel_id=1, source_target_pairs={{0,1},{1,0},{2,3},{3,2},{4,5},{5,4},{6,7},{7,6},{8,9},{9,8},{10,11... | collective-permute-start | bytes 786440 | tf_op jit(solution)/shard_map/cond/branch_1_fun/ppermute | solution.py:181
  129.5 1.5 %collective-permute-done.56 = bf16[256,512]{1,0:T(8,128)(2,1)} collective-permute-done((bf16[256,512]{1,0:T(8,128)(2,1)}, bf16[256,512]{1,0:T(8,128)(2,1)}, u32[]{:S(2)}, u32[]{:S(2)}) %collective-permute-start.56) | collective-permute-done | bytes 262176 | tf_op jit(solution)/shard_map/cond/branch_1_fun/ppermute | solution.py:181
  131.0 0.0 all-to-all-done.2
  131.0 6.7 %attend.1 = bf16[512,512]{1,0:T(8,128)(2,1)} custom-call(s32[16]{0:T(128)S(1)} %convert_add_fusion.slots_ref, s32[2]{0:T(128)S(1)} %dynamic_slice.3.lens_ref, s32[2]{0:T(128)S(1)} %compare_select_fusion.mates_ref, s32[1]{0:T(128)} %bitcast.10.core_ref, bf16[256,512]{1,0:T(8,128)(2,1)} %get-tuple-element.168.same_ref, ...), custom_call_target="tpu_custom_call" | custom-call | tf_op jit(solution)/shard_map/attend/pallas_call | solution.py:326
  (14 shorter events, 0.1 us)
Async XLA Ops:
  18.8 4.8 %copy-start = (bf16[512,1024]{1,0:T(8,128)(2,1)S(1)}, bf16[512,1024]{1,0:T(8,128)(2,1)}, u32[]{:S(2)}) copy-start(bf16[512,1024]{1,0:T(8,128)(2,1)} %tokens_ref.1) | copy-start | bytes 3145732
  18.8 10.9 %copy-start.2 = (s32[32]{0:T(128)S(1)}, s32[32]{0:T(128)}, u32[]{:S(2)}) copy-start(s32[32]{0:T(128)} %param.62) | copy-start | bytes 388
  18.8 11.0 %copy-start.4 = (s32[2]{0:T(128)S(1)}, s32[2]{0:T(128)}, u32[]{:S(2)}) copy-start(s32[2]{0:T(128)} %param.64) | copy-start | bytes 28
  18.8 11.6 %copy-start.3 = (s32[2]{0:T(128)S(1)}, s32[2]{0:T(128)}, u32[]{:S(2)}) copy-start(s32[2]{0:T(128)} %param.63) | copy-start | bytes 28
  18.8 68.7 %all-to-all-start.1 = ((bf16[16,2,64,1024]{3,2,1,0:T(8,128)(2,1)}), bf16[16,2,64,1024]{3,2,1,0:T(8,128)(2,1)}, u32[]{:S(2)}, u32[]{:S(2)}) async-start(bf16[16,2,64,1024]{3,2,1,0:T(8,128)(2,1)} %bitcast.47), calls=%async_computation.1 | async-start | bytes 8388608 | tf_op jit(solution)/shard_map/all_to_all | solution.py:381
  23.5 25.5 %collective-permute-start.57 = (bf16[512,1024]{1,0:T(8,128)(2,1)S(1)}, bf16[512,1024]{1,0:T(8,128)(2,1)S(1)}, u32[]{:S(2)}, u32[]{:S(2)}) collective-permute-start(bf16[512,1024]{1,0:T(8,128)(2,1)S(1)} %copy-done), channel_id=1, source_target_pairs={{0,2},{1,3},{2,4},{3,5},{4,6},{5,7},{6,0},{7,1},{8,10},{9,11},{10,... | collective-permute-start | bytes 3145736 | tf_op jit(solution)/shard_map/ppermute | solution.py:186
  25.2 23.7 %collective-permute-start.58 = (bf16[512,1024]{1,0:T(8,128)(2,1)S(1)}, bf16[512,1024]{1,0:T(8,128)(2,1)S(1)}, u32[]{:S(2)}, u32[]{:S(2)}) collective-permute-start(bf16[512,1024]{1,0:T(8,128)(2,1)S(1)} %copy-done), channel_id=1, source_target_pairs={{0,6},{1,7},{2,0},{3,1},{4,2},{5,3},{6,4},{7,5},{8,14},{9,15},{10,... | collective-permute-start | bytes 3145736 | tf_op jit(solution)/shard_map/ppermute | solution.py:186
  27.4 28.6 %collective-permute-start.61 = (bf16[512,1024]{1,0:T(8,128)(2,1)S(1)}, bf16[512,1024]{1,0:T(8,128)(2,1)}, u32[]{:S(2)}, u32[]{:S(2)}) collective-permute-start(bf16[512,1024]{1,0:T(8,128)(2,1)S(1)} %copy-done), channel_id=1, source_target_pairs={{0,1},{1,0},{2,3},{3,2},{4,5},{5,4},{6,7},{7,6},{8,9},{9,8},{10,11... | collective-permute-start | bytes 3145736 | tf_op jit(solution)/shard_map/ppermute | solution.py:181
  49.0 7.0 %collective-permute-start.62 = (bf16[512,1024]{1,0:T(8,128)(2,1)S(1)}, bf16[512,1024]{1,0:T(8,128)(2,1)}, u32[]{:S(2)}, u32[]{:S(2)}) collective-permute-start(bf16[512,1024]{1,0:T(8,128)(2,1)S(1)} %collective-permute-done.57.refs_2_), channel_id=1, source_target_pairs={{0,1},{1,0},{2,3},{3,2},{4,5},{5,4},{6,7},{7,6},{8,9},{9,8},{10,11... | collective-permute-start | bytes 3145736 | tf_op jit(solution)/shard_map/ppermute | solution.py:181
  51.5 4.5 %collective-permute-start.63 = (bf16[512,1024]{1,0:T(8,128)(2,1)S(1)}, bf16[512,1024]{1,0:T(8,128)(2,1)}, u32[]{:S(2)}, u32[]{:S(2)}) collective-permute-start(bf16[512,1024]{1,0:T(8,128)(2,1)S(1)} %collective-permute-done.58.refs_4_), channel_id=1, source_target_pairs={{0,1},{1,0},{2,3},{3,2},{4,5},{5,4},{6,7},{7,6},{8,9},{9,8},{10,11... | collective-permute-start | bytes 3145736 | tf_op jit(solution)/shard_map/ppermute | solution.py:181
  53.1 14.7 %collective-permute-start.59 = (bf16[256,1024]{1,0:T(8,128)(2,1)}, bf16[256,1024]{1,0:T(8,128)(2,1)}, u32[]{:S(2)}, u32[]{:S(2)}) collective-permute-start(bf16[256,1024]{1,0:T(8,128)(2,1)} %slice.32), channel_id=1, source_target_pairs={{0,2},{1,3},{2,4},{3,5},{4,6},{5,7},{6,0},{7,1},{8,10},{9,11},{10,... | collective-permute-start | bytes 1572872 | tf_op jit(solution)/shard_map/ppermute | solution.py:186
  54.1 13.7 %collective-permute-start.60 = (bf16[256,1024]{1,0:T(8,128)(2,1)}, bf16[256,1024]{1,0:T(8,128)(2,1)}, u32[]{:S(2)}, u32[]{:S(2)}) collective-permute-start(bf16[256,1024]{1,0:T(8,128)(2,1)} %slice.33), channel_id=1, source_target_pairs={{0,6},{1,7},{2,0},{3,1},{4,2},{5,3},{6,4},{7,5},{8,14},{9,15},{10,... | collective-permute-start | bytes 1572872 | tf_op jit(solution)/shard_map/ppermute | solution.py:186
  67.8 3.0 %collective-permute-start.64 = (bf16[256,1024]{1,0:T(8,128)(2,1)}, bf16[256,1024]{1,0:T(8,128)(2,1)S(1)}, u32[]{:S(2)}, u32[]{:S(2)}) collective-permute-start(bf16[256,1024]{1,0:T(8,128)(2,1)} %collective-permute-done.59.refs_2_), channel_id=1, source_target_pairs={{0,1},{1,0},{2,3},{3,2},{4,5},{5,4},{6,7},{7,6},{8,9},{9,8},{10,11... | collective-permute-start | bytes 1572872 | tf_op jit(solution)/shard_map/ppermute | solution.py:181
  69.1 2.5 %collective-permute-start.65 = (bf16[256,1024]{1,0:T(8,128)(2,1)}, bf16[256,1024]{1,0:T(8,128)(2,1)S(1)}, u32[]{:S(2)}, u32[]{:S(2)}) collective-permute-start(bf16[256,1024]{1,0:T(8,128)(2,1)} %collective-permute-done.60.refs_3_), channel_id=1, source_target_pairs={{0,1},{1,0},{2,3},{3,2},{4,5},{5,4},{6,7},{7,6},{8,9},{9,8},{10,11... | collective-permute-start | bytes 1572872 | tf_op jit(solution)/shard_map/ppermute | solution.py:181
  79.6 7.9 %collective-permute-start.2 = (bf16[2,256,128]{2,1,0:T(8,128)(2,1)S(1)}, bf16[2,256,128]{2,1,0:T(8,128)(2,1)}, u32[]{:S(2)}, u32[]{:S(2)}) collective-permute-start(bf16[2,256,128]{2,1,0:T(8,128)(2,1)S(1)} %param.2), channel_id=1, source_target_pairs={{0,24},{8,16},{16,8},{24,0},{32,56},{40,48},{48,40},{56,32},{64,88... | collective-permute-start | bytes 393224 | tf_op jit(solution)/shard_map/cond/branch_2_fun/ppermute | solution.py:31
  87.5 7.6 %copy-start.1 = (bf16[2,512,128]{2,1,0:T(8,128)(2,1)S(1)}, bf16[2,512,128]{2,1,0:T(8,128)(2,1)}, u32[]{:S(2)}) copy-start(bf16[2,512,128]{2,1,0:T(8,128)(2,1)} %get-tuple-element.163.own_ref) | copy-start | bytes 786436
  87.5 43.4 %all-to-all-start.2 = ((bf16[16,2,64,512]{3,2,1,0:T(8,128)(2,1)}), bf16[16,2,64,512]{3,2,1,0:T(8,128)(2,1)S(1)}, u32[]{:S(2)}, u32[]{:S(2)}) async-start(bf16[16,2,64,512]{3,2,1,0:T(8,128)(2,1)} %bitcast.48), calls=%async_computation.2 | async-start | bytes 4194304 | tf_op jit(solution)/shard_map/all_to_all | solution.py:403
  95.4 3.1 %collective-permute-start.52 = (f32[256,512]{1,0:T(8,128)S(1)}, f32[256,512]{1,0:T(8,128)S(1)}, u32[]{:S(2)}, u32[]{:S(2)}) collective-permute-start(f32[256,512]{1,0:T(8,128)S(1)} %get-tuple-element.122), channel_id=1, source_target_pairs={{0,1},{1,0},{2,3},{3,2},{4,5},{5,4},{6,7},{7,6},{8,9},{9,8},{10,11... | collective-permute-start | bytes 1572872 | tf_op jit(solution)/shard_map/cond/branch_1_fun/ppermute | solution.py:181
  98.6 26.4 %collective-permute-start.53 = (bf16[256,512]{1,0:T(8,128)(2,1)S(1)}, bf16[256,512]{1,0:T(8,128)(2,1)S(1)}, u32[]{:S(2)}, u32[]{:S(2)}) collective-permute-start(bf16[256,512]{1,0:T(8,128)(2,1)S(1)} %get-tuple-element.174), channel_id=1, source_target_pairs={{0,2},{1,3},{2,0},{3,1},{4,6},{5,7},{6,4},{7,5},{8,10},{9,11},{10,... | collective-permute-start | bytes 786440 | tf_op jit(solution)/shard_map/cond/branch_1_fun/ppermute | solution.py:181
  99.7 25.3 %collective-permute-start.54 = (bf16[256,512]{1,0:T(8,128)(2,1)S(1)}, bf16[256,512]{1,0:T(8,128)(2,1)}, u32[]{:S(2)}, u32[]{:S(2)}) collective-permute-start(bf16[256,512]{1,0:T(8,128)(2,1)S(1)} %get-tuple-element.174), channel_id=1, source_target_pairs={{0,4},{1,5},{2,6},{3,7},{4,0},{5,1},{6,2},{7,3},{8,12},{9,13},{10,... | collective-permute-start | bytes 786440 | tf_op jit(solution)/shard_map/cond/branch_1_fun/ppermute | solution.py:181
  103.0 22.0 %collective-permute-start.55 = (bf16[256,512]{1,0:T(8,128)(2,1)S(1)}, bf16[256,512]{1,0:T(8,128)(2,1)}, u32[]{:S(2)}, u32[]{:S(2)}) collective-permute-start(bf16[256,512]{1,0:T(8,128)(2,1)S(1)} %get-tuple-element.174), channel_id=1, source_target_pairs={{0,6},{1,7},{2,4},{3,5},{4,2},{5,3},{6,0},{7,1},{8,14},{9,15},{10,... | collective-permute-start | bytes 786440 | tf_op jit(solution)/shard_map/cond/branch_1_fun/ppermute | solution.py:181
  104.4 20.6 %collective-permute-start.39 = (bf16[2,256,128]{2,1,0:T(8,128)(2,1)S(1)}, bf16[2,256,128]{2,1,0:T(8,128)(2,1)}, u32[]{:S(2)}, u32[]{:S(2)}) collective-permute-start(bf16[2,256,128]{2,1,0:T(8,128)(2,1)S(1)} %param.40), channel_id=1, source_target_pairs={{0,80},{8,88},{16,64},{24,72},{32,112},{40,120},{48,96},{56,104},{... | collective-permute-start | bytes 393224 | tf_op jit(solution)/shard_map/cond/branch_1_fun/cond/branch_9_fun/ppermute | solution.py:31
  126.9 4.1 %collective-permute-start.56 = (bf16[256,512]{1,0:T(8,128)(2,1)}, bf16[256,512]{1,0:T(8,128)(2,1)}, u32[]{:S(2)}, u32[]{:S(2)}) collective-permute-start(bf16[256,512]{1,0:T(8,128)(2,1)} %add_convert_fusion.1), channel_id=1, source_target_pairs={{0,1},{1,0},{2,3},{3,2},{4,5},{5,4},{6,7},{7,6},{8,9},{9,8},{10,11... | collective-permute-start | bytes 786440 | tf_op jit(solution)/shard_map/cond/branch_1_fun/ppermute | solution.py:181
